TPU v7x, 32 devices: a whole 2x2x4 slice. The times are simulated.
32 devices in a mesh: rep: 8 (over z, x), shard: 4 (over y, core).
Axes of the slice: x: 2, y: 2, z: 4, core: 2. Of those that a mesh axis runs over, the one named last changes fastest.
Arguments:
- tokens: bfloat16 [16384, 768], P(('rep', 'shard')), may hold values from -6 to 6
- condition: bfloat16 [64, 768], P(('rep', 'shard')), may hold values from -5 to 5
- counts: int32 [32], P(('rep', 'shard')), may hold values from 0 to 2, as said below
- cotangent: bfloat16 [16384, 768], P(('rep', 'shard')), may hold values from -6 to 6
- ada_weight: bfloat16 [768, 4608], P('shard'), may hold values from -0.21875 to 0.21875
- ada_bias: bfloat16 [4608], P('shard'), may hold values from -3 to 3
- qkv_weight: bfloat16 [768, 2304], P('shard'), may hold values from -0.21875 to 0.21875
- qv_bias: bfloat16 [1536], P('shard'), may hold values from -3 to 3
- proj_weight: bfloat16 [768, 768], P('shard'), may hold values from -0.875 to 0.875
- proj_bias: bfloat16 [768], P('shard'), may hold values from -3 to 3
- fc1_weight: bfloat16 [768, 3072], P('shard'), may hold values from -0.21875 to 0.21875
- fc1_bias: bfloat16 [3072], P('shard'), may hold values from -3 to 3
- fc2_weight: bfloat16 [3072, 768], P('shard'), may hold values from -0.109375 to 0.109375
- fc2_bias: bfloat16 [768], P('shard'), may hold values from -3 to 3
Outputs:
- block_out: bfloat16 [16384, 768], P(('rep', 'shard'))
- grad_tokens: float32 [16384, 768], P(('rep', 'shard'))
- grad_condition: float32 [64, 768], P(('rep', 'shard'))
- grad_ada_weight: float32 [768, 4608], P('shard')
- grad_ada_bias: float32 [4608], P('shard')
- grad_qkv_weight: float32 [768, 2304], P('shard')
- grad_qv_bias: float32 [1536], P('shard')
- grad_proj_weight: float32 [768, 768], P('shard')
- grad_proj_bias: float32 [768], P('shard')
- grad_fc1_weight: float32 [768, 3072], P('shard')
- grad_fc1_bias: float32 [3072], P('shard')
- grad_fc2_weight: float32 [3072, 768], P('shard')
- grad_fc2_bias: float32 [768], P('shard')
Inputs may be any that keep to these rules, and one draw needn't show every extreme that they name: counts[i] is the number of live latent slots of device i, devices taken in the order of rep then shard, each device holding 2 slots with its live ones first; the counts of the 4 devices of one replica group (consecutive entries) sum to 4; in every group some device holds 2 live latents and some holds none.
All inputs are finite; a program needn't handle non-finite values.
Results may differ from a plain program's by a relative error of at most 0.012.
The roundings to bfloat16 on the way count: a program that leaves them out, or rounds other values in their place, can miss the bound.
Values may be sent and summed in bfloat16 or wider, within the bound.
No kernel may reach another device: no remote copies, remote signals or barrier semaphores. Data moves between devices by JAX's collectives and lax.ppermute only.
A program may use at most 192 MiB of HBM per device.

v0:
```python
import jax
import jax.numpy as jnp
from jax import lax
from jax.sharding import PartitionSpec as P

HEADS = 12
HEAD_DIM = 64


EPS = 1e-06
GELU_C = 0.7978845608028654
GELU_A = 0.044715


def normalize(values):
    center = values - jnp.mean(values, axis=-1, keepdims=True)
    inv_std = lax.rsqrt(jnp.mean(center * center, axis=-1, keepdims=True) + EPS)
    return (center * inv_std, inv_std)


def norm_back(grad_hat, normed, inv_std):
    return inv_std * (
        grad_hat
        - jnp.mean(grad_hat, axis=-1, keepdims=True)
        - normed * jnp.mean(grad_hat * normed, axis=-1, keepdims=True)
    )


def gelu_pair(pre_act):
    tanh_arg = GELU_C * (pre_act + GELU_A * pre_act * pre_act * pre_act)
    tanh_val = jnp.tanh(tanh_arg)
    activated = 0.5 * pre_act * (1.0 + tanh_val)
    derivative = 0.5 * (1.0 + tanh_val) + 0.5 * pre_act * (1.0 - tanh_val * tanh_val) * GELU_C * (
        1.0 + 3.0 * GELU_A * pre_act * pre_act
    )
    return (activated, derivative)


def contract_rows(left, right):
    return lax.dot_general(
        left, right, (((0,), (0,)), ((), ())), preferred_element_type=jnp.float32
    )


def times_trans(left, right):
    return lax.dot_general(
        left, right, (((1,), (1,)), ((), ())), preferred_element_type=jnp.float32
    )


def batched(form, left, right):
    return jnp.einsum(form, left, right, preferred_element_type=jnp.float32)


def head_split(rows):
    return rows.reshape(rows.shape[0], HEADS, HEAD_DIM)


def attention_probs(queries, key_rows, log_total):
    scores = batched("qhd,khd->hqk", head_split(queries), head_split(key_rows)) * HEAD_DIM ** (-0.5)
    if log_total is None:
        row_max = jnp.max(scores, axis=-1, keepdims=True)
        log_total = row_max + jnp.log(jnp.sum(jnp.exp(scores - row_max), axis=-1, keepdims=True))
    return (jnp.exp(scores - log_total), log_total)


def forward_latent(tok_rows, cond_row, attn_params, mlp_params):
    ada_w, ada_b, qkv_w, qv_b, proj_w, proj_b = attn_params
    fc1_w, fc1_b, fc2_w, fc2_b = mlp_params
    width = tok_rows.shape[1]
    silu_cond = jax.nn.silu(cond_row.astype(jnp.float32)).astype(jnp.bfloat16)
    modulation = jnp.dot(silu_cond[None, :], ada_w, preferred_element_type=jnp.float32)[
        0
    ] + ada_b.astype(jnp.float32)
    shift_one, scale_one, gate_one, shift_two, scale_two, gate_two = jnp.split(modulation, 6)
    resid_in = tok_rows.astype(jnp.float32)
    normed_one, inv_one = normalize(resid_in)
    hidden_one = (normed_one * (1.0 + scale_one) + shift_one).astype(jnp.bfloat16)
    projected = jnp.dot(hidden_one, qkv_w, preferred_element_type=jnp.float32)
    bias_wide = qv_b.astype(jnp.float32)
    queries = (projected[:, :width] + bias_wide[:width]).astype(jnp.bfloat16)
    key_rows = projected[:, width : 2 * width].astype(jnp.bfloat16)
    value_rows = (projected[:, 2 * width :] + bias_wide[width:]).astype(jnp.bfloat16)
    attn_probs, log_total = attention_probs(queries, key_rows, None)
    probs_low = attn_probs.astype(jnp.bfloat16)
    mixed = (
        batched("hqk,khd->qhd", probs_low, head_split(value_rows))
        .reshape(-1, width)
        .astype(jnp.bfloat16)
    )
    branch_one = jnp.dot(mixed, proj_w, preferred_element_type=jnp.float32) + proj_b.astype(
        jnp.float32
    )
    resid_mid = resid_in + gate_one * branch_one
    normed_two, inv_two = normalize(resid_mid)
    hidden_two = (normed_two * (1.0 + scale_two) + shift_two).astype(jnp.bfloat16)
    pre_act = jnp.dot(hidden_two, fc1_w, preferred_element_type=jnp.float32) + fc1_b.astype(
        jnp.float32
    )
    activated, derivative = gelu_pair(pre_act)
    act_low = activated.astype(jnp.bfloat16)
    branch_two = jnp.dot(act_low, fc2_w, preferred_element_type=jnp.float32) + fc2_b.astype(
        jnp.float32
    )
    block_rows = (resid_mid + gate_two * branch_two).astype(jnp.bfloat16)
    saved = (
        silu_cond,
        modulation,
        normed_one,
        inv_one,
        hidden_one,
        queries,
        key_rows,
        value_rows,
        log_total,
        mixed,
        branch_one,
        normed_two,
        inv_two,
        hidden_two,
        pre_act,
        act_low,
        branch_two,
    )
    return (block_rows, saved)


def blank_forward(seq_len, width, hidden_units):
    wide_rows = jnp.zeros((seq_len, width), jnp.float32)
    low_rows = jnp.zeros((seq_len, width), jnp.bfloat16)
    column = jnp.zeros((seq_len, 1), jnp.float32)
    saved = (
        jnp.zeros((width,), jnp.bfloat16),
        jnp.zeros((6 * width,), jnp.float32),
        wide_rows,
        column,
        low_rows,
        low_rows,
        low_rows,
        low_rows,
        jnp.zeros((HEADS, seq_len, 1), jnp.float32),
        low_rows,
        wide_rows,
        wide_rows,
        column,
        low_rows,
        jnp.zeros((seq_len, hidden_units), jnp.float32),
        jnp.zeros((seq_len, hidden_units), jnp.bfloat16),
        wide_rows,
    )
    return (low_rows, saved)


def live_or_blank(alive, live_fn, blank_fn, operands):
    return lax.cond(alive, live_fn, blank_fn, operands)


def mlp_backward(cot_rows, saved, mlp_params):
    fc1_w, fc1_b, fc2_w, fc2_b = mlp_params
    modulation = saved[1]
    normed_two, inv_two, hidden_two, pre_act, act_low, branch_two = saved[11:17]
    shift_one, scale_one, gate_one, shift_two, scale_two, gate_two = jnp.split(modulation, 6)
    cot_wide = cot_rows.astype(jnp.float32)
    grad_branch_two = gate_two * cot_wide
    grad_gate_two = jnp.sum(cot_wide * branch_two, axis=0)
    low_two = grad_branch_two.astype(jnp.bfloat16)
    grad_fc2_b = jnp.sum(grad_branch_two, axis=0)
    activated, derivative = gelu_pair(pre_act)
    grad_pre = times_trans(low_two, fc2_w) * derivative
    low_pre = grad_pre.astype(jnp.bfloat16)
    grad_fc1_b = jnp.sum(grad_pre, axis=0)
    grad_hidden_two = times_trans(low_pre, fc1_w)
    grad_shift_two = jnp.sum(grad_hidden_two, axis=0)
    grad_scale_two = jnp.sum(grad_hidden_two * normed_two, axis=0)
    grad_mid = cot_wide + norm_back(grad_hidden_two * (1.0 + scale_two), normed_two, inv_two)
    return (
        grad_mid,
        (grad_shift_two, grad_scale_two, grad_gate_two),
        (low_two, low_pre),
        (grad_fc1_b, grad_fc2_b),
    )


def attn_backward(grad_mid, mod_two, saved, cond_row, attn_params):
    ada_w, ada_b, qkv_w, qv_b, proj_w, proj_b = attn_params
    (
        modulation,
        normed_one,
        inv_one,
        hidden_one,
        queries,
        key_rows,
        value_rows,
        log_total,
        mixed,
        branch_one,
    ) = saved[1:11]
    shift_one, scale_one, gate_one, shift_two, scale_two, gate_two = jnp.split(modulation, 6)
    width = grad_mid.shape[1]
    grad_branch_one = gate_one * grad_mid
    grad_gate_one = jnp.sum(grad_mid * branch_one, axis=0)
    low_one = grad_branch_one.astype(jnp.bfloat16)
    grad_proj_b = jnp.sum(grad_branch_one, axis=0)
    grad_mixed = times_trans(low_one, proj_w).astype(jnp.bfloat16)
    attn_probs, log_total = attention_probs(queries, key_rows, log_total)
    probs_low = attn_probs.astype(jnp.bfloat16)
    grad_heads = head_split(grad_mixed)
    grad_values = batched("hqk,qhd->khd", probs_low, grad_heads).reshape(-1, width)
    grad_probs = batched("qhd,khd->hqk", grad_heads, head_split(value_rows))
    row_dot = jnp.sum(attn_probs * grad_probs, axis=-1, keepdims=True)
    grad_scores = (attn_probs * (grad_probs - row_dot) * HEAD_DIM ** (-0.5)).astype(jnp.bfloat16)
    grad_queries = batched("hqk,khd->qhd", grad_scores, head_split(key_rows)).reshape(-1, width)
    grad_keys = batched("hqk,qhd->khd", grad_scores, head_split(queries)).reshape(-1, width)
    grad_qkv = jnp.concatenate([grad_queries, grad_keys, grad_values], axis=1).astype(jnp.bfloat16)
    grad_qv_b = jnp.concatenate([jnp.sum(grad_queries, axis=0), jnp.sum(grad_values, axis=0)])
    grad_hidden_one = times_trans(grad_qkv, qkv_w)
    grad_shift_one = jnp.sum(grad_hidden_one, axis=0)
    grad_scale_one = jnp.sum(grad_hidden_one * normed_one, axis=0)
    grad_rows = grad_mid + norm_back(grad_hidden_one * (1.0 + scale_one), normed_one, inv_one)
    grad_mod = jnp.concatenate(
        [grad_shift_one, grad_scale_one, grad_gate_one, mod_two[0], mod_two[1], mod_two[2]]
    ).astype(jnp.bfloat16)
    grad_silu = times_trans(grad_mod[None, :], ada_w)[0]
    cond_wide = cond_row.astype(jnp.float32)
    logistic = jax.nn.sigmoid(cond_wide)
    grad_cond = grad_silu * logistic * (1.0 + cond_wide * (1.0 - logistic))
    return (grad_rows, grad_cond, grad_mod, (low_one, grad_qkv), (grad_qv_b, grad_proj_b))


def per_device(
    tokens,
    condition,
    counts,
    cotangent,
    ada_weight,
    ada_bias,
    qkv_weight,
    qv_bias,
    proj_weight,
    proj_bias,
    fc1_weight,
    fc1_bias,
    fc2_weight,
    fc2_bias,
):
    own_count = counts[0]
    slot_total = condition.shape[0]
    width = tokens.shape[1]
    seq_len = tokens.shape[0] // slot_total
    hidden_units = fc1_weight.shape[1]
    attn_full = (
        lax.all_gather(ada_weight, "shard", axis=0, tiled=True),
        lax.all_gather(ada_bias, "shard", axis=0, tiled=True),
        lax.all_gather(qkv_weight, "shard", axis=0, tiled=True),
        lax.all_gather(qv_bias, "shard", axis=0, tiled=True),
        lax.all_gather(proj_weight, "shard", axis=0, tiled=True),
        lax.all_gather(proj_bias, "shard", axis=0, tiled=True),
    )
    work_items = [
        (
            tokens[slot_index * seq_len : (slot_index + 1) * seq_len],
            condition[slot_index],
            cotangent[slot_index * seq_len : (slot_index + 1) * seq_len],
            own_count > slot_index,
        )
        for slot_index in range(slot_total)
    ]
    mlp_full = (
        lax.all_gather(fc1_weight, "shard", axis=0, tiled=True),
        lax.all_gather(fc1_bias, "shard", axis=0, tiled=True),
        lax.all_gather(fc2_weight, "shard", axis=0, tiled=True),
        lax.all_gather(fc2_bias, "shard", axis=0, tiled=True),
    )
    block_list = []
    saved_list = []
    for work_item in work_items:
        block_rows, saved = live_or_blank(
            work_item[3],
            lambda operands: forward_latent(operands[0], operands[1], attn_full, mlp_full),
            lambda operands: blank_forward(seq_len, width, hidden_units),
            (work_item[0], work_item[1]),
        )
        block_list.append(block_rows)
        saved_list.append(saved)
    mlp_back_w = (
        lax.all_gather(fc1_weight, "shard", axis=0, tiled=True),
        lax.all_gather(fc1_bias, "shard", axis=0, tiled=True),
        lax.all_gather(fc2_weight, "shard", axis=0, tiled=True),
        lax.all_gather(fc2_bias, "shard", axis=0, tiled=True),
    )

    def mlp_blank(operands):
        zero_wide = jnp.zeros((width,), jnp.float32)
        return (
            jnp.zeros((seq_len, width), jnp.float32),
            (zero_wide, zero_wide, zero_wide),
            (
                jnp.zeros((seq_len, width), jnp.bfloat16),
                jnp.zeros((seq_len, hidden_units), jnp.bfloat16),
            ),
            (jnp.zeros((hidden_units,), jnp.float32), zero_wide),
        )

    mid_list = []
    two_list = []
    low_two_list = []
    low_pre_list = []
    fc1_b_total = jnp.zeros((hidden_units,), jnp.float32)
    fc2_b_total = jnp.zeros((width,), jnp.float32)
    for work_item, saved in zip(work_items, saved_list):
        grad_mid, mod_two, low_pair, bias_pair = live_or_blank(
            work_item[3],
            lambda operands: mlp_backward(operands[0], operands[1], mlp_back_w),
            mlp_blank,
            (work_item[2], saved),
        )
        mid_list.append(grad_mid)
        two_list.append(mod_two)
        low_two_list.append(low_pair[0])
        low_pre_list.append(low_pair[1])
        fc1_b_total = fc1_b_total + bias_pair[0]
        fc2_b_total = fc2_b_total + bias_pair[1]
    act_rows = jnp.concatenate([saved[15] for saved in saved_list], axis=0)
    hidden_two_rows = jnp.concatenate([saved[13] for saved in saved_list], axis=0)
    fc2_w_total = contract_rows(act_rows, jnp.concatenate(low_two_list, axis=0))
    fc1_w_total = contract_rows(hidden_two_rows, jnp.concatenate(low_pre_list, axis=0))
    mlp_pieces = (
        lax.psum_scatter(fc1_w_total, "shard", scatter_dimension=0, tiled=True),
        lax.psum_scatter(fc1_b_total, "shard", scatter_dimension=0, tiled=True),
        lax.psum_scatter(fc2_w_total, "shard", scatter_dimension=0, tiled=True),
        lax.psum_scatter(fc2_b_total, "shard", scatter_dimension=0, tiled=True),
    )
    attn_back_w = (
        lax.all_gather(ada_weight, "shard", axis=0, tiled=True),
        lax.all_gather(ada_bias, "shard", axis=0, tiled=True),
        lax.all_gather(qkv_weight, "shard", axis=0, tiled=True),
        lax.all_gather(qv_bias, "shard", axis=0, tiled=True),
        lax.all_gather(proj_weight, "shard", axis=0, tiled=True),
        lax.all_gather(proj_bias, "shard", axis=0, tiled=True),
    )

    def attn_blank(operands):
        return (
            jnp.zeros((seq_len, width), jnp.float32),
            jnp.zeros((width,), jnp.float32),
            jnp.zeros((6 * width,), jnp.bfloat16),
            (
                jnp.zeros((seq_len, width), jnp.bfloat16),
                jnp.zeros((seq_len, 3 * width), jnp.bfloat16),
            ),
            (jnp.zeros((2 * width,), jnp.float32), jnp.zeros((width,), jnp.float32)),
        )

    grad_row_list = []
    grad_cond_list = []
    grad_mod_list = []
    low_one_list = []
    qkv_grad_list = []
    qv_b_total = jnp.zeros((2 * width,), jnp.float32)
    proj_b_total = jnp.zeros((width,), jnp.float32)
    for position, work_item in enumerate(work_items):
        grad_rows, grad_cond, grad_mod, low_pair, bias_pair = live_or_blank(
            work_item[3],
            lambda operands: attn_backward(
                operands[0], operands[1], operands[2], operands[3], attn_back_w
            ),
            attn_blank,
            (mid_list[position], two_list[position], saved_list[position], work_item[1]),
        )
        grad_row_list.append(grad_rows)
        grad_cond_list.append(grad_cond)
        grad_mod_list.append(grad_mod)
        low_one_list.append(low_pair[0])
        qkv_grad_list.append(low_pair[1])
        qv_b_total = qv_b_total + bias_pair[0]
        proj_b_total = proj_b_total + bias_pair[1]
    mixed_rows = jnp.concatenate([saved[9] for saved in saved_list], axis=0)
    hidden_one_rows = jnp.concatenate([saved[4] for saved in saved_list], axis=0)
    proj_w_total = contract_rows(mixed_rows, jnp.concatenate(low_one_list, axis=0))
    qkv_w_total = contract_rows(hidden_one_rows, jnp.concatenate(qkv_grad_list, axis=0))
    attn_totals = (qkv_w_total, qv_b_total, proj_w_total, proj_b_total)
    silu_stack = jnp.stack([saved[0] for saved in saved_list])
    mod_stack = jnp.stack(grad_mod_list)
    ada_w_total = contract_rows(silu_stack, mod_stack)
    ada_b_total = jnp.sum(mod_stack.astype(jnp.float32), axis=0)
    attn_pieces = (
        lax.psum_scatter(ada_w_total, "shard", scatter_dimension=0, tiled=True),
        lax.psum_scatter(ada_b_total, "shard", scatter_dimension=0, tiled=True),
        lax.psum_scatter(attn_totals[0], "shard", scatter_dimension=0, tiled=True),
        lax.psum_scatter(attn_totals[1], "shard", scatter_dimension=0, tiled=True),
        lax.psum_scatter(attn_totals[2], "shard", scatter_dimension=0, tiled=True),
        lax.psum_scatter(attn_totals[3], "shard", scatter_dimension=0, tiled=True),
    )
    summed = lax.psum(
        (
            attn_pieces[0],
            attn_pieces[1],
            attn_pieces[2],
            attn_pieces[3],
            attn_pieces[4],
            attn_pieces[5],
            mlp_pieces[0],
            mlp_pieces[1],
            mlp_pieces[2],
            mlp_pieces[3],
        ),
        "rep",
    )
    grad_ada_w, grad_ada_b = (summed[0], summed[1])
    core = summed[2:6]
    feed = summed[6:10]
    block_out = jnp.concatenate(block_list, axis=0)
    grad_tokens = jnp.concatenate(grad_row_list, axis=0)
    grad_condition = jnp.stack(grad_cond_list)
    return (
        block_out,
        grad_tokens,
        grad_condition,
        grad_ada_w,
        grad_ada_b,
        core[0],
        core[1],
        core[2],
        core[3],
        feed[0],
        feed[1],
        feed[2],
        feed[3],
    )


def solution(mesh):
    return jax.shard_map(
        per_device,
        mesh=mesh,
        in_specs=(
            P(("rep", "shard"), None),
            P(("rep", "shard"), None),
            P(("rep", "shard")),
            P(("rep", "shard"), None),
            P("shard", None),
            P("shard"),
            P("shard", None),
            P("shard"),
            P("shard", None),
            P("shard"),
            P("shard", None),
            P("shard"),
            P("shard", None),
            P("shard"),
        ),
        out_specs=(
            P(("rep", "shard"), None),
            P(("rep", "shard"), None),
            P(("rep", "shard"), None),
            P("shard", None),
            P("shard"),
            P("shard", None),
            P("shard"),
            P("shard", None),
            P("shard"),
            P("shard", None),
            P("shard"),
            P("shard", None),
            P("shard"),
        ),
        check_vma=False,
    )
```

profile of v0, /device:TPU:0, one launch (start us, length us, event | category | flops | bytes accessed | tf_op | source)
XLA Modules:
  0.0 1136.5 jit_solution(1093338560251603169)
XLA Ops:
  10.7 6.2 all-gather
  17.1 5.4 all-gather.2
  23.1 5.2 all-gather.1
  30.8 7.9 all-reduce.10
  39.2 23.1 %all-gather.11.cloned.1.call-done = bf16[768,2304]{1,0:T(8,128)(2,1)} async-done(((bf16[192,2304]{1,0:T(8,128)(2,1)}), bf16[768,2304]{1,0:T(8,128)(2,1)}) %all-gather.11.cloned.1.call-update) | async-done | bytes 3538960 | tf_op jit(solution)/shard_map/all_gather | solution.py:254
  62.3 39.1 %all-gather.15.cloned.1.call-done = bf16[768,3072]{1,0:T(8,128)(2,1)} async-done(((bf16[192,3072]{1,0:T(8,128)(2,1)}), bf16[768,3072]{1,0:T(8,128)(2,1)}) %all-gather.15.cloned.1.call-update) | async-done | bytes 4718608 | tf_op jit(solution)/shard_map/all_gather | solution.py:269
  101.4 38.9 %all-gather.17.cloned.1.call-done = bf16[3072,768]{1,0:T(8,128)(2,1)} async-done(((bf16[768,768]{1,0:T(8,128)(2,1)}), bf16[3072,768]{1,0:T(8,128)(2,1)}) %all-gather.17.cloned.1.call-update) | async-done | bytes 4718608 | tf_op jit(solution)/shard_map/all_gather | solution.py:271
  140.3 52.3 %all-gather.9.cloned.1.call-done = bf16[768,4608]{1,0:T(8,128)(2,1)} async-done(((bf16[192,4608]{1,0:T(8,128)(2,1)}), bf16[768,4608]{1,0:T(8,128)(2,1)}) %all-gather.9.cloned.1.call-update) | async-done | bytes 7077904 | tf_op jit(solution)/shard_map/all_gather | solution.py:252
  192.6 13.7 %conditional.6 = (bf16[256,768]{1,0:T(8,128)(2,1)}, f32[4608]{0:T(1024)}, f32[256,768]{1,0:T(8,128)}, f32[256,1]{0,1:T(1,128)S(1)}, bf16[256,768]{1,0:T(8,128)(2...) conditional(s32[]{:T(128)} %bitcast.42, () %tuple.68, ...), branch_computations={%region_0.0_spmd, %region_1.8_spmd} | conditional | flops 3854910464 | bytes 101574952 | solution.py:155
  209.7 5.3 conditional.9
  215.0 13.9 %conditional.7 = (bf16[256,768]{1,0:T(8,128)(2,1)}, f32[4608]{0:T(1024)}, f32[256,768]{1,0:T(8,128)}, f32[256,1]{0,1:T(1,128)S(1)}, bf16[256,768]{1,0:T(8,128)(2...) conditional(s32[]{:T(128)} %bitcast.44, () %tuple.70, ...), branch_computations={%region_8.9_spmd, %region_9.16_spmd} | conditional | flops 3854910464 | bytes 101611848 | solution.py:155
  232.1 7.3 conditional.11
  243.8 6.2 fusion.128
  251.1 8.1 fusion.124
  259.3 8.3 fusion.120
  268.3 7.8 fusion.148
  276.2 164.8 %reduce-scatter.10.cloned.1.call-done = f32[192,768]{1,0:T(8,128)} async-done(((f32[768,768]{1,0:T(8,128)}), f32[192,768]{1,0:T(8,128)}) %reduce-scatter.10.cloned.1.call-update) | async-done | bytes 589840 | tf_op jit(solution)/shard_map/reduce_scatter | solution.py:391
  441.0 66.4 %reduce-scatter.8.cloned.1.call-done = f32[192,2304]{1,0:T(8,128)} async-done(((f32[768,2304]{1,0:T(8,128)}), f32[192,2304]{1,0:T(8,128)}) %reduce-scatter.8.cloned.1.call-update) | async-done | bytes 1769488 | tf_op jit(solution)/shard_map/reduce_scatter | solution.py:389
  507.4 81.1 %reduce-scatter.14.cloned.1.call-done = f32[768,768]{1,0:T(8,128)} async-done(((f32[3072,768]{1,0:T(8,128)}), f32[768,768]{1,0:T(8,128)}) %reduce-scatter.14.cloned.1.call-update) | async-done | bytes 2359312 | tf_op jit(solution)/shard_map/reduce_scatter | solution.py:330
  588.4 81.1 %reduce-scatter.12.cloned.1.call-done = f32[192,3072]{1,0:T(8,128)} async-done(((f32[768,3072]{1,0:T(8,128)}), f32[192,3072]{1,0:T(8,128)}) %reduce-scatter.12.cloned.1.call-update) | async-done | bytes 2359312 | tf_op jit(solution)/shard_map/reduce_scatter | solution.py:328
  669.5 112.0 %reduce-scatter.6.cloned.1.call-done = f32[192,4608]{1,0:T(8,128)} async-done(((f32[768,4608]{1,0:T(8,128)}), f32[192,4608]{1,0:T(8,128)}) %reduce-scatter.6.cloned.1.call-update) | async-done | bytes 3538960 | tf_op jit(solution)/shard_map/reduce_scatter | solution.py:387
  786.6 11.0 all-reduce.9
  798.0 39.9 %all-reduce.7 = (f32[1152]{0:T(1024)}, f32[384]{0:T(512)}, f32[192]{0:T(256)}, f32[768]{0:T(1024)}, f32[192]{0:T(256)}) all-reduce(f32[1152]{0:T(1024)S(1)} %dynamic-slice.3, f32[384]{0:T(512)S(1)} %dynamic-slice.5, f32[192]{0:T(256)S(1)} %dynamic-slice.7, f32[768]{0:T(1024)S(1)} %dynamic-slice.9, ...), channel_id=1, replica_groups=mesh['rep'=8,'shard'=4] {'rep'}, use_global_device_ids=true, to_apply=%region_60.61 | all-reduce | flops 2688 | bytes 21504 | tf_op jit(solution)/shard_map/psum | solution.py:394
  843.9 276.0 %all-reduce.13.cloned.1.call-done = (f32[192,4608]{1,0:T(8,128)}, f32[192,2304]{1,0:T(8,128)}, f32[192,768]{1,0:T(8,128)}, f32[192,3072]{1,0:T(8,128)}, f32[768,768]{1,0:T(8,128)}) async-done(((f32[192,4608]{1,0:T(8,128)}, f32[192,2304]{1,0:T(8,128)}, f32[192,768]{1,0:T(8,128)}, f32[192,3072]{1,0:T(8,128)}, f32[768,768]{1,0:T(8,128)}), (f32[192,4608]{1,0:T(8,128)}, f32[192,2304]{1,0:T(8,128)}, ...) | async-done | bytes 10616848 | tf_op jit(solution)/shard_map/psum | solution.py:394
  (211 shorter events, 77.0 us)
Async XLA Ops:
  7.2 21.8 %copy-start.122 = (u32[32]{0:T(128)S(1)}, u32[32]{0:T(128)}, u32[]{:S(2)}) copy-start(u32[32]{0:T(128)} %constant.152) | copy-start | bytes 388
  7.2 9.8 copy-start.123
  7.2 15.9 %copy-start.124 = (bf16[384]{0:T(512)(128)(2,1)S(1)}, bf16[384]{0:T(512)(128)(2,1)}, u32[]{:S(2)}) copy-start(bf16[384]{0:T(512)(128)(2,1)} %param.33) | copy-start | bytes 2308
  7.2 23.1 %copy-start.129 = (bf16[192]{0:T(256)(128)(2,1)S(1)}, bf16[192]{0:T(256)(128)(2,1)}, u32[]{:S(2)}) copy-start(bf16[192]{0:T(256)(128)(2,1)} %param.35) | copy-start | bytes 1156
  7.2 23.3 %copy-start.130 = (bf16[192]{0:T(256)(128)(2,1)S(1)}, bf16[192]{0:T(256)(128)(2,1)}, u32[]{:S(2)}) copy-start(bf16[192]{0:T(256)(128)(2,1)} %param.39) | copy-start | bytes 1156
  7.2 31.4 %copy-start.96 = (bf16[2,768]{1,0:T(2,128)(2,1)S(1)}, bf16[2,768]{1,0:T(2,128)(2,1)}, u32[]{:S(2)}) copy-start(bf16[2,768]{1,0:T(2,128)(2,1)} %param.27) | copy-start | bytes 9220
  7.3 185.3 %copy-start = (bf16[512,768]{1,0:T(8,128)(2,1)S(1)}, bf16[512,768]{1,0:T(8,128)(2,1)}, u32[]{:S(2)}) copy-start(bf16[512,768]{1,0:T(8,128)(2,1)} %param.26) | copy-start | bytes 2359300
  7.3 32.0 %all-gather.13.cloned.1.call-start = ((), (), s32[]{:S(2)}) async-start(), calls=%async_computation.7 | async-start | bytes 1474560 | tf_op jit(solution)/shard_map/all_gather | solution.py:256
  8.0 54.3 %all-gather.11.cloned.1.call-start = ((), (), s32[]{:S(2)}) async-start(), calls=%async_computation.6 | async-start | bytes 4423680 | tf_op jit(solution)/shard_map/all_gather | solution.py:254
  8.7 92.6 %all-gather.15.cloned.1.call-start = ((), (), s32[]{:S(2)}) async-start(), calls=%async_computation.8 | async-start | bytes 5898240 | tf_op jit(solution)/shard_map/all_gather | solution.py:269
  9.5 130.8 %all-gather.17.cloned.1.call-start = ((), (), s32[]{:S(2)}) async-start(), calls=%async_computation.9 | async-start | bytes 5898240 | tf_op jit(solution)/shard_map/all_gather | solution.py:271
  10.1 182.5 %all-gather.9.cloned.1.call-start = ((), (), s32[]{:S(2)}) async-start(), calls=%async_computation.5 | async-start | bytes 8847360 | tf_op jit(solution)/shard_map/all_gather | solution.py:252
  10.6 430.3 %reduce-scatter.10.cloned.1.call-start = ((), (), s32[]{:S(2)}) async-start(), calls=%async_computation.12 | async-start | bytes 2949120 | tf_op jit(solution)/shard_map/reduce_scatter | solution.py:391
  17.0 175.5 %copy-start.49 = (bf16[4608]{0:T(1024)(128)(2,1)}, bf16[4608]{0:T(1024)(128)(2,1)S(1)}, u32[]{:S(2)}) copy-start(bf16[4608]{0:T(1024)(128)(2,1)S(1)} %reshape.497) | copy-start | bytes 27652
  28.3 164.3 %copy-start.48 = (bf16[1536]{0:T(1024)(128)(2,1)}, bf16[1536]{0:T(1024)(128)(2,1)S(1)}, u32[]{:S(2)}) copy-start(bf16[1536]{0:T(1024)(128)(2,1)S(1)} %reshape.499) | copy-start | bytes 9220
  39.2 153.4 %copy-start.64 = (bf16[768]{0:T(1024)(128)(2,1)}, bf16[768]{0:T(1024)(128)(2,1)S(1)}, u32[]{:S(2)}) copy-start(bf16[768]{0:T(1024)(128)(2,1)S(1)} %get-tuple-element.615) | copy-start | bytes 4612
  209.0 6.0 copy-start.1
  243.7 263.7 %reduce-scatter.8.cloned.1.call-start = ((), (), s32[]{:S(2)}) async-start(), calls=%async_computation.11 | async-start | bytes 8847360 | tf_op jit(solution)/shard_map/reduce_scatter | solution.py:389
  250.0 338.4 %reduce-scatter.14.cloned.1.call-start = ((), (), s32[]{:S(2)}) async-start(), calls=%async_computation.14 | async-start | bytes 11796480 | tf_op jit(solution)/shard_map/reduce_scatter | solution.py:330
  259.2 410.3 %reduce-scatter.12.cloned.1.call-start = ((), (), s32[]{:S(2)}) async-start(), calls=%async_computation.13 | async-start | bytes 11796480 | tf_op jit(solution)/shard_map/reduce_scatter | solution.py:328
  267.6 513.9 %reduce-scatter.6.cloned.1.call-start = ((), (), s32[]{:S(2)}) async-start(), calls=%async_computation.10 | async-start | bytes 17694720 | tf_op jit(solution)/shard_map/reduce_scatter | solution.py:387
  276.1 843.7 %all-reduce.13.cloned.1.call-start = ((), (), s32[]{:S(2)}) async-start(), calls=%async_computation.15 | async-start | bytes 21233664 | tf_op jit(solution)/shard_map/psum | solution.py:394
  781.5 4.2 copy-start.77
  781.5 4.2 copy-start.79
  (30 other events, 57.1 us)
Sparse Core Ops, SparseCore 0:
  9.7 20.1 all-gather.12
  31.5 30.8 all-gather.10
  63.9 37.4 all-gather.14
  102.8 37.4 all-gather.16
  141.7 50.8 all-gather.8
  243.8 197.0 reduce-scatter.9
  443.7 63.6 reduce-scatter.7
  510.0 78.4 reduce-scatter.13
  591.0 78.4 reduce-scatter.11
  671.9 109.4 reduce-scatter.5
  786.3 333.4 all-reduce.12
where the time goes:
time: 1150 us; the launch traced here: 1140 us
  waiting for transfers between devices  938 us (82%)
  blocking collectives  75.5 us (7%)
  local copies, waits for them, and re-layouts  57.7 us (5%)
  matrix products  34.1 us (3%)
  between operations  18.8 us (2%)
    psum x1, waiting for transfers between devices, per_device(): lax.psum((attn_pieces[0], attn_pieces[1], attn_pieces[2], attn_pieces[3],...  276 us
    reduce_scatter x1, waiting for transfers between devices, per_device(): lax.psum_scatter(attn_totals[2], 'shard', scatter_dimension=0, tiled=True)  165 us
    reduce_scatter x1, waiting for transfers between devices, per_device(): lax.psum_scatter(ada_w_total, 'shard', scatter_dimension=0, tiled=True)  112 us
    reduce_scatter x1, waiting for transfers between devices, per_device(): lax.psum_scatter(fc1_w_total, 'shard', scatter_dimension=0, tiled=True)  81.1 us
    reduce_scatter x1, waiting for transfers between devices, per_device(): lax.psum_scatter(fc2_w_total, 'shard', scatter_dimension=0, tiled=True)  81.1 us
    reduce_scatter x1, waiting for transfers between devices, per_device(): lax.psum_scatter(attn_totals[0], 'shard', scatter_dimension=0, tiled=True)  66.4 us
    all_gather x1, waiting for transfers between devices, per_device(): lax.all_gather(ada_weight, 'shard', axis=0, tiled=True)  52.3 us
    psum x1, blocking collectives, per_device(): lax.psum((attn_pieces[0], attn_pieces[1], attn_pieces[2], attn_pieces[3],...  39.9 us
  transfers between devices with their start and end apart: 11, of which 10 were waited for; matrix products, arithmetic and copies ran while one was open for 4% of the time, Pallas kernels for 0%

commit v1 on v0

v1 whole, which is shorter than its diff:
```python
import functools

import jax
import jax.numpy as jnp
from jax import lax
from jax.experimental import pallas as pl
from jax.experimental.pallas import tpu as pltpu
from jax.sharding import PartitionSpec as P

HEADS = 12
HEAD_DIM = 64
EPS = 1e-06
GELU_C = 0.7978845608028654
GELU_A = 0.044715
F32 = jnp.float32
BF16 = jnp.bfloat16
VMEM_LIMIT = 56 * 1024 * 1024


def normalize(values):
    center = values - jnp.mean(values, axis=-1, keepdims=True)
    inv_std = lax.rsqrt(jnp.mean(center * center, axis=-1, keepdims=True) + EPS)
    return (center * inv_std, inv_std)


def norm_back(grad_hat, normed, inv_std):
    return inv_std * (
        grad_hat
        - jnp.mean(grad_hat, axis=-1, keepdims=True)
        - normed * jnp.mean(grad_hat * normed, axis=-1, keepdims=True)
    )


def gelu_pair(pre_act):
    tanh_arg = GELU_C * (pre_act + GELU_A * pre_act * pre_act * pre_act)
    tanh_val = jnp.tanh(tanh_arg)
    activated = 0.5 * pre_act * (1.0 + tanh_val)
    derivative = 0.5 * (1.0 + tanh_val) + 0.5 * pre_act * (1.0 - tanh_val * tanh_val) * GELU_C * (
        1.0 + 3.0 * GELU_A * pre_act * pre_act
    )
    return (activated, derivative)


def dot_nn(left, right):
    return lax.dot_general(left, right, (((1,), (0,)), ((), ())), preferred_element_type=F32)


def dot_nt(left, right):
    return lax.dot_general(left, right, (((1,), (1,)), ((), ())), preferred_element_type=F32)


def dot_tn(left, right):
    return lax.dot_general(left, right, (((0,), (0,)), ((), ())), preferred_element_type=F32)


def pair_masks(rows):
    lane = lax.broadcasted_iota(jnp.int32, (rows, 2 * HEAD_DIM), 1)
    return lane < HEAD_DIM


def head_probs(query_pair, key_pair, first, head):
    keep = first if head == 0 else jnp.logical_not(first)
    query_head = jnp.where(keep, query_pair, jnp.zeros_like(query_pair))
    scores = dot_nt(query_head, key_pair) * HEAD_DIM ** (-0.5)
    row_max = jnp.max(scores, axis=-1, keepdims=True)
    exped = jnp.exp(scores - row_max)
    return exped * (1.0 / jnp.sum(exped, axis=-1, keepdims=True))


def attn_fwd_kernel(qkv_ref, mixed_ref):
    rows = qkv_ref.shape[0]
    width = mixed_ref.shape[1]
    first = pair_masks(rows)
    for pair in range(HEADS // 2):
        cols = pl.ds(pair * 128, 128)
        query_pair = qkv_ref[:, cols]
        key_pair = qkv_ref[:, pl.ds(width + pair * 128, 128)]
        value_pair = qkv_ref[:, pl.ds(2 * width + pair * 128, 128)]
        parts = []
        for head in range(2):
            probs_low = head_probs(query_pair, key_pair, first, head).astype(BF16)
            parts.append(dot_nn(probs_low, value_pair))
        mixed_ref[:, cols] = jnp.where(first, parts[0], parts[1]).astype(BF16)


def attn_fwd(qkv, slots):
    seq = qkv.shape[0] // slots
    width = qkv.shape[1] // 3
    return pl.pallas_call(
        attn_fwd_kernel,
        grid=(slots,),
        in_specs=[pl.BlockSpec((seq, 3 * width), lambda s: (s, 0))],
        out_specs=pl.BlockSpec((seq, width), lambda s: (s, 0)),
        out_shape=jax.ShapeDtypeStruct((slots * seq, width), BF16),
        compiler_params=pltpu.CompilerParams(vmem_limit_bytes=VMEM_LIMIT),
    )(qkv)


def attn_bwd_kernel(qkv_ref, grad_ref, out_ref, bias_ref):
    rows = qkv_ref.shape[0]
    width = grad_ref.shape[1]
    first = pair_masks(rows)
    for pair in range(HEADS // 2):
        query_cols = pl.ds(pair * 128, 128)
        key_cols = pl.ds(width + pair * 128, 128)
        value_cols = pl.ds(2 * width + pair * 128, 128)
        query_pair = qkv_ref[:, query_cols]
        key_pair = qkv_ref[:, key_cols]
        value_pair = qkv_ref[:, value_cols]
        grad_pair = grad_ref[:, query_cols]
        grads = []
        for head in range(2):
            keep = first if head == 0 else jnp.logical_not(first)
            probs = head_probs(query_pair, key_pair, first, head)
            grad_head = jnp.where(keep, grad_pair, jnp.zeros_like(grad_pair))
            grad_probs = dot_nt(grad_head, value_pair)
            row_dot = jnp.sum(probs * grad_probs, axis=-1, keepdims=True)
            grad_scores = (probs * (grad_probs - row_dot) * HEAD_DIM ** (-0.5)).astype(BF16)
            grads.append(
                (
                    dot_nn(grad_scores, key_pair),
                    dot_tn(grad_scores, query_pair),
                    dot_tn(probs.astype(BF16), grad_pair),
                )
            )
        grad_query, grad_key, grad_value = (
            jnp.where(first, left, right) for left, right in zip(grads[0], grads[1])
        )
        out_ref[:, query_cols] = grad_query.astype(BF16)
        out_ref[:, key_cols] = grad_key.astype(BF16)
        out_ref[:, value_cols] = grad_value.astype(BF16)
        bias_ref[0, :, query_cols] = jnp.sum(grad_query, axis=0, keepdims=True)
        bias_ref[0, :, key_cols] = jnp.sum(grad_value, axis=0, keepdims=True)


def attn_bwd(qkv, grad_mixed, slots):
    seq = qkv.shape[0] // slots
    width = qkv.shape[1] // 3
    return pl.pallas_call(
        attn_bwd_kernel,
        grid=(slots,),
        in_specs=[
            pl.BlockSpec((seq, 3 * width), lambda s: (s, 0)),
            pl.BlockSpec((seq, width), lambda s: (s, 0)),
        ],
        out_specs=[
            pl.BlockSpec((seq, 3 * width), lambda s: (s, 0)),
            pl.BlockSpec((1, 1, 2 * width), lambda s: (s, 0, 0)),
        ],
        out_shape=[
            jax.ShapeDtypeStruct((slots * seq, 3 * width), BF16),
            jax.ShapeDtypeStruct((slots, 1, 2 * width), F32),
        ],
        compiler_params=pltpu.CompilerParams(vmem_limit_bytes=VMEM_LIMIT),
    )(qkv, grad_mixed)


class Axis:
    def __init__(self, name, size):
        self.name = name
        self.size = size
        self.index = lax.axis_index(name)
        self.bits = [1 << k for k in range(size.bit_length() - 1)]

    def swap(self, value, bit):
        return lax.ppermute(value, self.name, [(i, i ^ bit) for i in range(self.size)])

    def high(self, bit):
        return (self.index & bit) != 0


def ordered(high, mine, other, axis=0):
    return jnp.where(
        high, jnp.concatenate([other, mine], axis), jnp.concatenate([mine, other], axis)
    )


def gather_ordered(value, axis):
    value = value[None]
    for bit in axis.bits:
        value = ordered(axis.high(bit), value, axis.swap(value, bit))
    return value


def gather_any_order(value, steps):
    for axis, bit in steps:
        value = jnp.concatenate([value, axis.swap(value, bit)], 0)
    return value


def halves(value, high, dim):
    size = value.shape[dim] // 2
    offset = high.astype(jnp.int32) * size
    keep = lax.dynamic_slice_in_dim(value, offset, size, dim)
    send = lax.dynamic_slice_in_dim(value, size - offset, size, dim)
    return keep, send


def scatter_sum(value, axis, wire):
    for bit in reversed(axis.bits):
        keep, send = halves(value, axis.high(bit), 0)
        value = keep + axis.swap(send.astype(wire), bit).astype(F32)
    return value[0]


def gather_weight(piece, shard, rep):
    pieces = {0: piece}
    half_rows = piece.shape[0] // 2
    for bit in reversed(shard.bits):
        for offset in list(pieces):
            held = pieces[offset]
            if bit == 1 or rep.size == 1:
                pieces[offset ^ bit] = shard.swap(held, bit)
            else:
                mine = lax.dynamic_slice_in_dim(
                    held, rep.high(1).astype(jnp.int32) * half_rows, half_rows, 0
                )
                near = shard.swap(mine, bit)
                far = rep.swap(near, 1)
                pieces[offset ^ bit] = ordered(rep.high(1), near, far)
    rows = piece.shape[0]
    whole = jnp.zeros((rows * shard.size, piece.shape[1]), piece.dtype)
    for offset, held in pieces.items():
        whole = lax.dynamic_update_slice(whole, held, ((shard.index ^ offset) * rows, 0))
    return whole


def reduce_weight(total, shard, rep):
    total = total.reshape((shard.size // 2, 2, -1, total.shape[1]))
    keep, send = halves(total, shard.high(1), 1)
    value = (keep + shard.swap(send.astype(BF16), 1).astype(F32))[:, 0]
    for bit in reversed(shard.bits[1:]):
        keep, send = halves(value, shard.high(bit), 0)
        value = keep + shard.swap(send.astype(BF16), bit).astype(F32)
    value = value[0]
    dims = []
    for bit in rep.bits:
        dim = 1 if value.shape[0] % 32 and value.shape[1] % 256 == 0 else 0
        dims.append(dim)
        keep, send = halves(value, rep.high(bit), dim)
        value = keep + rep.swap(send.astype(BF16), bit).astype(F32)
    value = value.astype(BF16)
    for bit, dim in zip(reversed(rep.bits), reversed(dims)):
        value = ordered(rep.high(bit), value, rep.swap(value, bit), dim)
    return value.astype(F32)


def per_device(
    shard_size,
    rep_size,
    tokens,
    condition,
    counts,
    cotangent,
    ada_weight,
    ada_bias,
    qkv_weight,
    qv_bias,
    proj_weight,
    proj_bias,
    fc1_weight,
    fc1_bias,
    fc2_weight,
    fc2_bias,
):
    shard = Axis("shard", shard_size)
    rep = Axis("rep", rep_size)
    slots, width = condition.shape
    seq = tokens.shape[0] // slots
    rows = slots * seq
    depth = ada_weight.shape[0]
    live = lax.iota(jnp.int32, slots) < counts[0]

    biases = jnp.concatenate([ada_bias, qv_bias, proj_bias, fc1_bias, fc2_bias])
    packed = jnp.concatenate([condition.reshape(-1), biases])
    packed = jnp.pad(packed, (0, -packed.shape[0] % 128)).reshape(-1, 128)
    group = gather_ordered(packed, shard).reshape(shard.size, -1)
    group_cond = group[:, : slots * width].reshape(shard.size * slots, width)
    wide = []
    start = slots * width
    for bias in (ada_bias, qv_bias, proj_bias, fc1_bias, fc2_bias):
        wide.append(group[:, start : start + bias.shape[0]].reshape(-1).astype(F32))
        start += bias.shape[0]
    ada_b, qv_b, proj_b, fc1_b, fc2_b = wide

    qkv_w = gather_weight(qkv_weight, shard, rep)
    proj_w = gather_weight(proj_weight, shard, rep)
    fc1_w = gather_weight(fc1_weight, shard, rep)
    fc2_w = gather_weight(fc2_weight, shard, rep)

    silu_group = jax.nn.silu(group_cond.astype(F32)).astype(BF16)
    my_cols = lax.dynamic_slice_in_dim(silu_group, shard.index * depth, depth, 1)
    mod_part = dot_nn(my_cols, ada_weight).reshape(shard.size, slots, -1)
    modulation = scatter_sum(mod_part, shard, F32) + ada_b
    shift_one, scale_one, gate_one, shift_two, scale_two, gate_two = (
        part[:, None, :] for part in jnp.split(modulation, 6, axis=1)
    )

    def flat(value):
        return value.reshape(rows, value.shape[-1])

    def per_slot(value):
        return value.reshape(slots, seq, value.shape[-1])

    resid_in = per_slot(tokens).astype(F32)
    normed_one, inv_one = normalize(resid_in)
    hidden_one = flat((normed_one * (1.0 + scale_one) + shift_one).astype(BF16))
    zero = jnp.zeros((width,), F32)
    qkv_b = jnp.concatenate([qv_b[:width], zero, qv_b[width:]])
    qkv = (dot_nn(hidden_one, qkv_w) + qkv_b).astype(BF16)
    mixed = attn_fwd(qkv, slots)
    branch_one = per_slot(dot_nn(mixed, proj_w) + proj_b)
    resid_mid = resid_in + gate_one * branch_one
    normed_two, inv_two = normalize(resid_mid)
    hidden_two = flat((normed_two * (1.0 + scale_two) + shift_two).astype(BF16))
    pre_act = dot_nn(hidden_two, fc1_w) + fc1_b
    activated, derivative = gelu_pair(pre_act)
    act_low = activated.astype(BF16)
    branch_two = per_slot(dot_nn(act_low, fc2_w) + fc2_b)
    block = resid_mid + gate_two * branch_two
    block_out = flat(jnp.where(live[:, None, None], block, 0.0).astype(BF16))

    cot_wide = jnp.where(live[:, None, None], per_slot(cotangent).astype(F32), 0.0)
    grad_branch_two = gate_two * cot_wide
    low_two = flat(grad_branch_two.astype(BF16))
    grad_gate_two = jnp.sum(cot_wide * branch_two, axis=1)
    grad_fc2_b = jnp.sum(grad_branch_two, axis=(0, 1))
    grad_fc2_w = reduce_weight(dot_tn(act_low, low_two), shard, rep)
    grad_pre = dot_nt(low_two, fc2_w) * derivative
    low_pre = grad_pre.astype(BF16)
    grad_fc1_b = jnp.sum(grad_pre, axis=0)
    grad_fc1_w = reduce_weight(dot_tn(hidden_two, low_pre), shard, rep)
    grad_hidden_two = per_slot(dot_nt(low_pre, fc1_w))
    grad_shift_two = jnp.sum(grad_hidden_two, axis=1)
    grad_scale_two = jnp.sum(grad_hidden_two * normed_two, axis=1)
    grad_mid = cot_wide + norm_back(grad_hidden_two * (1.0 + scale_two), normed_two, inv_two)

    grad_branch_one = gate_one * grad_mid
    grad_gate_one = jnp.sum(grad_mid * branch_one, axis=1)
    low_one = flat(grad_branch_one.astype(BF16))
    grad_proj_b = jnp.sum(grad_branch_one, axis=(0, 1))
    grad_proj_w = reduce_weight(dot_tn(mixed, low_one), shard, rep)
    grad_mixed = dot_nt(low_one, proj_w).astype(BF16)
    grad_qkv, qv_sums = attn_bwd(qkv, grad_mixed, slots)
    grad_qv_b = jnp.sum(qv_sums[:, 0], axis=0)
    grad_qkv_w = reduce_weight(dot_tn(hidden_one, grad_qkv), shard, rep)
    grad_hidden_one = per_slot(dot_nt(grad_qkv, qkv_w))
    grad_shift_one = jnp.sum(grad_hidden_one, axis=1)
    grad_scale_one = jnp.sum(grad_hidden_one * normed_one, axis=1)
    grad_tokens = flat(
        grad_mid + norm_back(grad_hidden_one * (1.0 + scale_one), normed_one, inv_one)
    )
    grad_mod = jnp.concatenate(
        [grad_shift_one, grad_scale_one, grad_gate_one, grad_shift_two, grad_scale_two, grad_gate_two],
        axis=1,
    ).astype(BF16)

    group_mod = gather_ordered(grad_mod, shard).reshape(shard.size * slots, -1)
    grad_silu = gather_ordered(dot_nt(group_mod, ada_weight), shard)
    grad_silu = lax.dynamic_slice_in_dim(grad_silu, shard.index * slots, slots, 1)
    grad_silu = jnp.swapaxes(grad_silu, 0, 1).reshape(slots, width)
    cond_wide = condition.astype(F32)
    logistic = jax.nn.sigmoid(cond_wide)
    grad_cond = grad_silu * logistic * (1.0 + cond_wide * (1.0 - logistic))

    steps = [(rep, bit) for bit in reversed(rep.bits)] + [(shard, bit) for bit in reversed(shard.bits)]
    silu_own = jax.nn.silu(cond_wide).astype(BF16)
    silu_all = gather_any_order(silu_own, steps)
    mod_all = gather_any_order(grad_mod, steps)
    silu_cols = lax.dynamic_slice_in_dim(silu_all, shard.index * depth, depth, 1)
    grad_ada_w = dot_tn(silu_cols, mod_all)
    ada_b_all = jnp.sum(mod_all.astype(F32), axis=0)
    grad_ada_b = lax.dynamic_slice_in_dim(
        ada_b_all, shard.index * ada_bias.shape[0], ada_bias.shape[0], 0
    )

    bias_grads = jnp.concatenate(
        [v.reshape(shard.size, -1) for v in (grad_qv_b, grad_proj_b, grad_fc1_b, grad_fc2_b)], axis=1
    )
    bias_sum = scatter_sum(bias_grads, shard, F32).reshape(-1, 128)
    for bit in rep.bits:
        bias_sum = bias_sum + rep.swap(bias_sum, bit)
    bias_sum = bias_sum.reshape(-1)
    bias_out = []
    start = 0
    for bias in (qv_bias, proj_bias, fc1_bias, fc2_bias):
        bias_out.append(bias_sum[start : start + bias.shape[0]])
        start += bias.shape[0]

    return (
        block_out,
        grad_tokens,
        grad_cond,
        grad_ada_w,
        grad_ada_b,
        grad_qkv_w,
        bias_out[0],
        grad_proj_w,
        bias_out[1],
        grad_fc1_w,
        bias_out[2],
        grad_fc2_w,
        bias_out[3],
    )


def solution(mesh):
    rows = P(("rep", "shard"), None)
    weights = (P("shard", None), P("shard"))
    return jax.shard_map(
        functools.partial(per_device, mesh.shape["shard"], mesh.shape["rep"]),
        mesh=mesh,
        in_specs=(rows, rows, P(("rep", "shard")), rows) + weights * 5,
        out_specs=(rows, rows, rows) + weights * 5,
        check_vma=False,
    )
```

time: 1150 us -> 459 us (0.40)
  waiting for transfers between devices: 938 us -> 184 us
  blocking collectives: 75.5 us -> 0 us
  starting transfers between devices: 0.44 us -> 62.7 us
  other arithmetic: 8.3 us -> 37.6 us
  matrix products: 34.1 us -> 62.1 us
  Pallas kernels: 0 us -> 22.6 us
  local copies, waits for them, and re-layouts: 57.7 us -> 80.2 us
  between operations: 18.8 us -> 2.98 us
    reduce_scatter x5 -> x0, waiting for transfers between devices: 505 us -> none  [the longest x1 165 us: per_device(): lax.psum_scatter(attn_totals[2], 'shard', scatter_dimension=0, tiled=True)]
    psum x1 -> x0, waiting for transfers between devices: 276 us -> none  [per_device(): lax.psum((attn_pieces[0], attn_pieces[1], attn_pieces[2], attn_pieces[3],...]
    ppermute x0 -> x71, waiting for transfers between devices: none -> 184 us  [swap(): lax.ppermute(value, self.name, [(i, i ^ bit) for i in range(self.size)])]
    all_gather x5 -> x0, waiting for transfers between devices: 153 us -> none  [the longest x1 52.3 us: per_device(): lax.all_gather(ada_weight, 'shard', axis=0, tiled=True)]
    ppermute x0 -> x71, starting transfers between devices: none -> 62.7 us  [swap(): lax.ppermute(value, self.name, [(i, i ^ bit) for i in range(self.size)])]
    another operation x66 -> x0, local copies, waits for them, and re-layouts: 40.2 us -> none
    psum x1 -> x0, blocking collectives: 39.9 us -> none  [per_device(): lax.psum((attn_pieces[0], attn_pieces[1], attn_pieces[2], attn_pieces[3],...]
    dot_general x5 -> x15, matrix products: 34.1 us -> 62.1 us  [the longest x5 26.6 us: dot_nn(): lax.dot_general(left, right, (((1,), (0,)), ((), ())), preferred_element_...]
  transfers between devices with their start and end apart: 11 -> 71, of which waited for: 10 -> 36; matrix products, arithmetic and copies ran while one was open for 4% -> 26% of each run, Pallas kernels for 0% -> 1%
where the time goes in v1:
time: 459 us; the launch traced here: 452 us
  waiting for transfers between devices  184 us (40%)
  local copies, waits for them, and re-layouts  80.2 us (17%)
  starting transfers between devices  62.7 us (14%)
  matrix products  62.1 us (14%)
  other arithmetic  37.6 us (8%)
  Pallas kernels  22.6 us (5%)
    ppermute x71, waiting for transfers between devices, swap(): lax.ppermute(value, self.name, [(i, i ^ bit) for i in range(self.size)])  184 us
    ppermute x71, starting transfers between devices, swap(): lax.ppermute(value, self.name, [(i, i ^ bit) for i in range(self.size)])  62.7 us
    dot_general x5, matrix products, dot_nn(): lax.dot_general(left, right, (((1,), (0,)), ((), ())), preferred_element_...  26.6 us
    dot_general x5, matrix products, dot_nt(): lax.dot_general(left, right, (((1,), (1,)), ((), ())), preferred_element_...  23.5 us
    dynamic_update_slice x12, local copies, waits for them, and re-layouts, gather_weight(): lax.dynamic_update_slice(whole, held, ((shard.index ^ offset) * rows, 0))  18.6 us
    pallas_call x1, Pallas kernels, attn_bwd(): pl.pallas_call(attn_bwd_kernel, grid=(slots,), in_specs=[pl.BlockSpec((se...  16 us
    unnamed x100, local copies, waits for them, and re-layouts  13 us
    dot_general x4, local copies, waits for them, and re-layouts, dot_tn(): lax.dot_general(left, right, (((0,), (0,)), ((), ())), preferred_element_...  11.9 us
  transfers between devices with their start and end apart: 71, of which 36 were waited for; matrix products, arithmetic and copies ran while one was open for 26% of the time, Pallas kernels for 1%

profile of v1, /device:TPU:0, one launch (start us, length us, event | category | flops | bytes accessed | tf_op | source)
XLA Modules:
  0.0 451.8 jit_solution(17324271963313754324)
XLA Ops:
  57.6 9.3 %collective-permute-done.12 = bf16[96,3072]{1,0:T(8,128)(2,1)} collective-permute-done((bf16[96,3072]{1,0:T(8,128)(2,1)}, bf16[96,3072]{1,0:T(8,128)(2,1)}, u32[]{:S(2)}, u32[]{:S(2)}) %collective-permute-start.12) | collective-permute-done | bytes 589856 | tf_op jit(solution)/shard_map/ppermute | solution.py:166
  73.6 9.8 %collective-permute-done.17 = bf16[384,768]{1,0:T(8,128)(2,1)S(1)} collective-permute-done((bf16[384,768]{1,0:T(8,128)(2,1)}, bf16[384,768]{1,0:T(8,128)(2,1)S(1)}, u32[]{:S(2)}, u32[]{:S(2)}) %collective-permute-start.17) | collective-permute-done | bytes 589856 | tf_op jit(solution)/shard_map/ppermute | solution.py:166
  86.4 8.0 %collective-permute-done.13 = bf16[96,3072]{1,0:T(8,128)(2,1)S(1)} collective-permute-done((bf16[96,3072]{1,0:T(8,128)(2,1)}, bf16[96,3072]{1,0:T(8,128)(2,1)S(1)}, u32[]{:S(2)}, u32[]{:S(2)}) %collective-permute-start.13) | collective-permute-done | bytes 589856 | tf_op jit(solution)/shard_map/ppermute | solution.py:166
  100.8 5.4 %fusion.11.qkv_ref = bf16[512,2304]{1,0:T(8,128)(2,1)} fusion(bf16[512,768]{1,0:T(8,128)(2,1)S(1)} %copy-done.19, bf16[768,2304]{1,0:T(8,128)(2,1)} %constant_dynamic-update-slice_fusion.24, f32[2304]{0:T(1024)S(1)} %pad_maximum_fusion.4), kind=kOutput, calls=%fused_computation.21 | convolution fusion | flops 1814298624 | bytes 6693888 | tf_op jit(solution)/shard_map/dot_general | solution.py:45
  106.2 6.6 %shard_map.237 = bf16[512,768]{1,0:T(8,128)(2,1)} custom-call(bf16[512,2304]{1,0:T(8,128)(2,1)} %fusion.11.qkv_ref), custom_call_target="tpu_custom_call" | custom-call | tf_op jit(solution)/shard_map/pallas_call | solution.py:89
  125.3 7.8 %fusion.10 = (bf16[3072,512]{0,1:T(8,128)(2,1)}, f32[512,3072]{1,0:T(8,128)S(1)}) fusion(f32[3072]{0:T(1024)S(1)} %reshape.504, bf16[512,768]{1,0:T(8,128)(2,1)S(1)} %copy-done.20, bf16[768,3072]{1,0:T(8,128)(2,1)} %constant_dynamic-update-slice_fusion.16), kind=kOutput, calls=%fused_computation.13 | convolution fusion | flops 2431647744 | bytes 14954496 | tf_op jit(solution)/shard_map/dot_general | solution.py:45
  136.4 7.6 %fusion.81 = (f32[3072]{0:T(1024)S(1)}, bf16[512,3072]{1,0:T(8,128)(2,1)S(1)}) fusion(f32[512,3072]{1,0:T(8,128)S(1)} %get-tuple-element.64, f32[3072]{0:T(1024)S(1)} %reshape.504, bf16[512,768]{1,0:T(8,128)(2,1)S(1)} %copy-done.30, bf16[3072,768]{1,0:T(8,128)(2,1)} %constant_dynamic-update-slice_fusion.12), kind=kOutput, calls=%fused_computation.254 | convolution fusion | flops 2448946176 | bytes 14966784 | tf_op jit(solution)/shard_map/dot_general | solution.py:49
  144.0 7.3 %fusion.36 = (f32[512]{0:T(512)S(1)}, f32[512]{0:T(512)S(1)}, f32[512,768]{1,0:T(8,128)}) fusion(f32[2,768]{1,0:T(2,128)S(1)} %get-tuple-element.45, f32[512]{0:T(512)S(1)} %add_rsqrt_fusion, f32[512,768]{1,0:T(8,128)S(1)} %get-tuple-element.34, f32[512]{0:T(512)S(1)} %broadcast_multiply_fusion.4, ...), kind=kOutput, calls=%fused_computation.81 | convolution fusion | flops 2418277376 | bytes 11024384 | tf_op jit(solution)/shard_map/dot_general | solution.py:49
  151.4 9.3 %fusion.30 = (f32[768]{0:T(1024)S(1)}, f32[512,768]{1,0:T(8,128)S(1)}, bf16[512,768]{1,0:T(8,128)(2,1)}, f32[768]{0:T(1024)S(1)}, f32[512,768]{1,0:T(8,128)S(1)}) fusion(f32[2,768]{1,0:T(2,128)S(1)} %get-tuple-element.48, f32[512]{0:T(512)S(1)} %get-tuple-element.65, f32[512,768]{1,0:T(8,128)S(1)} %get-tuple-element.34, ...), kind=kOutput, calls=%fused_computation.70 | convolution fusion | flops 2439117312 | bytes 18923008 | tf_op jit(solution)/shard_map/dot_general | solution.py:45
  165.9 16.0 %shard_map.238 = (bf16[512,2304]{1,0:T(8,128)(2,1)}, f32[2,1,1536]{2,1,0:T(1,128)}) custom-call(bf16[512,2304]{1,0:T(8,128)(2,1)} %fusion.11.qkv_ref, bf16[512,768]{1,0:T(8,128)(2,1)} %convolution_convert_fusion.grad_ref), custom_call_target="tpu_custom_call" | custom-call | tf_op jit(solution)/shard_map/pallas_call | solution.py:139
  181.9 5.0 %fusion.35 = (f32[512]{0:T(512)S(1)}, f32[512]{0:T(512)S(1)}, f32[512,768]{1,0:T(8,128)S(1)}) fusion(f32[2,768]{1,0:T(2,128)S(1)} %get-tuple-element.47, f32[512]{0:T(512)S(1)} %add_rsqrt_fusion.1, f32[512]{0:T(512)S(1)} %broadcast_multiply_fusion.5, bf16[512,768]{1,0:T(8,128)(2,1)S(1)} %copy-done.2, bf16[512,2304]{1,0:T(8,128)(2,1)} %get-tuple-element.15, ...), kind=kOutput, calls=%fused_computation.80 | convolution fusion | flops 1814690816 | bytes 8271872 | tf_op jit(solution)/shard_map/dot_general | solution.py:49
  188.7 4.9 %copy.45 = bf16[3072,512]{1,0:T(8,128)(2,1)} copy(bf16[3072,512]{0,1:T(8,128)(2,1)} %get-tuple-element.63) | data formatting | bytes 6291456 | tf_op jit(solution)/shard_map/dot_general | solution.py:53
  304.2 9.9 %collective-permute-done.35 = bf16[1,192,2304]{2,1,0:T(8,128)(2,1)S(1)} collective-permute-done((bf16[1,192,2304]{2,1,0:T(8,128)(2,1)S(1)}, bf16[1,192,2304]{2,1,0:T(8,128)(2,1)S(1)}, u32[]{:S(2)}, u32[]{:S(2)}) %collective-permute-start.35) | collective-permute-done | bytes 884768 | tf_op jit(solution)/shard_map/ppermute | solution.py:166
  318.1 6.5 %collective-permute-done.36 = bf16[96,2304]{1,0:T(8,128)(2,1)S(1)} collective-permute-done((bf16[96,2304]{1,0:T(8,128)(2,1)S(1)}, bf16[96,2304]{1,0:T(8,128)(2,1)S(1)}, u32[]{:S(2)}, u32[]{:S(2)}) %collective-permute-start.36) | collective-permute-done | bytes 442400 | tf_op jit(solution)/shard_map/ppermute | solution.py:166
  334.4 4.9 %collective-permute-done.64 = bf16[1,768,768]{2,1,0:T(8,128)(2,1)S(1)} collective-permute-done((bf16[1,768,768]{2,1,0:T(8,128)(2,1)S(1)}, bf16[1,768,768]{2,1,0:T(8,128)(2,1)S(1)}, u32[]{:S(2)}, u32[]{:S(2)}) %collective-permute-start.64) | collective-permute-done | bytes 1179680 | tf_op jit(solution)/shard_map/ppermute | solution.py:166
  340.9 22.8 %collective-permute-done.56 = bf16[1,192,3072]{2,1,0:T(8,128)(2,1)S(1)} collective-permute-done((bf16[1,192,3072]{2,1,0:T(8,128)(2,1)S(1)}, bf16[1,192,3072]{2,1,0:T(8,128)(2,1)S(1)}, u32[]{:S(2)}, u32[]{:S(2)}) %collective-permute-start.56) | collective-permute-done | bytes 1179680 | tf_op jit(solution)/shard_map/ppermute | solution.py:166
  367.6 11.0 %collective-permute-done.57 = bf16[96,3072]{1,0:T(8,128)(2,1)S(1)} collective-permute-done((bf16[96,3072]{1,0:T(8,128)(2,1)S(1)}, bf16[96,3072]{1,0:T(8,128)(2,1)S(1)}, u32[]{:S(2)}, u32[]{:S(2)}) %collective-permute-start.57) | collective-permute-done | bytes 589856 | tf_op jit(solution)/shard_map/ppermute | solution.py:166
  381.3 7.9 %collective-permute-done.58 = bf16[48,3072]{1,0:T(8,128)(2,1)S(1)} collective-permute-done((bf16[48,3072]{1,0:T(8,128)(2,1)S(1)}, bf16[48,3072]{1,0:T(8,128)(2,1)S(1)}, u32[]{:S(2)}, u32[]{:S(2)}) %collective-permute-start.58) | collective-permute-done | bytes 294944 | tf_op jit(solution)/shard_map/ppermute | solution.py:166
  392.4 9.5 %collective-permute-done.59 = bf16[48,1536]{1,0:T(8,128)(2,1)S(1)} collective-permute-done((bf16[48,1536]{1,0:T(8,128)(2,1)S(1)}, bf16[48,1536]{1,0:T(8,128)(2,1)S(1)}, u32[]{:S(2)}, u32[]{:S(2)}) %collective-permute-start.59) | collective-permute-done | bytes 147488 | tf_op jit(solution)/shard_map/ppermute | solution.py:166
  405.1 4.7 %collective-permute-done.60 = bf16[48,1536]{1,0:T(8,128)(2,1)S(1)} collective-permute-done((bf16[48,1536]{1,0:T(8,128)(2,1)S(1)}, bf16[48,1536]{1,0:T(8,128)(2,1)S(1)}, u32[]{:S(2)}, u32[]{:S(2)}) %collective-permute-start.60) | collective-permute-done | bytes 147488 | tf_op jit(solution)/shard_map/ppermute | solution.py:166
  413.7 6.2 %collective-permute-done.69 = bf16[192,768]{1,0:T(8,128)(2,1)S(1)} collective-permute-done((bf16[192,768]{1,0:T(8,128)(2,1)S(1)}, bf16[192,768]{1,0:T(8,128)(2,1)S(1)}, u32[]{:S(2)}, u32[]{:S(2)}) %collective-permute-start.69) | collective-permute-done | bytes 294944 | tf_op jit(solution)/shard_map/ppermute | solution.py:166
  420.1 5.3 %collective-permute-done.61 = bf16[48,3072]{1,0:T(8,128)(2,1)S(1)} collective-permute-done((bf16[48,3072]{1,0:T(8,128)(2,1)S(1)}, bf16[48,3072]{1,0:T(8,128)(2,1)S(1)}, u32[]{:S(2)}, u32[]{:S(2)}) %collective-permute-start.61) | collective-permute-done | bytes 294944 | tf_op jit(solution)/shard_map/ppermute | solution.py:166
  428.1 11.3 %collective-permute-done.70 = bf16[384,768]{1,0:T(8,128)(2,1)S(1)} collective-permute-done((bf16[384,768]{1,0:T(8,128)(2,1)S(1)}, bf16[384,768]{1,0:T(8,128)(2,1)S(1)}, u32[]{:S(2)}, u32[]{:S(2)}) %collective-permute-start.70) | collective-permute-done | bytes 589856 | tf_op jit(solution)/shard_map/ppermute | solution.py:166
  441.1 8.6 %collective-permute-done.62 = bf16[96,3072]{1,0:T(8,128)(2,1)S(1)} collective-permute-done((bf16[96,3072]{1,0:T(8,128)(2,1)S(1)}, bf16[96,3072]{1,0:T(8,128)(2,1)S(1)}, u32[]{:S(2)}, u32[]{:S(2)}) %collective-permute-start.62) | collective-permute-done | bytes 589856 | tf_op jit(solution)/shard_map/ppermute | solution.py:166
  (406 shorter events, 243.3 us)
Async XLA Ops:
  5.5 41.6 %collective-permute-start.10 = (bf16[192,768]{1,0:T(8,128)(2,1)}, bf16[192,768]{1,0:T(8,128)(2,1)}, u32[]{:S(2)}, u32[]{:S(2)}) collective-permute-start(bf16[192,768]{1,0:T(8,128)(2,1)} %param.22), channel_id=1, source_target_pairs={{0,1},{1,0},{2,3},{3,2},{4,5},{5,4},{6,7},{7,6},{8,9},{9,8},{10,11... | collective-permute-start | bytes 884744 | tf_op jit(solution)/shard_map/ppermute | solution.py:166
  6.5 33.8 %collective-permute-start.8 = (bf16[96,768]{1,0:T(8,128)(2,1)S(1)}, bf16[96,768]{1,0:T(8,128)(2,1)S(1)}, u32[]{:S(2)}, u32[]{:S(2)}) collective-permute-start(bf16[96,768]{1,0:T(8,128)(2,1)S(1)} %constant_dynamic-slice_fusion.6), channel_id=1, source_target_pairs={{0,2},{1,3},{2,0},{3,1},{4,6},{5,7},{6,4},{7,5},{8,10},{9,11},{10,... | collective-permute-start | bytes 442376 | tf_op jit(solution)/shard_map/ppermute | solution.py:166
  9.5 61.9 %collective-permute-start.6 = (bf16[192,2304]{1,0:T(8,128)(2,1)}, bf16[192,2304]{1,0:T(8,128)(2,1)}, u32[]{:S(2)}, u32[]{:S(2)}) collective-permute-start(bf16[192,2304]{1,0:T(8,128)(2,1)} %param.20), channel_id=1, source_target_pairs={{0,1},{1,0},{2,3},{3,2},{4,5},{5,4},{6,7},{7,6},{8,9},{9,8},{10,11... | collective-permute-start | bytes 2654216 | tf_op jit(solution)/shard_map/ppermute | solution.py:166
  11.3 35.8 %collective-permute-start.4 = (bf16[96,2304]{1,0:T(8,128)(2,1)}, bf16[96,2304]{1,0:T(8,128)(2,1)}, u32[]{:S(2)}, u32[]{:S(2)}) collective-permute-start(bf16[96,2304]{1,0:T(8,128)(2,1)} %constant_dynamic-slice_fusion.7), channel_id=1, source_target_pairs={{0,2},{1,3},{2,0},{3,1},{4,6},{5,7},{6,4},{7,5},{8,10},{9,11},{10,... | collective-permute-start | bytes 1327112 | tf_op jit(solution)/shard_map/ppermute | solution.py:166
  55.4 43.3 %collective-permute-start.14 = (bf16[192,3072]{1,0:T(8,128)(2,1)}, bf16[192,3072]{1,0:T(8,128)(2,1)S(1)}, u32[]{:S(2)}, u32[]{:S(2)}) collective-permute-start(bf16[192,3072]{1,0:T(8,128)(2,1)} %param.24), channel_id=1, source_target_pairs={{0,1},{1,0},{2,3},{3,2},{4,5},{5,4},{6,7},{7,6},{8,9},{9,8},{10,11... | collective-permute-start | bytes 3538952 | tf_op jit(solution)/shard_map/ppermute | solution.py:166
  57.2 40.3 %collective-permute-start.18 = (bf16[768,768]{1,0:T(8,128)(2,1)S(1)}, bf16[768,768]{1,0:T(8,128)(2,1)S(1)}, u32[]{:S(2)}, u32[]{:S(2)}) collective-permute-start(bf16[768,768]{1,0:T(8,128)(2,1)S(1)} %copy-done.26), channel_id=1, source_target_pairs={{0,1},{1,0},{2,3},{3,2},{4,5},{5,4},{6,7},{7,6},{8,9},{9,8},{10,11... | collective-permute-start | bytes 3538952 | tf_op jit(solution)/shard_map/ppermute | solution.py:166
  68.6 25.7 %collective-permute-start.13 = (bf16[96,3072]{1,0:T(8,128)(2,1)}, bf16[96,3072]{1,0:T(8,128)(2,1)S(1)}, u32[]{:S(2)}, u32[]{:S(2)}) collective-permute-start(bf16[96,3072]{1,0:T(8,128)(2,1)} %collective-permute-done.12), channel_id=1, source_target_pairs={{0,4},{4,0},{8,12},{12,8},{16,20},{20,16},{24,28},{28,24},{1,5},{5... | collective-permute-start | bytes 1769480 | tf_op jit(solution)/shard_map/ppermute | solution.py:166
  71.4 28.4 %collective-permute-start.7 = (bf16[192,2304]{1,0:T(8,128)(2,1)S(1)}, bf16[192,2304]{1,0:T(8,128)(2,1)S(1)}, u32[]{:S(2)}, u32[]{:S(2)}) collective-permute-start(bf16[192,2304]{1,0:T(8,128)(2,1)S(1)} %get-tuple-element.40), channel_id=1, source_target_pairs={{0,1},{1,0},{2,3},{3,2},{4,5},{5,4},{6,7},{7,6},{8,9},{9,8},{10,11... | collective-permute-start | bytes 2654216 | tf_op jit(solution)/shard_map/ppermute | solution.py:166
  86.3 46.7 %collective-permute-start.19 = (bf16[768,768]{1,0:T(8,128)(2,1)}, bf16[768,768]{1,0:T(8,128)(2,1)}, u32[]{:S(2)}, u32[]{:S(2)}) collective-permute-start(bf16[768,768]{1,0:T(8,128)(2,1)} %get-tuple-element.36), channel_id=1, source_target_pairs={{0,1},{1,0},{2,3},{3,2},{4,5},{5,4},{6,7},{7,6},{8,9},{9,8},{10,11... | collective-permute-start | bytes 3538952 | tf_op jit(solution)/shard_map/ppermute | solution.py:166
  97.5 25.3 %collective-permute-start.15 = (bf16[192,3072]{1,0:T(8,128)(2,1)}, bf16[192,3072]{1,0:T(8,128)(2,1)}, u32[]{:S(2)}, u32[]{:S(2)}) collective-permute-start(bf16[192,3072]{1,0:T(8,128)(2,1)} %get-tuple-element.32), channel_id=1, source_target_pairs={{0,1},{1,0},{2,3},{3,2},{4,5},{5,4},{6,7},{7,6},{8,9},{9,8},{10,11... | collective-permute-start | bytes 3538952 | tf_op jit(solution)/shard_map/ppermute | solution.py:166
  194.2 32.0 %collective-permute-start.42 = (f32[2,1536]{1,0:T(2,128)S(1)}, f32[2,1536]{1,0:T(2,128)S(1)}, u32[]{:S(2)}, u32[]{:S(2)}) collective-permute-start(f32[2,1536]{1,0:T(2,128)S(1)} %constant_dynamic-slice_fusion.2), channel_id=1, source_target_pairs={{0,2},{1,3},{2,0},{3,1},{4,6},{5,7},{6,4},{7,5},{8,10},{9,11},{10,... | collective-permute-start | bytes 36872 | tf_op jit(solution)/shard_map/ppermute | solution.py:166
  195.9 30.7 %collective-permute-start.20 = (bf16[1,2,4608]{2,1,0:T(2,128)(2,1)S(1)}, bf16[1,2,4608]{2,1,0:T(2,128)(2,1)S(1)}, u32[]{:S(2)}, u32[]{:S(2)}) collective-permute-start(bf16[1,2,4608]{2,1,0:T(2,128)(2,1)S(1)} %constant_dynamic-update-slice_fusion), channel_id=1, source_target_pairs={{0,1},{1,0},{2,3},{3,2},{4,5},{5,4},{6,7},{7,6},{8,9},{9,8},{10,11... | collective-permute-start | bytes 55304 | tf_op jit(solution)/shard_map/ppermute | solution.py:166
  196.2 52.8 %collective-permute-start.29 = (bf16[2,4608]{1,0:T(2,128)(2,1)S(1)}, bf16[2,4608]{1,0:T(2,128)(2,1)S(1)}, u32[]{:S(2)}, u32[]{:S(2)}) collective-permute-start(bf16[2,4608]{1,0:T(2,128)(2,1)S(1)} %constant_dynamic-update-slice_fusion.6), channel_id=1, source_target_pairs={{0,16},{4,20},{8,24},{12,28},{16,0},{20,4},{24,8},{28,12},{1,17},{... | collective-permute-start | bytes 55304 | tf_op jit(solution)/shard_map/ppermute | solution.py:166
  202.3 57.1 %collective-permute-start.47 = (bf16[2,1,192,768]{3,2,1,0:T(8,128)(2,1)S(1)}, bf16[2,1,192,768]{3,2,1,0:T(8,128)(2,1)}, u32[]{:S(2)}, u32[]{:S(2)}) collective-permute-start(bf16[2,1,192,768]{3,2,1,0:T(8,128)(2,1)S(1)} %dynamic-slice_convert_fusion.8), channel_id=1, source_target_pairs={{0,1},{1,0},{2,3},{3,2},{4,5},{5,4},{6,7},{7,6},{8,9},{9,8},{10,11... | collective-permute-start | bytes 1769480 | tf_op jit(solution)/shard_map/ppermute | solution.py:166
  206.8 92.0 %collective-permute-start.63 = (bf16[2,1,768,768]{3,2,1,0:T(8,128)(2,1)}, bf16[2,1,768,768]{3,2,1,0:T(8,128)(2,1)}, u32[]{:S(2)}, u32[]{:S(2)}) collective-permute-start(bf16[2,1,768,768]{3,2,1,0:T(8,128)(2,1)} %dynamic-slice_convert_fusion), channel_id=1, source_target_pairs={{0,1},{1,0},{2,3},{3,2},{4,5},{5,4},{6,7},{7,6},{8,9},{9,8},{10,11... | collective-permute-start | bytes 7077896 | tf_op jit(solution)/shard_map/ppermute | solution.py:166
  226.1 62.4 %collective-permute-start.34 = (bf16[2,1,192,2304]{3,2,1,0:T(8,128)(2,1)}, bf16[2,1,192,2304]{3,2,1,0:T(8,128)(2,1)}, u32[]{:S(2)}, u32[]{:S(2)}) collective-permute-start(bf16[2,1,192,2304]{3,2,1,0:T(8,128)(2,1)} %dynamic-slice_convert_fusion.2), channel_id=1, source_target_pairs={{0,1},{1,0},{2,3},{3,2},{4,5},{5,4},{6,7},{7,6},{8,9},{9,8},{10,11... | collective-permute-start | bytes 5308424 | tf_op jit(solution)/shard_map/ppermute | solution.py:166
  277.6 37.9 %collective-permute-start.55 = (bf16[2,1,192,3072]{3,2,1,0:T(8,128)(2,1)}, bf16[2,1,192,3072]{3,2,1,0:T(8,128)(2,1)}, u32[]{:S(2)}, u32[]{:S(2)}) collective-permute-start(bf16[2,1,192,3072]{3,2,1,0:T(8,128)(2,1)} %dynamic-slice_convert_fusion.1), channel_id=1, source_target_pairs={{0,1},{1,0},{2,3},{3,2},{4,5},{5,4},{6,7},{7,6},{8,9},{9,8},{10,11... | collective-permute-start | bytes 7077896 | tf_op jit(solution)/shard_map/ppermute | solution.py:166
  297.8 127.8 %collective-permute-start.54 = (bf16[96,768]{1,0:T(8,128)(2,1)S(1)}, bf16[96,768]{1,0:T(8,128)(2,1)S(1)}, u32[]{:S(2)}, u32[]{:S(2)}) collective-permute-start(bf16[96,768]{1,0:T(8,128)(2,1)S(1)} %maximum_select_fusion.14), channel_id=1, source_target_pairs={{0,4},{4,0},{8,12},{12,8},{16,20},{20,16},{24,28},{28,24},{1,5},{5... | collective-permute-start | bytes 442376 | tf_op jit(solution)/shard_map/ppermute | solution.py:166
  302.7 36.7 %collective-permute-start.64 = (bf16[1,768,768]{2,1,0:T(8,128)(2,1)S(1)}, bf16[1,768,768]{2,1,0:T(8,128)(2,1)S(1)}, u32[]{:S(2)}, u32[]{:S(2)}) collective-permute-start(bf16[1,768,768]{2,1,0:T(8,128)(2,1)S(1)} %fusion.38), channel_id=1, source_target_pairs={{0,2},{1,3},{2,0},{3,1},{4,6},{5,7},{6,4},{7,5},{8,10},{9,11},{10,... | collective-permute-start | bytes 3538952 | tf_op jit(solution)/shard_map/ppermute | solution.py:166
  325.2 38.5 %collective-permute-start.56 = (bf16[1,192,3072]{2,1,0:T(8,128)(2,1)S(1)}, bf16[1,192,3072]{2,1,0:T(8,128)(2,1)S(1)}, u32[]{:S(2)}, u32[]{:S(2)}) collective-permute-start(bf16[1,192,3072]{2,1,0:T(8,128)(2,1)S(1)} %fusion.37), channel_id=1, source_target_pairs={{0,2},{1,3},{2,0},{3,1},{4,6},{5,7},{6,4},{7,5},{8,10},{9,11},{10,... | collective-permute-start | bytes 3538952 | tf_op jit(solution)/shard_map/ppermute | solution.py:166
  330.9 33.9 %collective-permute-start.38 = (bf16[48,1152]{1,0:T(8,128)(2,1)S(1)}, bf16[48,1152]{1,0:T(8,128)(2,1)S(1)}, u32[]{:S(2)}, u32[]{:S(2)}) collective-permute-start(bf16[48,1152]{1,0:T(8,128)(2,1)S(1)} %dynamic-slice_convert_fusion.17), channel_id=1, source_target_pairs={{0,16},{4,20},{8,24},{12,28},{16,0},{20,4},{24,8},{28,12},{1,17},{... | collective-permute-start | bytes 331784 | tf_op jit(solution)/shard_map/ppermute | solution.py:166
  339.6 27.3 %collective-permute-start.65 = (bf16[384,768]{1,0:T(8,128)(2,1)S(1)}, bf16[384,768]{1,0:T(8,128)(2,1)S(1)}, u32[]{:S(2)}, u32[]{:S(2)}) collective-permute-start(bf16[384,768]{1,0:T(8,128)(2,1)S(1)} %fusion.48), channel_id=1, source_target_pairs={{0,4},{4,0},{8,12},{12,8},{16,20},{20,16},{24,28},{28,24},{1,5},{5... | collective-permute-start | bytes 1769480 | tf_op jit(solution)/shard_map/ppermute | solution.py:166
  364.8 37.1 %collective-permute-start.39 = (bf16[48,1152]{1,0:T(8,128)(2,1)S(1)}, bf16[48,1152]{1,0:T(8,128)(2,1)S(1)}, u32[]{:S(2)}, u32[]{:S(2)}) collective-permute-start(bf16[48,1152]{1,0:T(8,128)(2,1)S(1)} %add_convert_fusion.2), channel_id=1, source_target_pairs={{0,16},{4,20},{8,24},{12,28},{16,0},{20,4},{24,8},{28,12},{1,17},{... | collective-permute-start | bytes 331784 | tf_op jit(solution)/shard_map/ppermute | solution.py:166
  425.6 24.1 %collective-permute-start.62 = (bf16[96,3072]{1,0:T(8,128)(2,1)S(1)}, bf16[96,3072]{1,0:T(8,128)(2,1)S(1)}, u32[]{:S(2)}, u32[]{:S(2)}) collective-permute-start(bf16[96,3072]{1,0:T(8,128)(2,1)S(1)} %maximum_select_fusion.6), channel_id=1, source_target_pairs={{0,4},{4,0},{8,12},{12,8},{16,20},{20,16},{24,28},{28,24},{1,5},{5... | collective-permute-start | bytes 1769480 | tf_op jit(solution)/shard_map/ppermute | solution.py:166
  (91 other events, 720.8 us)

commit v2 on v1

v2 whole, which is shorter than its diff:
```python
import functools

import jax
import jax.numpy as jnp
from jax import lax
from jax.experimental import pallas as pl
from jax.experimental.pallas import tpu as pltpu
from jax.sharding import PartitionSpec as P

HEADS = 12
HEAD_DIM = 64
EPS = 1e-06
GELU_C = 0.7978845608028654
GELU_A = 0.044715
F32 = jnp.float32
BF16 = jnp.bfloat16
VMEM_LIMIT = 56 * 1024 * 1024


def norm_back(grad_hat, normed, inv_std):
    return inv_std * (
        grad_hat
        - jnp.mean(grad_hat, axis=-1, keepdims=True)
        - normed * jnp.mean(grad_hat * normed, axis=-1, keepdims=True)
    )


def gelu_pair(pre_act):
    square = pre_act * pre_act
    tanh_val = jnp.tanh(pre_act * (GELU_C + GELU_C * GELU_A * square))
    half = 0.5 + 0.5 * tanh_val
    activated = pre_act * half
    derivative = half + activated * (1.0 - tanh_val) * (GELU_C + 3.0 * GELU_C * GELU_A * square)
    return (activated, derivative)


def dot_nn(left, right):
    return lax.dot_general(left, right, (((1,), (0,)), ((), ())), preferred_element_type=F32)


def dot_nt(left, right):
    return lax.dot_general(left, right, (((1,), (1,)), ((), ())), preferred_element_type=F32)


def dot_tn(left, right):
    return lax.dot_general(left, right, (((0,), (0,)), ((), ())), preferred_element_type=F32)


def specs(count, space=pltpu.VMEM):
    return [pl.BlockSpec(memory_space=space)] * count


def shape(dims, dtype):
    return jax.ShapeDtypeStruct(dims, dtype)


COST_SHARE = 0.0


def params(flops=0, bytes_moved=0, exps=0):
    return dict(
        compiler_params=pltpu.CompilerParams(vmem_limit_bytes=VMEM_LIMIT),
        cost_estimate=pl.CostEstimate(
            flops=int(COST_SHARE * flops),
            bytes_accessed=int(COST_SHARE * bytes_moved),
            transcendentals=int(COST_SHARE * exps),
        ),
    )


def high_bit(spot_ref, number, bit):
    return lax.rem(lax.div(spot_ref[number], jnp.int32(bit)), jnp.int32(2))


def piece_copies(refs, offsets, spot_ref, whole, sems):
    copies = []
    for k, (ref, offset) in enumerate(zip(refs, offsets)):
        count = ref.shape[0]
        place = whole.at[pl.ds(pl.multiple_of((spot_ref[0] ^ offset) * count, 16), count), :]
        copies.append(pltpu.make_async_copy(ref, place, sems.at[k]))
    return copies


def row_norm(value):
    center = value - jnp.mean(value, axis=-1, keepdims=True)
    inv_std = lax.rsqrt(jnp.mean(center * center, axis=-1, keepdims=True) + EPS)
    return center * inv_std, inv_std


def mod_part(mod_ref, slot, part, width):
    return mod_ref[slot : slot + 1, part * width : (part + 1) * width]


def qkv_kernel(offsets, slots, *refs):
    count = len(offsets)
    spot_ref, tok_ref, mod_ref, bias_ref = refs[:4]
    pieces = refs[4 : 4 + count]
    hidden_ref, qkv_ref, whole, sems = refs[4 + count :]
    copies = piece_copies(pieces, offsets, spot_ref, whole, sems)
    for copy in copies:
        copy.start()
    rows, width = tok_ref.shape
    seq = rows // slots
    for slot in range(slots):
        at = pl.ds(slot * seq, seq)
        normed, _ = row_norm(tok_ref[at, :].astype(F32))
        scale = 1.0 + mod_part(mod_ref, slot, 1, width)
        hidden_ref[at, :] = (normed * scale + mod_part(mod_ref, slot, 0, width)).astype(BF16)
    for copy in copies:
        copy.wait()
    for part in range(3):
        cols = pl.ds(part * width, width)
        qkv_ref[:, cols] = (
            dot_nn(hidden_ref[...], whole[:, cols]) + bias_ref[:, cols]
        ).astype(BF16)


def qkv_call(spot, tokens, modulation, bias, weight, slots):
    rows, width = tokens.shape
    pieces, offsets = weight
    return pl.pallas_call(
        functools.partial(qkv_kernel, offsets, slots),
        in_specs=specs(1, pltpu.SMEM) + specs(3) + specs(len(pieces), pl.ANY),
        out_specs=specs(2),
        out_shape=[shape((rows, width), BF16), shape((rows, 3 * width), BF16)],
        scratch_shapes=[
            pltpu.VMEM((width, 3 * width), BF16),
            pltpu.SemaphoreType.DMA((len(pieces),)),
        ],
        name="qkv_fwd",
        **params(6 * rows * width * width, 10 * rows * width + 6 * width * width),
    )(spot, tokens, modulation, bias, *pieces)


def pair_masks(rows):
    lane = lax.broadcasted_iota(jnp.int32, (rows, 2 * HEAD_DIM), 1)
    return lane < HEAD_DIM


def head_probs(query_pair, key_pair, first, head):
    keep = first if head == 0 else jnp.logical_not(first)
    query_head = jnp.where(keep, query_pair, jnp.zeros_like(query_pair))
    scores = dot_nt(query_head, key_pair) * HEAD_DIM ** (-0.5)
    row_max = jnp.max(scores, axis=-1, keepdims=True)
    exped = jnp.exp(scores - row_max)
    return exped * (1.0 / jnp.sum(exped, axis=-1, keepdims=True))


def attn_kernel(offsets, *refs):
    count = len(offsets)
    spot_ref, qkv_ref, tok_ref, cot_ref, mod_ref, bias_ref = refs[:6]
    pieces = refs[6 : 6 + count]
    mixed_ref, branch_ref, hidden_ref, low_ref, whole, sems = refs[6 + count :]
    rows, width = tok_ref.shape
    copies = piece_copies(pieces, offsets, spot_ref, whole, sems)

    @pl.when(pl.program_id(0) == 0)
    def _():
        for copy in copies:
            copy.start()

    first = pair_masks(rows)
    for pair in range(HEADS // 2):
        cols = pl.ds(pair * 128, 128)
        query_pair = qkv_ref[:, cols]
        key_pair = qkv_ref[:, pl.ds(width + pair * 128, 128)]
        value_pair = qkv_ref[:, pl.ds(2 * width + pair * 128, 128)]
        parts = []
        for head in range(2):
            probs_low = head_probs(query_pair, key_pair, first, head).astype(BF16)
            parts.append(dot_nn(probs_low, value_pair))
        mixed_ref[:, cols] = jnp.where(first, parts[0], parts[1]).astype(BF16)

    @pl.when(pl.program_id(0) == 0)
    def _():
        for copy in copies:
            copy.wait()

    mod = mod_ref[0]
    branch = dot_nn(mixed_ref[...], whole[...]) + bias_ref[...]
    branch_ref[...] = branch
    normed, _ = row_norm(tok_ref[...].astype(F32) + mod_part(mod, 0, 2, width) * branch)
    scale = 1.0 + mod_part(mod, 0, 4, width)
    hidden_ref[...] = (normed * scale + mod_part(mod, 0, 3, width)).astype(BF16)
    low_ref[...] = (mod_part(mod, 0, 5, width) * cot_ref[...].astype(F32)).astype(BF16)


def attn_call(spot, qkv, tokens, cot, modulation, bias, weight, slots):
    rows, width = tokens.shape
    seq = rows // slots
    pieces, offsets = weight
    by_slot = pl.BlockSpec((seq, width), lambda s: (s, 0))
    return pl.pallas_call(
        functools.partial(attn_kernel, offsets),
        grid=(slots,),
        in_specs=specs(1, pltpu.SMEM)
        + [
            pl.BlockSpec((seq, 3 * width), lambda s: (s, 0)),
            by_slot,
            by_slot,
            pl.BlockSpec((1, 1, 6 * width), lambda s: (s, 0, 0)),
            pl.BlockSpec((1, width), lambda s: (0, 0)),
        ]
        + specs(len(pieces), pl.ANY),
        out_specs=[by_slot] * 4,
        out_shape=[
            shape((rows, width), BF16),
            shape((rows, width), F32),
            shape((rows, width), BF16),
            shape((rows, width), BF16),
        ],
        scratch_shapes=[
            pltpu.VMEM((width, width), BF16),
            pltpu.SemaphoreType.DMA((len(pieces),)),
        ],
        name="attn_fwd",
        **params(
            2 * rows * width * width + 4 * rows * width * seq * 4,
            24 * rows * width,
            rows * seq * HEADS,
        ),
    )(spot, qkv, tokens, cot, modulation[:, None, :], bias, *pieces)


FF_BLOCK = 512


def gelu_kernel(offsets, *refs):
    count = len(offsets)
    spot_ref, hidden_ref, bias_ref = refs[:3]
    pieces = refs[3 : 3 + count]
    act_ref, deriv_ref, whole, sems = refs[3 + count :]
    step = pl.program_id(0)

    @pl.when(step == 0)
    def _():
        copies = piece_copies(pieces, offsets, spot_ref, whole, sems)
        for copy in copies:
            copy.start()
        for copy in copies:
            copy.wait()

    cols = pl.ds(pl.multiple_of(step * FF_BLOCK, FF_BLOCK), FF_BLOCK)
    pre_act = dot_nn(hidden_ref[...], whole[:, cols]) + bias_ref[...]
    activated, derivative = gelu_pair(pre_act)
    act_ref[...] = activated.astype(BF16)
    deriv_ref[...] = derivative


def gelu_call(spot, hidden, bias, weight):
    rows, width = hidden.shape
    pieces, offsets = weight
    hidden_units = bias.shape[1]
    block = pl.BlockSpec((rows, FF_BLOCK), lambda j: (0, j))
    return pl.pallas_call(
        functools.partial(gelu_kernel, offsets),
        grid=(hidden_units // FF_BLOCK,),
        in_specs=specs(1, pltpu.SMEM)
        + [
            pl.BlockSpec((rows, width), lambda j: (0, 0)),
            pl.BlockSpec((1, FF_BLOCK), lambda j: (0, j)),
        ]
        + specs(len(pieces), pl.ANY),
        out_specs=[block, block],
        out_shape=[shape((rows, hidden_units), BF16), shape((rows, hidden_units), F32)],
        scratch_shapes=[
            pltpu.VMEM((width, hidden_units), BF16),
            pltpu.SemaphoreType.DMA((len(pieces),)),
        ],
        name="fc1_gelu",
        **params(
            2 * rows * width * hidden_units, 8 * rows * hidden_units, rows * hidden_units
        ),
    )(spot, hidden, bias, *pieces)


def out_kernel(offsets, slots, *refs):
    count = len(offsets)
    spot_ref, live_ref, act_ref, tok_ref, branch_ref, cot_ref, mod_ref, bias_ref = refs[:8]
    pieces = refs[8 : 8 + count]
    block_ref, gate_ref, whole, sems = refs[8 + count :]
    copies = piece_copies(pieces, offsets, spot_ref, whole, sems)
    for copy in copies:
        copy.start()
    for copy in copies:
        copy.wait()
    rows, width = tok_ref.shape
    seq = rows // slots
    for slot in range(slots):
        at = pl.ds(slot * seq, seq)
        branch_two = dot_nn(act_ref[at, :], whole[...]) + bias_ref[...]
        gate_ref[slot : slot + 1, :] = jnp.sum(
            cot_ref[at, :].astype(F32) * branch_two, axis=0, keepdims=True
        )
        mid = tok_ref[at, :].astype(F32) + mod_part(mod_ref, slot, 2, width) * branch_ref[at, :]
        block = mid + mod_part(mod_ref, slot, 5, width) * branch_two
        block_ref[at, :] = jnp.where(live_ref[0] > slot, block, 0.0).astype(BF16)


def out_call(spot, counts, act_low, tokens, branch_one, cot, modulation, bias, weight, slots):
    rows, width = tokens.shape
    hidden_units = act_low.shape[1]
    pieces, offsets = weight
    return pl.pallas_call(
        functools.partial(out_kernel, offsets, slots),
        in_specs=specs(2, pltpu.SMEM) + specs(6) + specs(len(pieces), pl.ANY),
        out_specs=specs(2),
        out_shape=[shape((rows, width), BF16), shape((slots, width), F32)],
        scratch_shapes=[
            pltpu.VMEM((hidden_units, width), BF16),
            pltpu.SemaphoreType.DMA((len(pieces),)),
        ],
        name="fc2_fwd",
        **params(2 * rows * width * hidden_units, 2 * (rows + width) * hidden_units),
    )(spot, counts, act_low, tokens, branch_one, cot, modulation, bias, *pieces)


def mlp_bwd_kernel(offsets, slots, *refs):
    count = len(offsets)
    spot_ref, low_ref, deriv_ref, tok_ref, branch_ref, cot_ref, mod_ref = refs[:7]
    one_pieces = refs[7 : 7 + count]
    two_pieces = refs[7 + count : 7 + 2 * count]
    (low_pre_ref, fc1_b_ref, mid_ref, low_one_ref, sums_ref, one, two, acc, sems_one, sems_two) = refs[
        7 + 2 * count :
    ]
    step = pl.program_id(0)
    copies_two = piece_copies(two_pieces, offsets, spot_ref, two, sems_two)
    copies_one = piece_copies(one_pieces, offsets, spot_ref, one, sems_one)

    @pl.when(step == 0)
    def _():
        for copy in copies_two + copies_one:
            copy.start()
        acc[...] = jnp.zeros_like(acc)
        for copy in copies_two:
            copy.wait()

    ff = pl.ds(pl.multiple_of(step * FF_BLOCK, FF_BLOCK), FF_BLOCK)
    grad_pre = dot_nt(low_ref[...], two[ff, :]) * deriv_ref[...]
    fc1_b_ref[...] = jnp.sum(grad_pre, axis=0, keepdims=True)
    low_pre = grad_pre.astype(BF16)
    low_pre_ref[...] = low_pre

    @pl.when(step == 0)
    def _():
        for copy in copies_one:
            copy.wait()

    acc[...] += dot_nt(low_pre, one[:, ff])

    @pl.when(step == pl.num_programs(0) - 1)
    def _():
        rows, width = tok_ref.shape
        seq = rows // slots
        for slot in range(slots):
            at = pl.ds(slot * seq, seq)
            branch = branch_ref[at, :]
            cot = cot_ref[at, :].astype(F32)
            gate_one = mod_part(mod_ref, slot, 2, width)
            normed, inv_std = row_norm(tok_ref[at, :].astype(F32) + gate_one * branch)
            grad_hidden = acc[at, :]
            scale = 1.0 + mod_part(mod_ref, slot, 4, width)
            grad_mid = cot + norm_back(grad_hidden * scale, normed, inv_std)
            mid_ref[at, :] = grad_mid
            grad_branch = gate_one * grad_mid
            low_one_ref[at, :] = grad_branch.astype(BF16)

            def put(part, value):
                sums_ref[part, slot : slot + 1, :] = jnp.sum(value, axis=0, keepdims=True)

            put(0, grad_mid * branch)
            put(1, grad_hidden)
            put(2, grad_hidden * normed)
            put(3, grad_branch)
            put(4, mod_part(mod_ref, slot, 5, width) * cot)


def mlp_bwd_call(spot, low_two, derivative, tokens, branch_one, cot, modulation, one, two, slots):
    rows, width = tokens.shape
    hidden_units = derivative.shape[1]
    block = pl.BlockSpec((rows, FF_BLOCK), lambda j: (0, j))
    whole = pl.BlockSpec((rows, width), lambda j: (0, 0))
    return pl.pallas_call(
        functools.partial(mlp_bwd_kernel, one[1], slots),
        grid=(hidden_units // FF_BLOCK,),
        in_specs=specs(1, pltpu.SMEM)
        + [whole, block, whole, whole, whole, pl.BlockSpec((slots, 6 * width), lambda j: (0, 0))]
        + specs(len(one[0]) + len(two[0]), pl.ANY),
        out_specs=[
            block,
            pl.BlockSpec((1, FF_BLOCK), lambda j: (0, j)),
            whole,
            whole,
            pl.BlockSpec((5, slots, width), lambda j: (0, 0, 0)),
        ],
        out_shape=[
            shape((rows, hidden_units), BF16),
            shape((1, hidden_units), F32),
            shape((rows, width), F32),
            shape((rows, width), BF16),
            shape((5, slots, width), F32),
        ],
        scratch_shapes=[
            pltpu.VMEM((width, hidden_units), BF16),
            pltpu.VMEM((hidden_units, width), BF16),
            pltpu.VMEM((rows, width), F32),
            pltpu.SemaphoreType.DMA((len(one[0]),)),
            pltpu.SemaphoreType.DMA((len(two[0]),)),
        ],
        name="mlp_bwd",
        **params(4 * rows * width * hidden_units, 6 * rows * hidden_units + 4 * width * hidden_units),
    )(spot, low_two, derivative, tokens, branch_one, cot, modulation, *one[0], *two[0])


def attn_bwd_kernel(qkv_ref, grad_ref, out_ref, bias_ref):
    rows = qkv_ref.shape[0]
    width = grad_ref.shape[1]
    first = pair_masks(rows)
    for pair in range(HEADS // 2):
        query_cols = pl.ds(pair * 128, 128)
        key_cols = pl.ds(width + pair * 128, 128)
        value_cols = pl.ds(2 * width + pair * 128, 128)
        query_pair = qkv_ref[:, query_cols]
        key_pair = qkv_ref[:, key_cols]
        value_pair = qkv_ref[:, value_cols]
        grad_pair = grad_ref[:, query_cols]
        grads = []
        for head in range(2):
            keep = first if head == 0 else jnp.logical_not(first)
            probs = head_probs(query_pair, key_pair, first, head)
            grad_head = jnp.where(keep, grad_pair, jnp.zeros_like(grad_pair))
            grad_probs = dot_nt(grad_head, value_pair)
            row_dot = jnp.sum(probs * grad_probs, axis=-1, keepdims=True)
            grad_scores = (probs * (grad_probs - row_dot) * HEAD_DIM ** (-0.5)).astype(BF16)
            grads.append(
                (
                    dot_nn(grad_scores, key_pair),
                    dot_tn(grad_scores, query_pair),
                    dot_tn(probs.astype(BF16), grad_pair),
                )
            )
        grad_query, grad_key, grad_value = (
            jnp.where(first, left, right) for left, right in zip(grads[0], grads[1])
        )
        out_ref[:, query_cols] = grad_query.astype(BF16)
        out_ref[:, key_cols] = grad_key.astype(BF16)
        out_ref[:, value_cols] = grad_value.astype(BF16)
        bias_ref[0, :, query_cols] = jnp.sum(grad_query, axis=0, keepdims=True)
        bias_ref[0, :, key_cols] = jnp.sum(grad_value, axis=0, keepdims=True)


def attn_bwd_call(qkv, grad_mixed, slots):
    rows, width = grad_mixed.shape
    seq = rows // slots
    return pl.pallas_call(
        attn_bwd_kernel,
        grid=(slots,),
        in_specs=[
            pl.BlockSpec((seq, 3 * width), lambda s: (s, 0)),
            pl.BlockSpec((seq, width), lambda s: (s, 0)),
        ],
        out_specs=[
            pl.BlockSpec((seq, 3 * width), lambda s: (s, 0)),
            pl.BlockSpec((1, 1, 2 * width), lambda s: (s, 0, 0)),
        ],
        out_shape=[
            shape((rows, 3 * width), BF16),
            shape((slots, 1, 2 * width), F32),
        ],
        name="attn_bwd",
        **params(20 * rows * width * seq, 16 * rows * width, rows * seq * HEADS),
    )(qkv, grad_mixed)


def mixed_bwd_kernel(offsets, *refs):
    count = len(offsets)
    spot_ref, low_ref = refs[:2]
    pieces = refs[2 : 2 + count]
    out_ref, whole, sems = refs[2 + count :]
    copies = piece_copies(pieces, offsets, spot_ref, whole, sems)
    for copy in copies:
        copy.start()
    for copy in copies:
        copy.wait()
    out_ref[...] = dot_nt(low_ref[...], whole[...]).astype(BF16)


def mixed_bwd_call(spot, low_one, weight):
    rows, width = low_one.shape
    pieces, offsets = weight
    return pl.pallas_call(
        functools.partial(mixed_bwd_kernel, offsets),
        in_specs=specs(1, pltpu.SMEM) + specs(1) + specs(len(pieces), pl.ANY),
        out_specs=pl.BlockSpec(memory_space=pltpu.VMEM),
        out_shape=shape((rows, width), BF16),
        scratch_shapes=[
            pltpu.VMEM((width, width), BF16),
            pltpu.SemaphoreType.DMA((len(pieces),)),
        ],
        name="proj_bwd",
        **params(2 * rows * width * width, 4 * rows * width + 2 * width * width),
    )(spot, low_one, *pieces)


def input_bwd_kernel(offsets, slots, *refs):
    count = len(offsets)
    spot_ref, grad_ref, tok_ref, mid_ref, mod_ref, sums_ref, gate_ref, cond_ref = refs[:8]
    pieces = refs[8 : 8 + count]
    out_ref, mod_out, whole, sems = refs[8 + count :]
    copies = piece_copies(pieces, offsets, spot_ref, whole, sems)
    for copy in copies:
        copy.start()
    for copy in copies:
        copy.wait()
    rows, width = tok_ref.shape
    seq = rows // slots

    def put(slot, part, value):
        mod_out[slot : slot + 1, part * width : (part + 1) * width] = value.astype(BF16)

    for slot in range(slots):
        at = pl.ds(slot * seq, seq)
        row = slice(slot, slot + 1)
        grad_hidden = dot_nt(grad_ref[at, :], whole[...])
        normed, inv_std = row_norm(tok_ref[at, :].astype(F32))
        scale = 1.0 + mod_part(mod_ref, slot, 1, width)
        out_ref[at, :] = mid_ref[at, :] + norm_back(grad_hidden * scale, normed, inv_std)
        put(slot, 0, jnp.sum(grad_hidden, axis=0, keepdims=True))
        put(slot, 1, jnp.sum(grad_hidden * normed, axis=0, keepdims=True))
        for part in range(3):
            put(slot, 2 + part, sums_ref[part, row, :])
        put(slot, 5, gate_ref[row, :])
        cond = cond_ref[row, :].astype(F32)
        put(slot, 6, cond * (1.0 / (1.0 + jnp.exp(-cond))))


def input_bwd_call(spot, grad_qkv, tokens, grad_mid, modulation, sums, gate_sums, condition, weight, slots):
    rows, width = tokens.shape
    pieces, offsets = weight
    return pl.pallas_call(
        functools.partial(input_bwd_kernel, offsets, slots),
        in_specs=specs(1, pltpu.SMEM) + specs(7) + specs(len(pieces), pl.ANY),
        out_specs=specs(2),
        out_shape=[shape((rows, width), F32), shape((slots, 7 * width), BF16)],
        scratch_shapes=[
            pltpu.VMEM((width, 3 * width), BF16),
            pltpu.SemaphoreType.DMA((len(pieces),)),
        ],
        name="qkv_bwd",
        **params(6 * rows * width * width, 16 * rows * width + 6 * width * width),
    )(spot, grad_qkv, tokens, grad_mid, modulation, sums, gate_sums, condition, *pieces)


def split_store(core, total, depth, keep_ref, send_ref, cols):
    for far in range(total.shape[0] // (2 * depth)):
        even = total[2 * far * depth : (2 * far + 1) * depth]
        odd = total[(2 * far + 1) * depth : (2 * far + 2) * depth]
        keep_ref[far, :, cols] = jnp.where(core == 0, even, odd)
        send_ref[far, :, cols] = jnp.where(core == 0, odd, even).astype(BF16)


def wide_grad_kernel(spot_ref, left_ref, right_ref, keep_ref, send_ref):
    total = dot_tn(left_ref[...], right_ref[...])
    split_store(spot_ref[0] & 1, total, keep_ref.shape[1], keep_ref, send_ref, slice(None))


def wide_grad(spot, left, right, shards, name):
    rows, in_dim = left.shape
    out_dim = right.shape[1]
    depth = in_dim // shards
    block = 512 if out_dim % 512 == 0 else 256
    per_step = shards // 2 if in_dim <= 768 else 1
    out_block = pl.BlockSpec((per_step, depth, block), lambda i, j: (i, 0, j))
    dims = (shards // 2, depth, out_dim)
    return pl.pallas_call(
        wide_grad_kernel,
        grid=(shards // 2 // per_step, out_dim // block),
        in_specs=specs(1, pltpu.SMEM)
        + [
            pl.BlockSpec((rows, 2 * depth * per_step), lambda i, j: (0, i)),
            pl.BlockSpec((rows, block), lambda i, j: (0, j)),
        ],
        out_specs=[out_block, out_block],
        out_shape=[shape(dims, F32), shape(dims, BF16)],
        name=name,
        **params(2 * rows * in_dim * out_dim, 3 * in_dim * out_dim + 2 * rows * (in_dim + out_dim)),
    )(spot, left, right)


EXTRA = 256


def bias_rows(count):
    return [(start, min(EXTRA, count - start)) for start in range(0, count, EXTRA)]


def attn_grad_kernel(shards, *refs):
    spot_ref, hidden_ref, qkv_ref, mixed_ref, low_ref, qv_ref, sums_ref, fc1_ref = refs[:8]
    keep_a, send_a, keep_b, send_b, extra = refs[8:]
    depth = keep_a.shape[1]
    width = hidden_ref.shape[1]
    core = spot_ref[0] & 1
    for part, (keep_ref, send_ref) in enumerate([(keep_a, send_a)] * 2 + [(keep_b, send_b)]):
        total = dot_tn(hidden_ref[...], qkv_ref[:, pl.ds(part * width, width)])
        split_store(core, total, depth, keep_ref, send_ref, pl.ds(part % 2 * width, width))
    total = dot_tn(mixed_ref[...], low_ref[...])
    split_store(core, total, depth, keep_b, send_b, pl.ds(width, width))
    extra[...] = jnp.zeros_like(extra)
    biases = (
        jnp.sum(qv_ref[...], axis=0),
        jnp.sum(sums_ref[3], axis=0, keepdims=True),
        fc1_ref[...],
        jnp.sum(sums_ref[4], axis=0, keepdims=True),
    )
    for place in range(shards):
        row = place * depth
        for bias in biases:
            count = bias.shape[1] // shards
            for start, size in bias_rows(count):
                first = place * count + start
                extra[row : row + 1, :size] = bias[:, first : first + size]
                row += 1
    split_store(core, extra[...], depth, keep_b, send_b, pl.ds(2 * width, EXTRA))


def attn_grad(spot, hidden, grad_qkv, mixed, low_one, qv_sums, sums, fc1_sums, shards):
    rows, width = hidden.shape
    first = (shards // 2, width // shards, 2 * width)
    second = (shards // 2, width // shards, 2 * width + EXTRA)
    outs = pl.pallas_call(
        functools.partial(attn_grad_kernel, shards),
        in_specs=specs(1, pltpu.SMEM) + specs(7),
        out_specs=specs(4),
        out_shape=[shape(first, F32), shape(first, BF16), shape(second, F32), shape(second, BF16)],
        scratch_shapes=[pltpu.VMEM((width, EXTRA), F32)],
        name="attn_weight_grads",
        **params(8 * rows * width * width, 12 * width * width + 14 * rows * width),
    )(spot, hidden, grad_qkv, mixed, low_one, qv_sums, sums, fc1_sums)
    return outs[:2], outs[2:]


def round_kernel(kinds, spot_ref, *refs):
    ins = list(refs[: sum(kind[1] for kind in kinds)])
    outs = list(refs[len(ins) :])
    for kind, count in kinds:
        args, ins = ins[:count], ins[count:]
        if kind == "halve":
            keep_out, send_out, outs = outs[0], outs[1], outs[2:]
            keep_out[...] = args[0][...] + args[2][...].astype(F32)
            send_out[...] = (args[1][...] + args[3][...].astype(F32)).astype(BF16)
        elif kind == "merge":
            keep_out, send_out, outs = outs[0], outs[1], outs[2:]
            half = keep_out.shape[2] // 2
            for part in range(2):
                mine, other, sent_mine, sent_other = args[4 * part : 4 * part + 4]
                cols = slice(part * half, (part + 1) * half)
                keep_out[:, :, cols] = mine[...] + sent_mine[...].astype(F32)
                send_out[:, :, cols] = (other[...] + sent_other[...].astype(F32)).astype(BF16)
        elif kind == "add":
            out, outs = outs[0], outs[1:]
            out[...] = (args[0][...].astype(F32) + args[1][...].astype(F32)).astype(BF16)
        else:
            out, outs = outs[0], outs[1:]
            rows = args[0].shape[1]
            out[:, :rows, :] = args[0][...]
            out[:, rows:, :] = args[1][...]


def round_call(spot, jobs):
    split = 2
    for job in jobs:
        cols = job["args"][0].shape[2] // (1 if job.get("part") is None else 2)
        if job["kind"] == "merge" or cols % 256:
            split = 1
    in_specs, args, out_specs, out_shape = [], [], [], []

    def halves_of(value, axis, bit, dim, base, dims, chunk):
        def spec(other):
            def place(j, spot_ref):
                half = high_bit(spot_ref, axis.number, bit)
                half = 1 - half if other else half
                return (half, 0, base + j) if dim == 0 else (0, half, base + j)

            return pl.BlockSpec((dims[0], dims[1], chunk), place)

        in_specs.extend([spec(False), spec(True)])
        args.extend([value, value])

    def plain(dims):
        return pl.BlockSpec((dims[0], dims[1], dims[2] // split), lambda j, spot_ref: (0, 0, j))

    kinds = []
    for job in jobs:
        values = job["args"]
        kind = job["kind"]
        dims = list(values[0].shape)
        before = len(args)
        if kind in ("halve", "merge"):
            axis, bit, dim = job["step"]
            dims[dim] //= 2
            part = job.get("part")
            if part is not None:
                dims[2] //= 2
            chunk = dims[2] // split
            base = 0 if part is None else part * split
            for value in values:
                halves_of(value, axis, bit, dim, base, dims, chunk)
            if kind == "merge":
                dims[2] *= 2
            out_specs += [plain(dims)] * 2
            out_shape += [shape(tuple(dims), F32), shape(tuple(dims), BF16)]
        else:
            in_specs += [plain(value.shape) for value in values]
            args += values
            if kind == "cat":
                dims[1] += values[1].shape[1]
            out_specs.append(plain(dims))
            out_shape.append(shape(tuple(dims), BF16))
        kinds.append((kind, len(args) - before))
    outs = pl.pallas_call(
        functools.partial(round_kernel, kinds),
        grid_spec=pltpu.PrefetchScalarGridSpec(
            num_scalar_prefetch=1, grid=(split,), in_specs=in_specs, out_specs=out_specs
        ),
        out_shape=out_shape,
        name="sum_round",
        **params(0, 0),
    )(spot, *args)
    outs = list(outs)
    results = []
    for kind, _ in kinds:
        count = 2 if kind in ("halve", "merge") else 1
        results.append(outs[:count])
        outs = outs[count:]
    return results


def first_row(spot_ref, terms, flips):
    row = 0
    for (number, bit, size), flip in zip(terms, flips):
        half = high_bit(spot_ref, number, bit)
        row = row + (1 - half if flip else half) * size
    return row


def row_places(spot_ref, refs, terms, flips, count):
    parts = []
    for ref in refs:
        parts += [(ref, slice(k * count, (k + 1) * count)) for k in range(ref.shape[1] // count)]
    for (ref, rows), flip in zip(parts, flips):
        at = first_row(spot_ref, terms, flip)
        if not isinstance(at, int):
            at = pl.multiple_of(at, 16)
        yield ref, rows, pl.ds(at, count)


def place_kernel(terms, flips, count, spot_ref, *refs):
    out_ref = refs[-1]
    for ref, rows, at in row_places(spot_ref, refs[:-1], terms, flips, count):
        out_ref[at, :] = ref[0, rows, :].astype(F32)


def place_rows(spot, done, rows):
    pieces, terms, flips, count = done
    cols = pieces[0].shape[2]
    return pl.pallas_call(
        functools.partial(place_kernel, terms, flips, count),
        in_specs=specs(1, pltpu.SMEM) + specs(len(pieces)),
        out_specs=pl.BlockSpec(memory_space=pltpu.VMEM),
        out_shape=shape((rows, cols), F32),
        name="place_rows",
        **params(0, rows * cols * 6),
    )(spot, *pieces)


def place_attn_kernel(plans, parts, biases, spot_ref, *refs):
    qkv_out, proj_out, *bias_outs, head = refs[2 * parts :]
    width = proj_out.shape[1]
    for ref, rows, at in row_places(spot_ref, refs[:parts], *plans[0]):
        qkv_out[at, : 2 * width] = ref[0, rows, :].astype(F32)
    for ref, rows, at in row_places(spot_ref, refs[parts : 2 * parts], *plans[1]):
        qkv_out[at, 2 * width :] = ref[0, rows, :width].astype(F32)
        proj_out[at, :] = ref[0, rows, width : 2 * width].astype(F32)
        head[at, :] = ref[0, rows, 2 * width :].astype(F32)
    row = 0
    for count, out in zip(biases, bias_outs):
        for start, size in bias_rows(count):
            out[:, start : start + size] = head[row : row + 1, :size]
            row += 1


def place_attn(spot, first, second, rows, width, biases):
    parts = len(first[0])
    return pl.pallas_call(
        functools.partial(place_attn_kernel, (first[1:], second[1:]), parts, biases),
        in_specs=specs(1, pltpu.SMEM) + specs(2 * parts),
        out_specs=specs(2 + len(biases)),
        out_shape=[shape((rows, 3 * width), F32), shape((rows, width), F32)]
        + [shape((1, count), F32) for count in biases],
        scratch_shapes=[pltpu.VMEM((rows, EXTRA), F32)],
        name="place_attn",
        **params(0, rows * width * 24),
    )(spot, *first[0], *second[0])


def cond_kernel(shards, spot_ref, grad_ref, cond_ref, out_ref):
    slots, width = cond_ref.shape
    depth = width // shards
    group = shards * slots
    for place in range(shards):
        total = jnp.zeros((slots, depth), F32)
        for offset in range(shards):
            first = offset * group + offset * slots
            part = grad_ref[first : first + slots, :]
            total = total + jnp.where((spot_ref[0] ^ offset) == place, part, 0.0)
        cond = cond_ref[:, place * depth : (place + 1) * depth].astype(F32)
        logistic = 1.0 / (1.0 + jnp.exp(-cond))
        out_ref[:, place * depth : (place + 1) * depth] = (
            total * logistic * (1.0 + cond * (1.0 - logistic))
        )


def cond_call(spot, grads, condition, shards):
    return pl.pallas_call(
        functools.partial(cond_kernel, shards),
        in_specs=specs(1, pltpu.SMEM) + specs(2),
        out_specs=pl.BlockSpec(memory_space=pltpu.VMEM),
        out_shape=shape(condition.shape, F32),
        name="grad_condition",
        **params(),
    )(spot, grads, condition)


def after(value, *others):
    return lax.optimization_barrier((value,) + others)[0]


class Axis:
    def __init__(self, name, size, number):
        self.name = name
        self.size = size
        self.number = number
        self.index = lax.axis_index(name)
        self.bits = [1 << k for k in range(size.bit_length() - 1)]

    def swap(self, value, bit):
        return lax.ppermute(value, self.name, [(i, i ^ bit) for i in range(self.size)])

    def high(self, bit):
        return (self.index & bit) != 0


def ordered(high, mine, other, axis=0):
    return jnp.where(
        high, jnp.concatenate([other, mine], axis), jnp.concatenate([mine, other], axis)
    )


def gather_ordered(value, axis):
    value = value[None]
    for bit in axis.bits:
        value = ordered(axis.high(bit), value, axis.swap(value, bit))
    return value


class Gather:
    def __init__(self, piece, shard):
        self.shard = shard
        self.own = piece
        self.swapped = [(shard.swap(piece, 1), 1)]

    def near(self, *gate):
        self.held = [(self.own, 0)]
        for bit in reversed(self.shard.bits[1:]):
            for value, offset in list(self.held):
                self.held.append((self.shard.swap(after(value, *gate), bit), offset ^ bit))
        return self.held[-1][0]

    def pieces(self, *gate):
        for value, offset in self.held[1:]:
            self.swapped.append((self.shard.swap(after(value, *gate), 1), offset ^ 1))
        held = self.held + self.swapped
        return [value for value, _ in held], tuple(offset for _, offset in held)


def plan(order, rows):
    stages = []
    back = []
    for at, (axis, bit) in enumerate(order):
        if axis.name == "shard":
            stages.append((axis, bit, 0))
        elif rows // 2 % 16 == 0 and at < len(order) - 1:
            rows //= 2
            stages.append((axis, bit, 1))
            back.insert(0, (axis, bit, rows))
        else:
            stages.append((axis, bit, None))
    return stages, back


class Reduction:
    def __init__(self, keep, operand, sent, stages, back):
        self.keep = keep
        self.operand = (operand,)
        self.sent = (sent,)
        self.stages, self.back = stages, back
        self.at = 0
        self.steps = len(stages) + len(back)

    def running(self):
        return self.at < self.steps

    def jobs(self):
        if self.at < len(self.stages):
            dim = self.stages[self.at][2]
            if dim is not None:
                return [dict(kind="halve", args=[self.keep, self.sent[0]], step=self.stages[self.at])]
        if self.at <= len(self.stages):
            return [dict(kind="add", args=[self.keep, self.sent[0]])]
        return [dict(kind="cat", args=[self.whole, self.sent[0]])]

    def commit(self, results):
        if self.at < len(self.stages):
            axis, bit, _ = self.stages[self.at]
            self.keep, operand = results[0][0], results[0][-1]
        else:
            axis, bit, _ = self.back[self.at - len(self.stages)]
            operand = self.whole = results[0][0]
        self.operand = (operand,)
        self.sent = (axis.swap(operand, bit),)
        self.at += 1

    def finish(self):
        terms = [(axis.number, bit, size) for axis, bit, size in self.back]
        flips = [(False,) * len(terms)]
        for k in range(len(terms)):
            flips += [flip[:k] + (True,) + flip[k + 1 :] for flip in flips]
        if self.back:
            pieces = [self.whole, self.sent[0]]
        else:
            total = self.keep.astype(F32) + self.sent[0].astype(F32)
            pieces = [total.astype(BF16)]
        count = sum(piece.shape[1] for piece in pieces) // len(flips)
        return pieces, terms, flips, count


def one_way(pair, shard, order):
    keep, send = pair
    return Reduction(keep, send, shard.swap(send, 1), *plan(order, keep.shape[1]))


class TwoWay:
    def __init__(self, pair, shard, rep):
        self.keeps, send = pair[0], pair[1]
        self.operand = (send,)
        self.sent = (shard.swap(send, 1),)
        inner = [(shard, bit, 0) for bit in reversed(shard.bits[1:])]
        near = (rep, 1, 1)
        self.orders = (inner + [near], [near] + inner)
        rows = self.keeps.shape[1] // 2
        self.stages, self.back = plan([(rep, bit) for bit in rep.bits[1:]], rows)
        self.back = self.back + [(rep, 1, rows)]
        self.round = 0
        self.inner = None

    def running(self):
        return self.inner is None or self.inner.running()

    def jobs(self):
        if self.inner is not None:
            self.inner.sent = self.sent
            return self.inner.jobs()
        if self.round == len(self.orders[0]):
            args = [self.keeps[0], self.sent[0], self.keeps[1], self.sent[1]]
            return [dict(kind="merge", args=args, step=self.stages[0])]
        jobs = []
        for part, order in enumerate(self.orders):
            if self.round == 0:
                jobs.append(dict(args=[self.keeps, self.sent[0]], part=part))
            else:
                jobs.append(dict(args=[self.keeps[part], self.sent[part]]))
            jobs[part].update(kind="halve", step=order[self.round])
        return jobs

    def commit(self, results):
        if self.inner is None and self.round < len(self.orders[0]):
            self.keeps = [keep for keep, _ in results]
            self.operand = tuple(operand for _, operand in results)
            steps = [order[self.round] for order in self.orders]
            self.sent = tuple(
                axis.swap(operand, bit) for (axis, bit, _), operand in zip(steps, self.operand)
            )
            self.round += 1
            return
        if self.inner is None:
            self.inner = Reduction(None, None, None, self.stages, self.back)
        self.inner.commit(results)
        self.operand, self.sent = self.inner.operand, self.inner.sent

    def finish(self):
        self.inner.sent = self.sent
        return self.inner.finish()


def two_way(pair, shard, rep):
    rows = pair[0].shape[1]
    if len(rep.bits) > 1 and rows // 4 % 16 == 0 and shard.size > 2:
        return TwoWay(pair, shard, rep)
    order = [(shard, bit) for bit in reversed(shard.bits[1:])] + [(rep, bit) for bit in rep.bits]
    return one_way(pair, shard, order)


class Chain:
    def __init__(self, value, steps):
        self.value = value
        self.todo = list(steps)
        self.send_next()

    def running(self):
        return self.join is not None

    def send_next(self):
        self.operand = (self.value,)
        axis, bit, self.join = self.todo.pop(0)
        self.sent = (axis.swap(self.value, bit),)

    def jobs(self):
        return []

    def commit(self, results):
        self.value = self.join(self.value, self.sent[0])
        self.join = None
        if self.todo:
            self.send_next()


def together(spot, chains, *values):
    got = lax.optimization_barrier((tuple(chain.sent for chain in chains), values))
    jobs = []
    shares = []
    for chain, sent in zip(chains, got[0]):
        chain.sent = sent
        shares.append(chain.jobs() if chain.running() else [])
        jobs += shares[-1]
    results = round_call(spot, jobs) if jobs else []
    for chain, share in zip(chains, shares):
        if chain.running():
            chain.commit(results[: len(share)])
            results = results[len(share) :]
    return got[1][0] if len(values) == 1 else got[1]


def launched(value, *chains):
    return after(value, *[operand for chain in chains for operand in chain.operand])


def per_device(
    shard_size,
    rep_size,
    tokens,
    condition,
    counts,
    cotangent,
    ada_weight,
    ada_bias,
    qkv_weight,
    qv_bias,
    proj_weight,
    proj_bias,
    fc1_weight,
    fc1_bias,
    fc2_weight,
    fc2_bias,
):
    shard = Axis("shard", shard_size, 0)
    rep = Axis("rep", rep_size, 1)
    spot = jnp.stack([shard.index, rep.index]).astype(jnp.int32)
    slots, width = condition.shape
    seq = tokens.shape[0] // slots
    rows = slots * seq
    depth = ada_weight.shape[0]

    qkv_gather = Gather(qkv_weight, shard)
    proj_gather = Gather(proj_weight, shard)
    fc1_gather = Gather(fc1_weight, shard)
    fc2_gather = Gather(fc2_weight, shard)

    slots_here = condition
    for bit in shard.bits:
        slots_here = jnp.concatenate([slots_here, shard.swap(slots_here, bit)], 0)
    near = proj_gather.near(qkv_gather.near())
    silu_group = jax.nn.silu(slots_here.astype(F32)).astype(BF16)
    my_cols = lax.dynamic_slice_in_dim(silu_group, shard.index * depth, depth, 1)
    own_bias = lax.dynamic_update_slice(
        jnp.zeros((6 * width,), F32), ada_bias.astype(F32), (shard.index * ada_bias.shape[0],)
    )
    modulation = dot_nn(my_cols, ada_weight) + own_bias[None]
    for bit in reversed(shard.bits):
        half = modulation.shape[0] // 2
        modulation = modulation[:half] + shard.swap(modulation[half:], bit)

    bias_list = (qv_bias, proj_bias, fc1_bias, fc2_bias)
    packed = jnp.concatenate([after(qv_bias, slots_here), *bias_list[1:]])
    packed = jnp.pad(packed, (0, -packed.shape[0] % 128)).reshape(-1, 128)
    group = gather_ordered(packed, shard).reshape(shard.size, -1)
    wide = []
    start = 0
    for bias in bias_list:
        wide.append(group[:, start : start + bias.shape[0]].reshape(1, -1).astype(F32))
        start += bias.shape[0]
    qv_b, proj_b, fc1_b, fc2_b = wide

    live_rows = lax.broadcasted_iota(jnp.int32, (rows, 1), 0) < counts[0] * seq
    cot = jnp.where(live_rows, cotangent, jnp.zeros_like(cotangent))

    near_one = fc1_gather.near(near)
    qkv_w = qkv_gather.pieces()
    proj_w = proj_gather.pieces()
    qkv_b = jnp.concatenate([qv_b[:, :width], jnp.zeros((1, width), F32), qv_b[:, width:]], axis=1)
    hidden_one, qkv = qkv_call(spot, tokens, after(modulation, near), qkv_b, qkv_w, slots)
    mixed, branch_one, hidden_two, low_two = attn_call(spot,
        qkv, tokens, cot, modulation, proj_b, proj_w, slots
    )
    fc2_gather.near(near_one, hidden_two)
    fc1_w = fc1_gather.pieces()
    act_low, derivative = gelu_call(spot, hidden_two, fc1_b, fc1_w)

    shard_steps = [(shard, bit) for bit in reversed(shard.bits[1:])]
    low_bits = [(rep, bit) for bit in rep.bits[:1]]
    high_bits = [(rep, bit) for bit in rep.bits[1:]]
    keep, send = wide_grad(spot, act_low, low_two, shard.size, "fc2_grad")
    fc2_w = fc2_gather.pieces(send)
    fc2_sum = two_way((keep, after(send, fc2_gather.held[-1][0])), shard, rep)
    block_out, gate_sums = out_call(spot,
        counts, launched(act_low, fc2_sum), tokens, branch_one, cot, modulation, fc2_b, fc2_w, slots
    )
    block_out, gate_sums = together(spot, [fc2_sum], block_out, gate_sums)
    low_pre, grad_fc1_b, grad_mid, low_one, sums = mlp_bwd_call(spot,
        launched(low_two, fc2_sum), derivative, tokens, branch_one, cot, modulation, fc1_w, fc2_w, slots
    )
    low_pre = together(spot, [fc2_sum], low_pre)
    keep, send = wide_grad(spot, hidden_two, launched(low_pre, fc2_sum), shard.size, "fc1_grad")
    keep, send, low_one = together(spot, [fc2_sum], keep, send, low_one)
    fc1_sum = two_way((keep, send), shard, rep)
    grad_mixed = mixed_bwd_call(spot, launched(low_one, fc1_sum, fc2_sum), proj_w)
    grad_mixed = together(spot, [fc1_sum, fc2_sum], grad_mixed)
    grad_qkv, qv_sums = attn_bwd_call(qkv, launched(grad_mixed, fc1_sum, fc2_sum), slots)
    grad_qkv, qv_sums = together(spot, [fc1_sum, fc2_sum], grad_qkv, qv_sums)
    first, second = attn_grad(
        spot,
        hidden_one,
        launched(grad_qkv, fc1_sum, fc2_sum),
        mixed,
        low_one,
        qv_sums,
        sums,
        grad_fc1_b,
        shard.size,
    )
    first, second, grad_qkv = together(spot, [fc1_sum, fc2_sum], first, second, grad_qkv)
    first_sum = one_way(first, shard, shard_steps + high_bits[:-1] + low_bits + high_bits[-1:])
    second_sum = one_way(second, shard, low_bits + shard_steps + high_bits)
    grad_tokens, slot_values = input_bwd_call(spot,
        launched(grad_qkv, first_sum, second_sum, fc1_sum, fc2_sum),
        tokens,
        grad_mid,
        modulation,
        sums,
        gate_sums,
        condition,
        qkv_w,
        slots,
    )
    sums_list = [first_sum, second_sum, fc1_sum, fc2_sum]
    grad_tokens, slot_values = together(spot, sums_list, grad_tokens, slot_values)

    def append(mine, other):
        return jnp.concatenate([mine, other], 0)

    every = [(rep, bit, append) for bit in reversed(rep.bits)]
    every += [(shard, bit, append) for bit in reversed(shard.bits)]
    all_slots = Chain(slot_values, every)

    def to_silu(mine, other):
        return dot_nt(append(mine, other), ada_weight)

    there = [(shard, bit, append) for bit in shard.bits[:-1]]
    there += [(shard, shard.bits[-1], to_silu)]
    there += [(shard, bit, append) for bit in shard.bits]
    to_cond = Chain(slot_values[:, : 6 * width], there)

    chains = [first_sum, second_sum, fc1_sum, fc2_sum, all_slots, to_cond]
    active = [chain for chain in chains if chain.running()]
    while active:
        together(spot, active)
        active = [chain for chain in chains if chain.running()]

    grad_cond = cond_call(spot, to_cond.value, condition, shard.size)

    mod_all = all_slots.value[:, : 6 * width]
    silu_cols = lax.dynamic_slice_in_dim(all_slots.value, 6 * width + shard.index * depth, depth, 1)
    grad_ada_w = dot_tn(silu_cols, mod_all)
    ada_b_all = jnp.sum(mod_all.astype(F32), axis=0)
    grad_ada_b = lax.dynamic_slice_in_dim(
        ada_b_all, shard.index * ada_bias.shape[0], ada_bias.shape[0], 0
    )

    grad_fc2_w = place_rows(spot, fc2_sum.finish(), fc2_weight.shape[0])
    grad_fc1_w = place_rows(spot, fc1_sum.finish(), fc1_weight.shape[0])
    bias_sizes = tuple(bias.shape[0] for bias in bias_list)
    grad_qkv_w, grad_proj_w, *bias_out = place_attn(
        spot, first_sum.finish(), second_sum.finish(), depth, width, bias_sizes
    )
    bias_out = [value.reshape(-1) for value in bias_out]

    return (
        block_out,
        grad_tokens,
        grad_cond,
        grad_ada_w,
        grad_ada_b,
        grad_qkv_w,
        bias_out[0],
        grad_proj_w,
        bias_out[1],
        grad_fc1_w,
        bias_out[2],
        grad_fc2_w,
        bias_out[3],
    )


def solution(mesh):
    rows = P(("rep", "shard"), None)
    weights = (P("shard", None), P("shard"))
    return jax.shard_map(
        functools.partial(per_device, mesh.shape["shard"], mesh.shape["rep"]),
        mesh=mesh,
        in_specs=(rows, rows, P(("rep", "shard")), rows) + weights * 5,
        out_specs=(rows, rows, rows) + weights * 5,
        check_vma=False,
    )
```

time: 459 us -> 346 us (0.75); the launches traced: 452 us -> 345 us
  Pallas kernels: 22.6 us -> 163 us
  waiting for transfers between devices: 184 us -> 85.3 us
  matrix products: 62.1 us -> 4.18 us
  local copies, waits for them, and re-layouts: 80.2 us -> 26.7 us
  other arithmetic: 37.6 us -> 12.2 us
  starting transfers between devices: 62.7 us -> 51.1 us
    pallas_call x2 -> x27, Pallas kernels: 22.6 us -> 163 us  [the longest x12 47.1 us: round_call(): pl.pallas_call(functools.partial(round_kernel, kinds), grid_spec=pltpu.Pr...]
    ppermute x71 -> x59, waiting for transfers between devices: 184 us -> 85.3 us  [swap(): lax.ppermute(value, self.name, [(i, i ^ bit) for i in range(self.size)])]
    dot_general x5 -> x1, matrix products: 26.6 us -> 1.13 us  [dot_nn(): lax.dot_general(left, right, (((1,), (0,)), ((), ())), preferred_element_...]
    dot_general x5 -> x1, matrix products: 23.5 us -> 0.54 us  [dot_nt(): lax.dot_general(left, right, (((1,), (1,)), ((), ())), preferred_element_...]
    dynamic_update_slice x12 -> x0, local copies, waits for them, and re-layouts: 18.6 us -> none  [gather_weight(): lax.dynamic_update_slice(whole, held, ((shard.index ^ offset) * rows, 0))]
    add x24 -> x2, other arithmetic: 13.7 us -> 0.95 us  [per_device(): modulation = modulation[:half] + shard.swap(modulation[half:], bit)]
    dot_general x4 -> x0, local copies, waits for them, and re-layouts: 11.9 us -> none  [dot_tn(): lax.dot_general(left, right, (((0,), (0,)), ((), ())), preferred_element_...]
    ppermute x71 -> x59, starting transfers between devices: 62.7 us -> 51.1 us  [swap(): lax.ppermute(value, self.name, [(i, i ^ bit) for i in range(self.size)])]
  transfers between devices with their start and end apart: 71 -> 59, of which waited for: 36 -> 22; matrix products, arithmetic and copies ran while one was open for 26% -> 7% of each run, Pallas kernels for 1% -> 39%
where the time goes in v2:
time: 346 us; the launch traced here: 345 us
  Pallas kernels  163 us (47%)
  waiting for transfers between devices  85.3 us (25%)
  starting transfers between devices  51.1 us (15%)
  local copies, waits for them, and re-layouts  26.7 us (8%)
  other arithmetic  12.2 us (4%)
  matrix products  4.18 us (1%)
    ppermute x59, waiting for transfers between devices, swap(): lax.ppermute(value, self.name, [(i, i ^ bit) for i in range(self.size)])  85.3 us
    ppermute x59, starting transfers between devices, swap(): lax.ppermute(value, self.name, [(i, i ^ bit) for i in range(self.size)])  51.1 us
    pallas_call x12, Pallas kernels, round_call(): pl.pallas_call(functools.partial(round_kernel, kinds), grid_spec=pltpu.Pr...  47.1 us
    pallas_call x1, Pallas kernels, mlp_bwd_call(): pl.pallas_call(functools.partial(mlp_bwd_kernel, one[1], slots), grid=(hi...  18.5 us
    pallas_call x1, Pallas kernels, attn_bwd_call(): pl.pallas_call(attn_bwd_kernel, grid=(slots,), in_specs=[pl.BlockSpec((se...  15.9 us
    pallas_call x2, Pallas kernels, wide_grad(): pl.pallas_call(wide_grad_kernel, grid=(shards // 2 // per_step, out_dim /...  15.8 us
    unnamed x94, local copies, waits for them, and re-layouts  15.2 us
    pallas_call x1, Pallas kernels, gelu_call(): pl.pallas_call(functools.partial(gelu_kernel, offsets), grid=(hidden_unit...  11.2 us
  transfers between devices with their start and end apart: 59, of which 22 were waited for; matrix products, arithmetic and copies ran while one was open for 7% of the time, Pallas kernels for 39%

profile of v2, /device:TPU:0, one launch (start us, length us, event | category | flops | bytes accessed | tf_op | source)
XLA Modules:
  0.0 344.7 jit_solution(15353633600088126465)
XLA Ops:
  17.3 10.7 %collective-permute-done.7 = bf16[2,12,128]{2,1,0:T(8,128)(2,1)S(1)} collective-permute-done((bf16[2,12,128]{2,1,0:T(8,128)(2,1)S(1)}, bf16[2,12,128]{2,1,0:T(8,128)(2,1)S(1)}, u32[]{:S(2)}, u32[]{:S(2)}) %collective-permute-start.7) | collective-permute-done | bytes 6176 | tf_op jit(solution)/shard_map/ppermute | solution.py:847
  35.4 5.2 %collective-permute-done.5.refs_7_.refs_3_ = bf16[192,768]{1,0:T(8,128)(2,1)S(1)} collective-permute-done((bf16[192,768]{1,0:T(8,128)(2,1)S(1)}, bf16[192,768]{1,0:T(8,128)(2,1)S(1)}, u32[]{:S(2)}, u32[]{:S(2)}) %collective-permute-start.5) | collective-permute-done | bytes 294944 | tf_op jit(solution)/shard_map/ppermute | solution.py:847
  48.5 6.6 %qkv_fwd.1 = (bf16[512,768]{1,0:T(8,128)(2,1)}, bf16[512,2304]{1,0:T(8,128)(2,1)}) custom-call(s32[2]{0:T(128)} %pad_add_fusion.refs_0_.spot_ref, bf16[512,768]{1,0:T(8,128)(2,1)} %refs_2_.5, f32[2,4608]{1,0:T(2,128)} %copy-done.17, f32[1,2304]{1,0:T(1,128)} %fusion.9.refs_3_, bf16[192,2304]{1,0:T(8,128)(2,1)} %refs_8_.3, bf16[192,2304]{1,0:T(8,128)(2,1)} %copy-done.8, ...), custom_call_target="tpu_custom_call" | custom-call | tf_op jit(solution)/shard_map/qkv_fwd/pallas_call | solution.py:121
  55.8 10.2 %attn_fwd.1 = (bf16[512,768]{1,0:T(8,128)(2,1)}, f32[512,768]{1,0:T(8,128)}, bf16[512,768]{1,0:T(8,128)(2,1)}, bf16[512,768]{1,0:T(8,128)(2,1)}) custom-call(s32[2]{0:T(128)} %pad_add_fusion.refs_0_.spot_ref, bf16[512,2304]{1,0:T(8,128)(2,1)} %get-tuple-element.161.refs_1_.qkv_ref, bf16[512,768]{1,0:T(8,128)(2,1)} %refs_2_.5, ...), custom_call_target="tpu_custom_call" | custom-call | tf_op jit(solution)/shard_map/attn_fwd/pallas_call | solution.py:193
  72.1 11.2 %fc1_gelu.1 = (bf16[512,3072]{1,0:T(8,128)(2,1)}, f32[512,3072]{1,0:T(8,128)}) custom-call(s32[2]{0:T(128)} %pad_add_fusion.refs_0_.spot_ref, bf16[512,768]{1,0:T(8,128)(2,1)} %get-tuple-element.162.refs_1_.left_ref, f32[1,3072]{1,0:T(1,128)} %bitcast.26, bf16[192,3072]{1,0:T(8,128)(2,1)} %refs_7_.2, ...), custom_call_target="tpu_custom_call" | custom-call | tf_op jit(solution)/shard_map/fc1_gelu/pallas_call | solution.py:255
  83.3 8.1 %fc2_grad.1 = (f32[2,768,768]{2,1,0:T(8,128)}, bf16[2,768,768]{2,1,0:T(8,128)(2,1)}) custom-call(s32[2]{0:T(128)} %pad_add_fusion.refs_0_.spot_ref, bf16[512,3072]{1,0:T(8,128)(2,1)} %get-tuple-element.169.left_ref.refs_2_, bf16[512,768]{1,0:T(8,128)(2,1)} %get-tuple-element.180.right_ref.refs_1_), custom_call_target="tpu_custom_call" | custom-call | tf_op jit(solution)/shard_map/fc2_grad/pallas_call | solution.py:575
  91.4 5.1 %collective-permute-done.15.refs_9_.refs_12_ = bf16[768,768]{1,0:T(8,128)(2,1)} collective-permute-done((bf16[768,768]{1,0:T(8,128)(2,1)S(1)}, bf16[768,768]{1,0:T(8,128)(2,1)}, u32[]{:S(2)}, u32[]{:S(2)}) %collective-permute-start.15) | collective-permute-done | bytes 1179680 | tf_op jit(solution)/shard_map/ppermute | solution.py:847
  97.7 6.5 %collective-permute-done.17.refs_10_.refs_13_ = bf16[768,768]{1,0:T(8,128)(2,1)} collective-permute-done((bf16[768,768]{1,0:T(8,128)(2,1)S(1)}, bf16[768,768]{1,0:T(8,128)(2,1)}, u32[]{:S(2)}, u32[]{:S(2)}) %collective-permute-start.17) | collective-permute-done | bytes 1179680 | tf_op jit(solution)/shard_map/ppermute | solution.py:847
  104.7 8.9 %fc2_fwd.1 = (bf16[512,768]{1,0:T(8,128)(2,1)}, f32[2,768]{1,0:T(2,128)}) custom-call(s32[2]{0:T(128)} %pad_add_fusion.refs_0_.spot_ref, s32[1]{0:T(128)S(6)} %copy.38.refs_1_, bf16[512,3072]{1,0:T(8,128)(2,1)} %get-tuple-element.169.left_ref.refs_2_, bf16[512,768]{1,0:T(8,128)(2,1)} %refs_2_.5, f32[512,768]{1,0:T(8,128)} %get-tuple-element.170.refs_4_, ...), custom_call_target="tpu_custom_call" | custom-call | tf_op jit(solution)/shard_map/fc2_fwd/pallas_call | solution.py:304
  113.6 5.6 %sum_round.12 = (f32[1,768,384]{2,1,0:T(8,128)}, bf16[1,768,384]{2,1,0:T(8,128)(2,1)}, f32[2,384,384]{2,1,0:T(8,128)}, bf16[2,384,384]{2,1,0:T(8,128)(2,1)}) custom-call(s32[2]{0:T(128)} %pad_add_fusion.refs_0_.spot_ref, f32[2,768,768]{2,1,0:T(8,128)} %get-tuple-element.175.refs_0_.refs_1_.refs_4_.refs_5_, ...), custom_call_target="tpu_custom_call" | custom-call | tf_op jit(solution)/shard_map/sum_round/pallas_call | solution.py:720
  121.9 18.5 %mlp_bwd.1 = (bf16[512,3072]{1,0:T(8,128)(2,1)}, f32[1,3072]{1,0:T(1,128)}, f32[512,768]{1,0:T(8,128)}, bf16[512,768]{1,0:T(8,128)(2,1)}, f32[5,2,768]{2,1,0:T(2,128)}) custom-call(s32[2]{0:T(128)} %pad_add_fusion.refs_0_.spot_ref, bf16[512,768]{1,0:T(8,128)(2,1)} %get-tuple-element.180.right_ref.refs_1_, f32[512,3072]{1,0:T(8,128)} %get-tuple-element.181.refs_2_, ...), custom_call_target="tpu_custom_call" | custom-call | tf_op jit(solution)/shard_map/mlp_bwd/pallas_call | solution.py:383
  146.7 7.8 %fc1_grad.1 = (f32[2,192,3072]{2,1,0:T(8,128)}, bf16[2,192,3072]{2,1,0:T(8,128)(2,1)}) custom-call(s32[2]{0:T(128)} %pad_add_fusion.refs_0_.spot_ref, bf16[512,768]{1,0:T(8,128)(2,1)} %get-tuple-element.162.refs_1_.left_ref, bf16[512,3072]{1,0:T(8,128)(2,1)} %get-tuple-element.189.right_ref), custom_call_target="tpu_custom_call" | custom-call | tf_op jit(solution)/shard_map/fc1_grad/pallas_call | solution.py:575
  160.4 4.1 %proj_bwd.1.grad_ref = bf16[512,768]{1,0:T(8,128)(2,1)} custom-call(s32[2]{0:T(128)} %pad_add_fusion.refs_0_.spot_ref, bf16[512,768]{1,0:T(8,128)(2,1)} %get-tuple-element.201.refs_1_.refs_4_, bf16[192,768]{1,0:T(8,128)(2,1)} %refs_2_.4, bf16[192,768]{1,0:T(8,128)(2,1)} %copy-done.19, bf16[192,768]{1,0:T(8,128)(2,1)} %collective-permute-done.10.refs_8_.refs_4_, ...), custom_call_target="tpu_custom_call" | custom-call | tf_op jit(solution)/shard_map/proj_bwd/pallas_call | solution.py:491
  169.1 5.6 %sum_round.15 = (f32[1,192,1536]{2,1,0:T(8,128)}, bf16[1,192,1536]{2,1,0:T(8,128)(2,1)}, f32[2,96,1536]{2,1,0:T(8,128)}, bf16[2,96,1536]{2,1,0:T(8,128)(2,1)}, bf16[1,192,768]{2,1,0:T(8,128)(2,1)}) custom-call(s32[2]{0:T(128)} %pad_add_fusion.refs_0_.spot_ref, f32[2,192,3072]{2,1,0:T(8,128)} %get-tuple-element.193.refs_0_.refs_1_.refs_4_.refs_5_, ...), custom_call_target="tpu_custom_call" | custom-call | tf_op jit(solution)/shard_map/sum_round/pallas_call | solution.py:720
  179.7 15.9 %attn_bwd.1 = (bf16[512,2304]{1,0:T(8,128)(2,1)}, f32[2,1,1536]{2,1,0:T(1,128)}) custom-call(bf16[512,2304]{1,0:T(8,128)(2,1)} %get-tuple-element.161.refs_1_.qkv_ref, bf16[512,768]{1,0:T(8,128)(2,1)} %proj_bwd.1.grad_ref), custom_call_target="tpu_custom_call" | custom-call | tf_op jit(solution)/shard_map/attn_bwd/pallas_call | solution.py:455
  204.2 7.0 %attn_weight_grads.1 = (f32[2,192,1536]{2,1,0:T(8,128)}, bf16[2,192,1536]{2,1,0:T(8,128)(2,1)}, f32[2,192,1792]{2,1,0:T(8,128)}, bf16[2,192,1792]{2,1,0:T(8,128)(2,1)}) custom-call(s32[2]{0:T(128)} %pad_add_fusion.refs_0_.spot_ref, bf16[512,768]{1,0:T(8,128)(2,1)} %get-tuple-element.220.refs_1_, bf16[512,2304]{1,0:T(8,128)(2,1)} %get-tuple-element.241.refs_2_.refs_1_, ...), custom_call_target="tpu_custom_call" | custom-call | tf_op jit(solution)/shard_map/attn_weight_grads/pallas_call | solution.py:630
  217.6 8.0 %qkv_bwd.1 = (f32[512,768]{1,0:T(8,128)}, bf16[2,5376]{1,0:T(2,128)(2,1)}) custom-call(s32[2]{0:T(128)} %pad_add_fusion.refs_0_.spot_ref, bf16[512,2304]{1,0:T(8,128)(2,1)} %get-tuple-element.241.refs_2_.refs_1_, bf16[512,768]{1,0:T(8,128)(2,1)} %refs_2_.5, f32[512,768]{1,0:T(8,128)} %get-tuple-element.242.refs_3_, f32[2,4608]{1,0:T(2,128)} %copy-done.17, ...), custom_call_target="tpu_custom_call" | custom-call | tf_op jit(solution)/shard_map/qkv_bwd/pallas_call | solution.py:540
  225.8 5.1 %collective-permute-done.34.refs_1_ = bf16[1,384,768]{2,1,0:T(8,128)(2,1)S(1)} collective-permute-done((bf16[1,384,768]{2,1,0:T(8,128)(2,1)}, bf16[1,384,768]{2,1,0:T(8,128)(2,1)S(1)}, u32[]{:S(2)}, u32[]{:S(2)}) %collective-permute-start.34) | collective-permute-done | bytes 589856 | tf_op jit(solution)/shard_map/ppermute | solution.py:847
  232.4 6.2 %sum_round.18 = (f32[1,192,1536]{2,1,0:T(8,128)}, bf16[1,192,1536]{2,1,0:T(8,128)(2,1)}, f32[2,96,1792]{2,1,0:T(8,128)}, bf16[2,96,1792]{2,1,0:T(8,128)(2,1)}, bf16[1,48,3072]{2,1,0:T(8,128)(2,1)}) custom-call(s32[2]{0:T(128)} %pad_add_fusion.refs_0_.spot_ref, f32[2,192,1536]{2,1,0:T(8,128)} %get-tuple-element.248.refs_0_.refs_1_, ...), custom_call_target="tpu_custom_call" | custom-call | tf_op jit(solution)/shard_map/sum_round/pallas_call | solution.py:720
  245.1 11.3 %collective-permute-done.38 = bf16[2,5376]{1,0:T(2,128)(2,1)S(1)} collective-permute-done((bf16[2,5376]{1,0:T(2,128)(2,1)S(1)}, bf16[2,5376]{1,0:T(2,128)(2,1)S(1)}, u32[]{:S(2)}, u32[]{:S(2)}) %collective-permute-start.38) | collective-permute-done | bytes 21536 | tf_op jit(solution)/shard_map/ppermute | solution.py:847
  257.5 4.1 %sum_round.19 = (f32[1,96,1536]{2,1,0:T(8,128)}, bf16[1,96,1536]{2,1,0:T(8,128)(2,1)}, f32[1,96,1792]{2,1,0:T(8,128)}, bf16[1,96,1792]{2,1,0:T(8,128)(2,1)}, bf16[1,48,3072]{2,1,0:T(8,128)(2,1)}) custom-call(s32[2]{0:T(128)} %pad_add_fusion.refs_0_.spot_ref, f32[1,192,1536]{2,1,0:T(8,128)} %get-tuple-element.258.refs_0_.refs_1_, ...), custom_call_target="tpu_custom_call" | custom-call | tf_op jit(solution)/shard_map/sum_round/pallas_call | solution.py:720
  265.8 8.3 %collective-permute-done.44 = bf16[4,4608]{1,0:T(4,128)(2,1)S(1)} collective-permute-done((bf16[4,4608]{1,0:T(4,128)(2,1)S(1)}, bf16[4,4608]{1,0:T(4,128)(2,1)S(1)}, u32[]{:S(2)}, u32[]{:S(2)}) %collective-permute-start.44) | collective-permute-done | bytes 36896 | tf_op jit(solution)/shard_map/ppermute | solution.py:847
  299.3 8.2 %collective-permute-done.49.refs_1_ = bf16[1,48,1536]{2,1,0:T(8,128)(2,1)S(1)} collective-permute-done((bf16[1,48,1536]{2,1,0:T(8,128)(2,1)}, bf16[1,48,1536]{2,1,0:T(8,128)(2,1)S(1)}, u32[]{:S(2)}, u32[]{:S(2)}) %collective-permute-start.49) | collective-permute-done | bytes 147488 | tf_op jit(solution)/shard_map/ppermute | solution.py:847
  333.4 4.6 %collective-permute-done.56.refs_1_ = bf16[1,96,1536]{2,1,0:T(8,128)(2,1)S(1)} collective-permute-done((bf16[1,96,1536]{2,1,0:T(8,128)(2,1)}, bf16[1,96,1536]{2,1,0:T(8,128)(2,1)S(1)}, u32[]{:S(2)}, u32[]{:S(2)}) %collective-permute-start.56) | collective-permute-done | bytes 294944 | tf_op jit(solution)/shard_map/ppermute | solution.py:847
  (257 shorter events, 150.0 us)
Async XLA Ops:
  4.1 50.9 %collective-permute-start.10 = (bf16[192,768]{1,0:T(8,128)(2,1)}, bf16[192,768]{1,0:T(8,128)(2,1)}, u32[]{:S(2)}, u32[]{:S(2)}) collective-permute-start(bf16[192,768]{1,0:T(8,128)(2,1)} %refs_2_.4), channel_id=1, source_target_pairs={{0,1},{1,0},{2,3},{3,2},{4,5},{5,4},{6,7},{7,6},{8,9},{9,8},{10,11... | collective-permute-start | bytes 884744 | tf_op jit(solution)/shard_map/ppermute | solution.py:847
  4.5 42.0 %collective-permute-start.8 = (bf16[192,2304]{1,0:T(8,128)(2,1)}, bf16[192,2304]{1,0:T(8,128)(2,1)S(1)}, u32[]{:S(2)}, u32[]{:S(2)}) collective-permute-start(bf16[192,2304]{1,0:T(8,128)(2,1)} %refs_8_.3), channel_id=1, source_target_pairs={{0,1},{1,0},{2,3},{3,2},{4,5},{5,4},{6,7},{7,6},{8,9},{9,8},{10,11... | collective-permute-start | bytes 2654216 | tf_op jit(solution)/shard_map/ppermute | solution.py:847
  4.7 27.7 %collective-permute-start.4 = (bf16[192,2304]{1,0:T(8,128)(2,1)}, bf16[192,2304]{1,0:T(8,128)(2,1)S(1)}, u32[]{:S(2)}, u32[]{:S(2)}) collective-permute-start(bf16[192,2304]{1,0:T(8,128)(2,1)} %refs_8_.3), channel_id=1, source_target_pairs={{0,2},{1,3},{2,0},{3,1},{4,6},{5,7},{6,4},{7,5},{8,10},{9,11},{10,... | collective-permute-start | bytes 2654216 | tf_op jit(solution)/shard_map/ppermute | solution.py:847
  41.4 26.6 %collective-permute-start.12 = (bf16[192,3072]{1,0:T(8,128)(2,1)}, bf16[192,3072]{1,0:T(8,128)(2,1)}, u32[]{:S(2)}, u32[]{:S(2)}) collective-permute-start(bf16[192,3072]{1,0:T(8,128)(2,1)} %refs_7_.2), channel_id=1, source_target_pairs={{0,2},{1,3},{2,0},{3,1},{4,6},{5,7},{6,4},{7,5},{8,10},{9,11},{10,... | collective-permute-start | bytes 3538952 | tf_op jit(solution)/shard_map/ppermute | solution.py:847
  46.5 23.5 %collective-permute-start.13 = (bf16[192,3072]{1,0:T(8,128)(2,1)}, bf16[192,3072]{1,0:T(8,128)(2,1)S(1)}, u32[]{:S(2)}, u32[]{:S(2)}) collective-permute-start(bf16[192,3072]{1,0:T(8,128)(2,1)} %refs_7_.2), channel_id=1, source_target_pairs={{0,1},{1,0},{2,3},{3,2},{4,5},{5,4},{6,7},{7,6},{8,9},{9,8},{10,11... | collective-permute-start | bytes 3538952 | tf_op jit(solution)/shard_map/ppermute | solution.py:847
  68.0 28.5 %collective-permute-start.15 = (bf16[768,768]{1,0:T(8,128)(2,1)S(1)}, bf16[768,768]{1,0:T(8,128)(2,1)}, u32[]{:S(2)}, u32[]{:S(2)}) collective-permute-start(bf16[768,768]{1,0:T(8,128)(2,1)S(1)} %copy-done.3), channel_id=1, source_target_pairs={{0,2},{1,3},{2,0},{3,1},{4,6},{5,7},{6,4},{7,5},{8,10},{9,11},{10,... | collective-permute-start | bytes 3538952 | tf_op jit(solution)/shard_map/ppermute | solution.py:847
  96.5 17.1 %collective-permute-start.16 = (bf16[2,768,768]{2,1,0:T(8,128)(2,1)}, bf16[2,768,768]{2,1,0:T(8,128)(2,1)}, u32[]{:S(2)}, u32[]{:S(2)}) collective-permute-start(bf16[2,768,768]{2,1,0:T(8,128)(2,1)} %get-tuple-element.168), channel_id=1, source_target_pairs={{0,1},{1,0},{2,3},{3,2},{4,5},{5,4},{6,7},{7,6},{8,9},{9,8},{10,11... | collective-permute-start | bytes 7077896 | tf_op jit(solution)/shard_map/ppermute | solution.py:847
  119.2 21.2 %collective-permute-start.19 = (bf16[1,768,384]{2,1,0:T(8,128)(2,1)}, bf16[1,768,384]{2,1,0:T(8,128)(2,1)S(1)}, u32[]{:S(2)}, u32[]{:S(2)}) collective-permute-start(bf16[1,768,384]{2,1,0:T(8,128)(2,1)} %get-tuple-element.178), channel_id=1, source_target_pairs={{0,2},{1,3},{2,0},{3,1},{4,6},{5,7},{6,4},{7,5},{8,10},{9,11},{10,... | collective-permute-start | bytes 1769480 | tf_op jit(solution)/shard_map/ppermute | solution.py:847
  120.6 19.9 %collective-permute-start.20 = (bf16[2,384,384]{2,1,0:T(8,128)(2,1)}, bf16[2,384,384]{2,1,0:T(8,128)(2,1)S(1)}, u32[]{:S(2)}, u32[]{:S(2)}) collective-permute-start(bf16[2,384,384]{2,1,0:T(8,128)(2,1)} %get-tuple-element.179), channel_id=1, source_target_pairs={{0,4},{4,0},{8,12},{12,8},{16,20},{20,16},{24,28},{28,24},{1,5},{5... | collective-permute-start | bytes 1769480 | tf_op jit(solution)/shard_map/ppermute | solution.py:847
  174.7 21.0 %collective-permute-start.25 = (bf16[1,192,1536]{2,1,0:T(8,128)(2,1)}, bf16[1,192,1536]{2,1,0:T(8,128)(2,1)S(1)}, u32[]{:S(2)}, u32[]{:S(2)}) collective-permute-start(bf16[1,192,1536]{2,1,0:T(8,128)(2,1)} %get-tuple-element.206), channel_id=1, source_target_pairs={{0,2},{1,3},{2,0},{3,1},{4,6},{5,7},{6,4},{7,5},{8,10},{9,11},{10,... | collective-permute-start | bytes 1769480 | tf_op jit(solution)/shard_map/ppermute | solution.py:847
  175.8 19.8 %collective-permute-start.26 = (bf16[2,96,1536]{2,1,0:T(8,128)(2,1)}, bf16[2,96,1536]{2,1,0:T(8,128)(2,1)S(1)}, u32[]{:S(2)}, u32[]{:S(2)}) collective-permute-start(bf16[2,96,1536]{2,1,0:T(8,128)(2,1)} %get-tuple-element.207), channel_id=1, source_target_pairs={{0,4},{4,0},{8,12},{12,8},{16,20},{20,16},{24,28},{28,24},{1,5},{5... | collective-permute-start | bytes 1769480 | tf_op jit(solution)/shard_map/ppermute | solution.py:847
  177.1 18.5 %collective-permute-start.27 = (bf16[1,192,768]{2,1,0:T(8,128)(2,1)}, bf16[1,192,768]{2,1,0:T(8,128)(2,1)S(1)}, u32[]{:S(2)}, u32[]{:S(2)}) collective-permute-start(bf16[1,192,768]{2,1,0:T(8,128)(2,1)} %get-tuple-element.208.refs_8_), channel_id=1, source_target_pairs={{0,16},{4,20},{8,24},{12,28},{16,0},{20,4},{24,8},{28,12},{1,17},{... | collective-permute-start | bytes 884744 | tf_op jit(solution)/shard_map/ppermute | solution.py:847
  211.3 19.6 %collective-permute-start.32 = (bf16[2,192,1792]{2,1,0:T(8,128)(2,1)}, bf16[2,192,1792]{2,1,0:T(8,128)(2,1)S(1)}, u32[]{:S(2)}, u32[]{:S(2)}) collective-permute-start(bf16[2,192,1792]{2,1,0:T(8,128)(2,1)} %get-tuple-element.232), channel_id=1, source_target_pairs={{0,1},{1,0},{2,3},{3,2},{4,5},{5,4},{6,7},{7,6},{8,9},{9,8},{10,11... | collective-permute-start | bytes 4128776 | tf_op jit(solution)/shard_map/ppermute | solution.py:847
  211.4 19.5 %collective-permute-start.31 = (bf16[2,192,1536]{2,1,0:T(8,128)(2,1)}, bf16[2,192,1536]{2,1,0:T(8,128)(2,1)S(1)}, u32[]{:S(2)}, u32[]{:S(2)}) collective-permute-start(bf16[2,192,1536]{2,1,0:T(8,128)(2,1)} %get-tuple-element.231), channel_id=1, source_target_pairs={{0,1},{1,0},{2,3},{3,2},{4,5},{5,4},{6,7},{7,6},{8,9},{9,8},{10,11... | collective-permute-start | bytes 3538952 | tf_op jit(solution)/shard_map/ppermute | solution.py:847
  215.6 15.2 %collective-permute-start.34 = (bf16[1,384,768]{2,1,0:T(8,128)(2,1)}, bf16[1,384,768]{2,1,0:T(8,128)(2,1)S(1)}, u32[]{:S(2)}, u32[]{:S(2)}) collective-permute-start(bf16[1,384,768]{2,1,0:T(8,128)(2,1)} %get-tuple-element.239.refs_0_), channel_id=1, source_target_pairs={{0,4},{4,0},{8,12},{12,8},{16,20},{20,16},{24,28},{28,24},{1,5},{5... | collective-permute-start | bytes 1769480 | tf_op jit(solution)/shard_map/ppermute | solution.py:847
  238.6 17.8 %collective-permute-start.36 = (bf16[2,96,1792]{2,1,0:T(8,128)(2,1)}, bf16[2,96,1792]{2,1,0:T(8,128)(2,1)S(1)}, u32[]{:S(2)}, u32[]{:S(2)}) collective-permute-start(bf16[2,96,1792]{2,1,0:T(8,128)(2,1)} %get-tuple-element.255), channel_id=1, source_target_pairs={{0,4},{4,0},{8,12},{12,8},{16,20},{20,16},{24,28},{28,24},{1,5},{5... | collective-permute-start | bytes 2064392 | tf_op jit(solution)/shard_map/ppermute | solution.py:847
  240.1 16.2 %collective-permute-start.35 = (bf16[1,192,1536]{2,1,0:T(8,128)(2,1)}, bf16[1,192,1536]{2,1,0:T(8,128)(2,1)S(1)}, u32[]{:S(2)}, u32[]{:S(2)}) collective-permute-start(bf16[1,192,1536]{2,1,0:T(8,128)(2,1)} %get-tuple-element.254), channel_id=1, source_target_pairs={{0,2},{1,3},{2,0},{3,1},{4,6},{5,7},{6,4},{7,5},{8,10},{9,11},{10,... | collective-permute-start | bytes 1769480 | tf_op jit(solution)/shard_map/ppermute | solution.py:847
  240.9 15.5 %collective-permute-start.37 = (bf16[1,48,3072]{2,1,0:T(8,128)(2,1)}, bf16[1,48,3072]{2,1,0:T(8,128)(2,1)S(1)}, u32[]{:S(2)}, u32[]{:S(2)}) collective-permute-start(bf16[1,48,3072]{2,1,0:T(8,128)(2,1)} %get-tuple-element.256.refs_8_), channel_id=1, source_target_pairs={{0,16},{4,20},{8,24},{12,28},{16,0},{20,4},{24,8},{28,12},{1,17},{... | collective-permute-start | bytes 884744 | tf_op jit(solution)/shard_map/ppermute | solution.py:847
  241.2 15.2 %collective-permute-start.38 = (bf16[2,5376]{1,0:T(2,128)(2,1)S(1)}, bf16[2,5376]{1,0:T(2,128)(2,1)S(1)}, u32[]{:S(2)}, u32[]{:S(2)}) collective-permute-start(bf16[2,5376]{1,0:T(2,128)(2,1)S(1)} %copy-done.26), channel_id=1, source_target_pairs={{0,16},{4,20},{8,24},{12,28},{16,0},{20,4},{24,8},{28,12},{1,17},{... | collective-permute-start | bytes 64520 | tf_op jit(solution)/shard_map/ppermute | solution.py:847
  256.5 17.7 %collective-permute-start.43 = (bf16[4,5376]{1,0:T(4,128)(2,1)S(1)}, bf16[4,5376]{1,0:T(4,128)(2,1)S(1)}, u32[]{:S(2)}, u32[]{:S(2)}) collective-permute-start(bf16[4,5376]{1,0:T(4,128)(2,1)S(1)} %pad_maximum_fusion.2), channel_id=1, source_target_pairs={{0,8},{4,12},{8,0},{12,4},{16,24},{20,28},{24,16},{28,20},{1,9},{5... | collective-permute-start | bytes 129032 | tf_op jit(solution)/shard_map/ppermute | solution.py:847
  284.2 34.5 %collective-permute-start.58 = (bf16[1,96,3072]{2,1,0:T(8,128)(2,1)S(1)}, bf16[1,96,3072]{2,1,0:T(8,128)(2,1)S(1)}, u32[]{:S(2)}, u32[]{:S(2)}) collective-permute-start(bf16[1,96,3072]{2,1,0:T(8,128)(2,1)S(1)} %copy-done.28), channel_id=1, source_target_pairs={{0,4},{4,0},{8,12},{12,8},{16,20},{20,16},{24,28},{28,24},{1,5},{5... | collective-permute-start | bytes 1769480 | tf_op jit(solution)/shard_map/ppermute | solution.py:847
  288.6 18.9 %collective-permute-start.51 = (bf16[16,5376]{1,0:T(8,128)(2,1)S(1)}, bf16[16,5376]{1,0:T(8,128)(2,1)S(1)}, u32[]{:S(2)}, u32[]{:S(2)}) collective-permute-start(bf16[16,5376]{1,0:T(8,128)(2,1)S(1)} %pad_maximum_fusion), channel_id=1, source_target_pairs={{0,2},{1,3},{2,0},{3,1},{4,6},{5,7},{6,4},{7,5},{8,10},{9,11},{10,... | collective-permute-start | bytes 516104 | tf_op jit(solution)/shard_map/ppermute | solution.py:847
  292.6 15.5 %collective-permute-start.50 = (bf16[1,48,1792]{2,1,0:T(8,128)(2,1)}, bf16[1,48,1792]{2,1,0:T(8,128)(2,1)S(1)}, u32[]{:S(2)}, u32[]{:S(2)}) collective-permute-start(bf16[1,48,1792]{2,1,0:T(8,128)(2,1)} %get-tuple-element.282.refs_2_), channel_id=1, source_target_pairs={{0,16},{4,20},{8,24},{12,28},{16,0},{20,4},{24,8},{28,12},{1,17},{... | collective-permute-start | bytes 516104 | tf_op jit(solution)/shard_map/ppermute | solution.py:847
  292.6 14.9 %collective-permute-start.49 = (bf16[1,48,1536]{2,1,0:T(8,128)(2,1)}, bf16[1,48,1536]{2,1,0:T(8,128)(2,1)S(1)}, u32[]{:S(2)}, u32[]{:S(2)}) collective-permute-start(bf16[1,48,1536]{2,1,0:T(8,128)(2,1)} %get-tuple-element.281.refs_0_), channel_id=1, source_target_pairs={{0,16},{4,20},{8,24},{12,28},{16,0},{20,4},{24,8},{28,12},{1,17},{... | collective-permute-start | bytes 442376 | tf_op jit(solution)/shard_map/ppermute | solution.py:847
  (80 other events, 480.2 us)

commit v3 on v2

--- a/solution.py
+++ b/solution.py
@@ -74,9 +74,12 @@
 
 def piece_copies(refs, offsets, spot_ref, whole, sems):
     copies = []
-    for k, (ref, offset) in enumerate(zip(refs, offsets)):
-        count = ref.shape[0]
-        place = whole.at[pl.ds(pl.multiple_of((spot_ref[0] ^ offset) * count, 16), count), :]
+    for k, (ref, (offset, part, rows)) in enumerate(zip(refs, offsets)):
+        first = (spot_ref[0] ^ offset) * rows
+        if part is not None:
+            half = high_bit(spot_ref, 1, 1)
+            first = first + (half if part == "near" else 1 - half) * (rows // 2)
+        place = whole.at[pl.ds(pl.multiple_of(first, 16), ref.shape[0]), :]
         copies.append(pltpu.make_async_copy(ref, place, sems.at[k]))
     return copies
 
@@ -137,15 +140,6 @@
     return lane < HEAD_DIM
 
 
-def head_probs(query_pair, key_pair, first, head):
-    keep = first if head == 0 else jnp.logical_not(first)
-    query_head = jnp.where(keep, query_pair, jnp.zeros_like(query_pair))
-    scores = dot_nt(query_head, key_pair) * HEAD_DIM ** (-0.5)
-    row_max = jnp.max(scores, axis=-1, keepdims=True)
-    exped = jnp.exp(scores - row_max)
-    return exped * (1.0 / jnp.sum(exped, axis=-1, keepdims=True))
-
-
 def attn_kernel(offsets, *refs):
     count = len(offsets)
     spot_ref, qkv_ref, tok_ref, cot_ref, mod_ref, bias_ref = refs[:6]
@@ -166,9 +160,13 @@
         key_pair = qkv_ref[:, pl.ds(width + pair * 128, 128)]
         value_pair = qkv_ref[:, pl.ds(2 * width + pair * 128, 128)]
         parts = []
+        none = jnp.zeros_like(query_pair)
         for head in range(2):
-            probs_low = head_probs(query_pair, key_pair, first, head).astype(BF16)
-            parts.append(dot_nn(probs_low, value_pair))
+            keep = first if head == 0 else jnp.logical_not(first)
+            scores = dot_nt(key_pair, jnp.where(keep, query_pair, none)) * HEAD_DIM ** (-0.5)
+            exped = jnp.exp(scores - jnp.max(scores, axis=0, keepdims=True))
+            probs = exped * (1.0 / jnp.sum(exped, axis=0, keepdims=True))
+            parts.append(dot_tn(probs.astype(BF16), value_pair))
         mixed_ref[:, cols] = jnp.where(first, parts[0], parts[1]).astype(BF16)
 
     @pl.when(pl.program_id(0) == 0)
@@ -222,7 +220,7 @@
     )(spot, qkv, tokens, cot, modulation[:, None, :], bias, *pieces)
 
 
-FF_BLOCK = 512
+FF_BLOCK = 768
 
 
 def gelu_kernel(offsets, *refs):
@@ -315,17 +313,17 @@
     )(spot, counts, act_low, tokens, branch_one, cot, modulation, bias, *pieces)
 
 
-def mlp_bwd_kernel(offsets, slots, *refs):
-    count = len(offsets)
+def mlp_bwd_kernel(one_offsets, two_offsets, slots, *refs):
+    count, both = len(one_offsets), len(one_offsets) + len(two_offsets)
     spot_ref, low_ref, deriv_ref, tok_ref, branch_ref, cot_ref, mod_ref = refs[:7]
     one_pieces = refs[7 : 7 + count]
-    two_pieces = refs[7 + count : 7 + 2 * count]
+    two_pieces = refs[7 + count : 7 + both]
     (low_pre_ref, fc1_b_ref, mid_ref, low_one_ref, sums_ref, one, two, acc, sems_one, sems_two) = refs[
-        7 + 2 * count :
+        7 + both :
     ]
     step = pl.program_id(0)
-    copies_two = piece_copies(two_pieces, offsets, spot_ref, two, sems_two)
-    copies_one = piece_copies(one_pieces, offsets, spot_ref, one, sems_one)
+    copies_two = piece_copies(two_pieces, two_offsets, spot_ref, two, sems_two)
+    copies_one = piece_copies(one_pieces, one_offsets, spot_ref, one, sems_one)
 
     @pl.when(step == 0)
     def _():
@@ -381,7 +379,7 @@
     block = pl.BlockSpec((rows, FF_BLOCK), lambda j: (0, j))
     whole = pl.BlockSpec((rows, width), lambda j: (0, 0))
     return pl.pallas_call(
-        functools.partial(mlp_bwd_kernel, one[1], slots),
+        functools.partial(mlp_bwd_kernel, one[1], two[1], slots),
         grid=(hidden_units // FF_BLOCK,),
         in_specs=specs(1, pltpu.SMEM)
         + [whole, block, whole, whole, whole, pl.BlockSpec((slots, 6 * width), lambda j: (0, 0))]
@@ -427,16 +425,18 @@
         grads = []
         for head in range(2):
             keep = first if head == 0 else jnp.logical_not(first)
-            probs = head_probs(query_pair, key_pair, first, head)
-            grad_head = jnp.where(keep, grad_pair, jnp.zeros_like(grad_pair))
-            grad_probs = dot_nt(grad_head, value_pair)
-            row_dot = jnp.sum(probs * grad_probs, axis=-1, keepdims=True)
-            grad_scores = (probs * (grad_probs - row_dot) * HEAD_DIM ** (-0.5)).astype(BF16)
+            none = jnp.zeros_like(query_pair)
+            scores = dot_nt(key_pair, jnp.where(keep, query_pair, none)) * HEAD_DIM ** (-0.5)
+            exped = jnp.exp(scores - jnp.max(scores, axis=0, keepdims=True))
+            probs = exped * (1.0 / jnp.sum(exped, axis=0, keepdims=True))
+            grad_probs = dot_nt(value_pair, jnp.where(keep, grad_pair, none))
+            dots = jnp.sum(probs * grad_probs, axis=0, keepdims=True)
+            grad_scores = (probs * (grad_probs - dots) * HEAD_DIM ** (-0.5)).astype(BF16)
             grads.append(
                 (
-                    dot_nn(grad_scores, key_pair),
-                    dot_tn(grad_scores, query_pair),
-                    dot_tn(probs.astype(BF16), grad_pair),
+                    dot_tn(grad_scores, key_pair),
+                    dot_nn(grad_scores, query_pair),
+                    dot_nn(probs.astype(BF16), grad_pair),
                 )
             )
         grad_query, grad_key, grad_value = (
@@ -568,7 +568,7 @@
     rows, in_dim = left.shape
     out_dim = right.shape[1]
     depth = in_dim // shards
-    block = 512 if out_dim % 512 == 0 else 256
+    block = out_dim // 2 if out_dim > 1024 else out_dim
     per_step = shards // 2 if in_dim <= 768 else 1
     out_block = pl.BlockSpec((per_step, depth, block), lambda i, j: (i, 0, j))
     dims = (shards // 2, depth, out_dim)
@@ -600,9 +600,9 @@
     depth = keep_a.shape[1]
     width = hidden_ref.shape[1]
     core = spot_ref[0] & 1
-    for part, (keep_ref, send_ref) in enumerate([(keep_a, send_a)] * 2 + [(keep_b, send_b)]):
-        total = dot_tn(hidden_ref[...], qkv_ref[:, pl.ds(part * width, width)])
-        split_store(core, total, depth, keep_ref, send_ref, pl.ds(part % 2 * width, width))
+    total = dot_tn(hidden_ref[...], qkv_ref[...])
+    split_store(core, total[:, : 2 * width], depth, keep_a, send_a, slice(None))
+    split_store(core, total[:, 2 * width :], depth, keep_b, send_b, pl.ds(0, width))
     total = dot_tn(mixed_ref[...], low_ref[...])
     split_store(core, total, depth, keep_b, send_b, pl.ds(width, width))
     extra[...] = jnp.zeros_like(extra)
@@ -857,30 +857,61 @@
 
 
 def gather_ordered(value, axis):
+    dims = value.shape
     value = value[None]
-    for bit in axis.bits:
-        value = ordered(axis.high(bit), value, axis.swap(value, bit))
+    for bit in reversed(axis.bits):
+        other = axis.swap(value, bit)
+        high = axis.high(bit)
+        value = jnp.stack([jnp.where(high, other, value), jnp.where(high, value, other)], 1)
+        value = value.reshape((-1,) + dims)
     return value
 
 
 class Gather:
-    def __init__(self, piece, shard):
-        self.shard = shard
+    def __init__(self, piece, shard, rep, split):
+        self.shard, self.rep = shard, rep
         self.own = piece
-        self.swapped = [(shard.swap(piece, 1), 1)]
+        half = piece.shape[0] // 2
+        self.split = split is not None and half % 16 == 0 and rep.size > 1
+        self.send = piece
+        if self.split:
+            late = after(piece, split)
+            self.send = lax.dynamic_slice_in_dim(late, rep.high(1).astype(jnp.int32) * half, half, 0)
+        self.held = [(piece, 0, None)]
+        self.fars = []
+        self.swapped = []
 
     def near(self, *gate):
-        self.held = [(self.own, 0)]
         for bit in reversed(self.shard.bits[1:]):
-            for value, offset in list(self.held):
-                self.held.append((self.shard.swap(after(value, *gate), bit), offset ^ bit))
+            for value, offset, part in list(self.held):
+                if value is self.own and self.split:
+                    value, part = self.send, "near"
+                self.held.append((self.shard.swap(after(value, *gate), bit), offset ^ bit, part))
         return self.held[-1][0]
 
-    def pieces(self, *gate):
-        for value, offset in self.held[1:]:
-            self.swapped.append((self.shard.swap(after(value, *gate), 1), offset ^ 1))
-        held = self.held + self.swapped
-        return [value for value, _ in held], tuple(offset for _, offset in held)
+    def far(self, *gate):
+        for value, offset, part in self.held:
+            if part == "near":
+                self.fars.append((self.rep.swap(after(value, *gate), 1), offset, "far"))
+        return self.fars[-1][0] if self.fars else self.held[-1][0]
+
+    def swap_own(self, *gate):
+        self.swap(self.held[:1], *gate)
+
+    def swap_near(self, *gate):
+        self.swap(self.held[1:], *gate)
+
+    def swap_far(self, *gate):
+        self.swap(self.fars, *gate)
+
+    def swap(self, held, *gate):
+        for value, offset, part in held:
+            self.swapped.append((self.shard.swap(after(value, *gate), 1), offset ^ 1, part))
+
+    def pieces(self):
+        every = self.held + self.fars + self.swapped
+        rows = self.own.shape[0]
+        return [value for value, _, _ in every], tuple((offset, part, rows) for _, offset, part in every)
 
 
 def plan(order, rows):
@@ -1048,6 +1079,14 @@
             chain.commit(results[: len(share)])
             results = results[len(share) :]
     return got[1][0] if len(values) == 1 else got[1]
+
+
+def rounds(spot, chains, most):
+    for _ in range(most):
+        running = [chain for chain in chains if chain.running()]
+        if not running:
+            return
+        together(spot, running)
 
 
 def launched(value, *chains):
@@ -1080,57 +1119,79 @@
     rows = slots * seq
     depth = ada_weight.shape[0]
 
-    qkv_gather = Gather(qkv_weight, shard)
-    proj_gather = Gather(proj_weight, shard)
-    fc1_gather = Gather(fc1_weight, shard)
-    fc2_gather = Gather(fc2_weight, shard)
-
-    slots_here = condition
-    for bit in shard.bits:
-        slots_here = jnp.concatenate([slots_here, shard.swap(slots_here, bit)], 0)
-    near = proj_gather.near(qkv_gather.near())
+    slots_here = condition[None]
+    arrived = []
+    for bit in reversed(shard.bits):
+        arrived.append(shard.swap(slots_here, bit))
+        slots_here = jnp.stack([slots_here, arrived[-1]], 1).reshape((-1,) + condition.shape)
+    slots_here = slots_here.reshape(-1, width)
     silu_group = jax.nn.silu(slots_here.astype(F32)).astype(BF16)
     my_cols = lax.dynamic_slice_in_dim(silu_group, shard.index * depth, depth, 1)
+    ada_late, counts, *bias_list = lax.optimization_barrier(
+        (ada_bias, counts, qv_bias, proj_bias, fc1_bias, fc2_bias, arrived[0])
+    )[:-1]
     own_bias = lax.dynamic_update_slice(
-        jnp.zeros((6 * width,), F32), ada_bias.astype(F32), (shard.index * ada_bias.shape[0],)
+        jnp.zeros((6 * width,), F32), ada_late.astype(F32), (shard.index * ada_bias.shape[0],)
     )
     modulation = dot_nn(my_cols, ada_weight) + own_bias[None]
+
+    packed = jnp.concatenate(bias_list).astype(F32)
+    packed = jnp.pad(packed, (0, 6 * width - packed.shape[0]))[None]
+    qkv_gather = Gather(qkv_weight, shard, rep, None)
+    near = qkv_gather.near(arrived[0])
+    qkv_gather.swap_own(slots_here)
+    queued = []
     for bit in reversed(shard.bits):
         half = modulation.shape[0] // 2
-        modulation = modulation[:half] + shard.swap(modulation[half:], bit)
-
-    bias_list = (qv_bias, proj_bias, fc1_bias, fc2_bias)
-    packed = jnp.concatenate([after(qv_bias, slots_here), *bias_list[1:]])
-    packed = jnp.pad(packed, (0, -packed.shape[0] % 128)).reshape(-1, 128)
-    group = gather_ordered(packed, shard).reshape(shard.size, -1)
+        queued.append(jnp.concatenate([modulation[half:], packed], 0))
+        came = shard.swap(queued[-1], bit)
+        modulation = modulation[:half] + came[:half]
+        other, high = came[half:], shard.high(bit)
+        packed = jnp.stack([jnp.where(high, other, packed), jnp.where(high, packed, other)], 1)
+        packed = packed.reshape(-1, 6 * width)
+    proj_gather = Gather(proj_weight, shard, rep, None)
+    near_proj = proj_gather.near(queued[0])
+    proj_gather.swap_own(slots_here)
+    fc1_gather = Gather(fc1_weight, shard, rep, queued[0])
+    fc2_gather = Gather(fc2_weight, shard, rep, queued[0])
+    near_one = fc1_gather.near(near)
+    near_two = fc2_gather.near(near_proj)
     wide = []
     start = 0
     for bias in bias_list:
-        wide.append(group[:, start : start + bias.shape[0]].reshape(1, -1).astype(F32))
+        wide.append(packed[:, start : start + bias.shape[0]].reshape(1, -1))
         start += bias.shape[0]
     qv_b, proj_b, fc1_b, fc2_b = wide
 
     live_rows = lax.broadcasted_iota(jnp.int32, (rows, 1), 0) < counts[0] * seq
     cot = jnp.where(live_rows, cotangent, jnp.zeros_like(cotangent))
 
-    near_one = fc1_gather.near(near)
+    qkv_gather.swap_near()
+    proj_gather.swap_near()
     qkv_w = qkv_gather.pieces()
     proj_w = proj_gather.pieces()
     qkv_b = jnp.concatenate([qv_b[:, :width], jnp.zeros((1, width), F32), qv_b[:, width:]], axis=1)
-    hidden_one, qkv = qkv_call(spot, tokens, after(modulation, near), qkv_b, qkv_w, slots)
-    mixed, branch_one, hidden_two, low_two = attn_call(spot,
-        qkv, tokens, cot, modulation, proj_b, proj_w, slots
-    )
-    fc2_gather.near(near_one, hidden_two)
+    hidden_one, qkv = qkv_call(spot, tokens, modulation, qkv_b, qkv_w, slots)
+    far_one = fc1_gather.far(qkv)
+    fc1_gather.swap_near(qkv)
+    fc1_gather.swap_own(qkv)
+    fc2_gather.swap_own(qkv)
+    mixed, branch_one, hidden_two, low_two = attn_call(
+        spot, after(qkv, near_one), tokens, cot, modulation, proj_b, proj_w, slots
+    )
+    far_two = fc2_gather.far(hidden_two)
+    fc2_gather.swap_near(hidden_two)
+    fc1_gather.swap_far(hidden_two)
     fc1_w = fc1_gather.pieces()
-    act_low, derivative = gelu_call(spot, hidden_two, fc1_b, fc1_w)
+    act_low, derivative = gelu_call(spot, after(hidden_two, near_two), fc1_b, fc1_w)
+    fc2_gather.swap_far(act_low)
+    fc2_w = fc2_gather.pieces()
 
     shard_steps = [(shard, bit) for bit in reversed(shard.bits[1:])]
     low_bits = [(rep, bit) for bit in rep.bits[:1]]
     high_bits = [(rep, bit) for bit in rep.bits[1:]]
-    keep, send = wide_grad(spot, act_low, low_two, shard.size, "fc2_grad")
-    fc2_w = fc2_gather.pieces(send)
-    fc2_sum = two_way((keep, after(send, fc2_gather.held[-1][0])), shard, rep)
+    keep, send = wide_grad(spot, act_low, after(low_two, far_two), shard.size, "fc2_grad")
+    fc2_sum = two_way((keep, after(send, *fc2_w[0])), shard, rep)
     block_out, gate_sums = out_call(spot,
         counts, launched(act_low, fc2_sum), tokens, branch_one, cot, modulation, fc2_b, fc2_w, slots
     )
@@ -1158,7 +1219,8 @@
         shard.size,
     )
     first, second, grad_qkv = together(spot, [fc1_sum, fc2_sum], first, second, grad_qkv)
-    first_sum = one_way(first, shard, shard_steps + high_bits[:-1] + low_bits + high_bits[-1:])
+    first_sum = one_way(first, shard, shard_steps + low_bits + high_bits)
+    first_sum.back.reverse()
     second_sum = one_way(second, shard, low_bits + shard_steps + high_bits)
     grad_tokens, slot_values = input_bwd_call(spot,
         launched(grad_qkv, first_sum, second_sum, fc1_sum, fc2_sum),
@@ -1177,23 +1239,13 @@
     def append(mine, other):
         return jnp.concatenate([mine, other], 0)
 
+    group_slots = Chain(slot_values, [(shard, bit, append) for bit in shard.bits])
+    rounds(spot, sums_list + [group_slots], len(shard.bits))
     every = [(rep, bit, append) for bit in reversed(rep.bits)]
-    every += [(shard, bit, append) for bit in reversed(shard.bits)]
-    all_slots = Chain(slot_values, every)
-
-    def to_silu(mine, other):
-        return dot_nt(append(mine, other), ada_weight)
-
-    there = [(shard, bit, append) for bit in shard.bits[:-1]]
-    there += [(shard, shard.bits[-1], to_silu)]
-    there += [(shard, bit, append) for bit in shard.bits]
-    to_cond = Chain(slot_values[:, : 6 * width], there)
-
-    chains = [first_sum, second_sum, fc1_sum, fc2_sum, all_slots, to_cond]
-    active = [chain for chain in chains if chain.running()]
-    while active:
-        together(spot, active)
-        active = [chain for chain in chains if chain.running()]
+    all_slots = Chain(group_slots.value, every)
+    grad_silu = dot_nt(group_slots.value[:, : 6 * width], ada_weight)
+    to_cond = Chain(grad_silu, [(shard, bit, append) for bit in shard.bits])
+    rounds(spot, sums_list + [all_slots, to_cond], 100)
 
     grad_cond = cond_call(spot, to_cond.value, condition, shard.size)
 

time: 346 us -> 326 us (0.942)
  waiting for transfers between devices: 85.3 us -> 73.9 us
  Pallas kernels: 163 us -> 155 us
  other arithmetic: 12.2 us -> 8.13 us
    ppermute x59, waiting for transfers between devices: 85.3 us -> 73.9 us  [swap(): lax.ppermute(value, self.name, [(i, i ^ bit) for i in range(self.size)])]
    pallas_call x1, Pallas kernels: 15.9 us -> 12.4 us  [attn_bwd_call(): pl.pallas_call(attn_bwd_kernel, grid=(slots,), in_specs=[pl.BlockSpec((se...]
    unnamed x94 -> x88, local copies, waits for them, and re-layouts: 15.2 us -> 14.6 us
  transfers between devices with their start and end apart: 59 -> 59, of which waited for: 22 -> 22; matrix products, arithmetic and copies ran while one was open for 7% -> 7% of each run, Pallas kernels for 39% -> 37%
where the time goes in v3:
time: 326 us; the launch traced here: 324 us
  Pallas kernels  155 us (48%)
  waiting for transfers between devices  73.9 us (23%)
  starting transfers between devices  52.6 us (16%)
  local copies, waits for them, and re-layouts  29.3 us (9%)
  other arithmetic  8.13 us (2%)
  matrix products  3.46 us (1%)
    ppermute x59, waiting for transfers between devices, swap(): lax.ppermute(value, self.name, [(i, i ^ bit) for i in range(self.size)])  73.9 us
    ppermute x59, starting transfers between devices, swap(): lax.ppermute(value, self.name, [(i, i ^ bit) for i in range(self.size)])  52.6 us
    pallas_call x12, Pallas kernels, round_call(): pl.pallas_call(functools.partial(round_kernel, kinds), grid_spec=pltpu.Pr...  47.2 us
    pallas_call x1, Pallas kernels, mlp_bwd_call(): pl.pallas_call(functools.partial(mlp_bwd_kernel, one[1], two[1], slots),...  18 us
    unnamed x88, local copies, waits for them, and re-layouts  14.6 us
    pallas_call x2, Pallas kernels, wide_grad(): pl.pallas_call(wide_grad_kernel, grid=(shards // 2 // per_step, out_dim /...  12.8 us
    pallas_call x1, Pallas kernels, attn_bwd_call(): pl.pallas_call(attn_bwd_kernel, grid=(slots,), in_specs=[pl.BlockSpec((se...  12.4 us
    pallas_call x1, Pallas kernels, gelu_call(): pl.pallas_call(functools.partial(gelu_kernel, offsets), grid=(hidden_unit...  10.7 us
  transfers between devices with their start and end apart: 59, of which 22 were waited for; matrix products, arithmetic and copies ran while one was open for 7% of the time, Pallas kernels for 37%

profile of v3, /device:TPU:0, one launch (start us, length us, event | category | flops | bytes accessed | tf_op | source)
XLA Modules:
  0.0 324.4 jit_solution(174315348638181032)
XLA Ops:
  16.5 15.7 %collective-permute-done.2 = f32[5,4608]{1,0:T(8,128)S(1)} collective-permute-done((f32[5,4608]{1,0:T(8,128)S(1)}, f32[5,4608]{1,0:T(8,128)S(1)}, u32[]{:S(2)}, u32[]{:S(2)}) %collective-permute-start.2) | collective-permute-done | bytes 92192 | tf_op jit(solution)/shard_map/ppermute | solution.py:847
  40.1 6.7 %qkv_fwd.1 = (bf16[512,768]{1,0:T(8,128)(2,1)}, bf16[512,2304]{1,0:T(8,128)(2,1)}) custom-call(s32[2]{0:T(128)} %pad_add_fusion.refs_0_.spot_ref, bf16[512,768]{1,0:T(8,128)(2,1)} %refs_2_.5, f32[2,4608]{1,0:T(2,128)} %get-tuple-element.339.refs_2_.refs_6_.refs_4_, f32[1,2304]{1,0:T(1,128)} %fusion.7.refs_3_, bf16[192,2304]{1,0:T(8,128)(2,1)} %refs_8_.3, ...), custom_call_target="tpu_custom_call" | custom-call | tf_op jit(solution)/shard_map/qkv_fwd/pallas_call | solution.py:124
  46.8 4.9 %collective-permute-done.7.refs_4_.refs_8_ = bf16[96,3072]{1,0:T(8,128)(2,1)S(1)} collective-permute-done((bf16[96,3072]{1,0:T(8,128)(2,1)}, bf16[96,3072]{1,0:T(8,128)(2,1)S(1)}, u32[]{:S(2)}, u32[]{:S(2)}) %collective-permute-start.7) | collective-permute-done | bytes 589856 | tf_op jit(solution)/shard_map/ppermute | solution.py:847
  58.5 9.4 %attn_fwd.1 = (bf16[512,768]{1,0:T(8,128)(2,1)}, f32[512,768]{1,0:T(8,128)}, bf16[512,768]{1,0:T(8,128)(2,1)}, bf16[512,768]{1,0:T(8,128)(2,1)}) custom-call(s32[2]{0:T(128)} %pad_add_fusion.refs_0_.spot_ref, bf16[512,2304]{1,0:T(8,128)(2,1)} %get-tuple-element.183.refs_1_.qkv_ref, bf16[512,768]{1,0:T(8,128)(2,1)} %refs_2_.5, ...), custom_call_target="tpu_custom_call" | custom-call | tf_op jit(solution)/shard_map/attn_fwd/pallas_call | solution.py:191
  71.1 10.7 %fc1_gelu.1 = (bf16[512,3072]{1,0:T(8,128)(2,1)}, f32[512,3072]{1,0:T(8,128)}) custom-call(s32[2]{0:T(128)} %pad_add_fusion.refs_0_.spot_ref, bf16[512,768]{1,0:T(8,128)(2,1)} %get-tuple-element.190.refs_1_.left_ref, f32[1,3072]{1,0:T(1,128)} %bitcast.39, bf16[192,3072]{1,0:T(8,128)(2,1)} %refs_7_.2, bf16[96,3072]{1,0:T(8,128)(2,1)} %copy-done.7, ...), custom_call_target="tpu_custom_call" | custom-call | tf_op jit(solution)/shard_map/fc1_gelu/pallas_call | solution.py:253
  84.0 6.5 %fc2_grad.1 = (f32[2,768,768]{2,1,0:T(8,128)}, bf16[2,768,768]{2,1,0:T(8,128)(2,1)}) custom-call(s32[2]{0:T(128)} %pad_add_fusion.refs_0_.spot_ref, bf16[512,3072]{1,0:T(8,128)(2,1)} %get-tuple-element.202.left_ref.refs_2_, bf16[512,768]{1,0:T(8,128)(2,1)} %get-tuple-element.212.right_ref.refs_1_), custom_call_target="tpu_custom_call" | custom-call | tf_op jit(solution)/shard_map/fc2_grad/pallas_call | solution.py:575
  93.4 8.9 %fc2_fwd.1 = (bf16[512,768]{1,0:T(8,128)(2,1)}, f32[2,768]{1,0:T(2,128)}) custom-call(s32[2]{0:T(128)} %pad_add_fusion.refs_0_.spot_ref, s32[1]{0:T(128)S(6)} %copy.34.refs_1_, bf16[512,3072]{1,0:T(8,128)(2,1)} %get-tuple-element.202.left_ref.refs_2_, bf16[512,768]{1,0:T(8,128)(2,1)} %refs_2_.5, f32[512,768]{1,0:T(8,128)} %get-tuple-element.203.refs_4_, ...), custom_call_target="tpu_custom_call" | custom-call | tf_op jit(solution)/shard_map/fc2_fwd/pallas_call | solution.py:302
  102.3 5.6 %sum_round.12 = (f32[1,768,384]{2,1,0:T(8,128)}, bf16[1,768,384]{2,1,0:T(8,128)(2,1)}, f32[2,384,384]{2,1,0:T(8,128)}, bf16[2,384,384]{2,1,0:T(8,128)(2,1)}) custom-call(s32[2]{0:T(128)} %pad_add_fusion.refs_0_.spot_ref, f32[2,768,768]{2,1,0:T(8,128)} %get-tuple-element.207.refs_0_.refs_1_.refs_4_.refs_5_, ...), custom_call_target="tpu_custom_call" | custom-call | tf_op jit(solution)/shard_map/sum_round/pallas_call | solution.py:720
  110.0 18.0 %mlp_bwd.1 = (bf16[512,3072]{1,0:T(8,128)(2,1)}, f32[1,3072]{1,0:T(1,128)}, f32[512,768]{1,0:T(8,128)}, bf16[512,768]{1,0:T(8,128)(2,1)}, f32[5,2,768]{2,1,0:T(2,128)}) custom-call(s32[2]{0:T(128)} %pad_add_fusion.refs_0_.spot_ref, bf16[512,768]{1,0:T(8,128)(2,1)} %get-tuple-element.212.right_ref.refs_1_, f32[512,3072]{1,0:T(8,128)} %get-tuple-element.213.refs_2_, ...), custom_call_target="tpu_custom_call" | custom-call | tf_op jit(solution)/shard_map/mlp_bwd/pallas_call | solution.py:381
  129.0 3.9 %sum_round.13 = (f32[1,384,384]{2,1,0:T(8,128)}, bf16[1,384,384]{2,1,0:T(8,128)(2,1)}, f32[1,384,384]{2,1,0:T(8,128)}, bf16[1,384,384]{2,1,0:T(8,128)(2,1)}) custom-call(s32[2]{0:T(128)} %pad_add_fusion.refs_0_.spot_ref, f32[1,768,384]{2,1,0:T(8,128)} %get-tuple-element.209.refs_0_.refs_1_, f32[1,768,384]{2,1,0:T(8,128)} %get-tuple-element.209.refs_0_.refs_1_, ...), custom_call_target="tpu_custom_call" | custom-call | tf_op jit(solution)/shard_map/sum_round/pallas_call | solution.py:720
  135.0 6.3 %fc1_grad.1 = (f32[2,192,3072]{2,1,0:T(8,128)}, bf16[2,192,3072]{2,1,0:T(8,128)(2,1)}) custom-call(s32[2]{0:T(128)} %pad_add_fusion.refs_0_.spot_ref, bf16[512,768]{1,0:T(8,128)(2,1)} %get-tuple-element.190.refs_1_.left_ref, bf16[512,3072]{1,0:T(8,128)(2,1)} %get-tuple-element.221.right_ref), custom_call_target="tpu_custom_call" | custom-call | tf_op jit(solution)/shard_map/fc1_grad/pallas_call | solution.py:575
  148.3 4.1 %proj_bwd.1.grad_ref = bf16[512,768]{1,0:T(8,128)(2,1)} custom-call(s32[2]{0:T(128)} %pad_add_fusion.refs_0_.spot_ref, bf16[512,768]{1,0:T(8,128)(2,1)} %get-tuple-element.233.refs_1_.refs_4_, bf16[192,768]{1,0:T(8,128)(2,1)} %refs_2_.4, bf16[192,768]{1,0:T(8,128)(2,1)} %collective-permute-done.8.refs_7_.refs_3_, ...), custom_call_target="tpu_custom_call" | custom-call | tf_op jit(solution)/shard_map/proj_bwd/pallas_call | solution.py:491
  157.2 5.6 %sum_round.15 = (f32[1,192,1536]{2,1,0:T(8,128)}, bf16[1,192,1536]{2,1,0:T(8,128)(2,1)}, f32[2,96,1536]{2,1,0:T(8,128)}, bf16[2,96,1536]{2,1,0:T(8,128)(2,1)}, bf16[1,192,768]{2,1,0:T(8,128)(2,1)}) custom-call(s32[2]{0:T(128)} %pad_add_fusion.refs_0_.spot_ref, f32[2,192,3072]{2,1,0:T(8,128)} %get-tuple-element.225.refs_0_.refs_1_.refs_4_.refs_5_, ...), custom_call_target="tpu_custom_call" | custom-call | tf_op jit(solution)/shard_map/sum_round/pallas_call | solution.py:720
  166.5 12.4 %attn_bwd.1 = (bf16[512,2304]{1,0:T(8,128)(2,1)}, f32[2,1,1536]{2,1,0:T(1,128)}) custom-call(bf16[512,2304]{1,0:T(8,128)(2,1)} %get-tuple-element.183.refs_1_.qkv_ref, bf16[512,768]{1,0:T(8,128)(2,1)} %proj_bwd.1.grad_ref), custom_call_target="tpu_custom_call" | custom-call | tf_op jit(solution)/shard_map/attn_bwd/pallas_call | solution.py:455
  180.0 4.0 %sum_round.16 = (f32[1,96,1536]{2,1,0:T(8,128)}, bf16[1,96,1536]{2,1,0:T(8,128)(2,1)}, f32[1,96,1536]{2,1,0:T(8,128)}, bf16[1,96,1536]{2,1,0:T(8,128)(2,1)}, bf16[1,192,768]{2,1,0:T(8,128)(2,1)}) custom-call(s32[2]{0:T(128)} %pad_add_fusion.refs_0_.spot_ref, f32[1,192,1536]{2,1,0:T(8,128)} %get-tuple-element.237.refs_0_.refs_1_, ...), custom_call_target="tpu_custom_call" | custom-call | tf_op jit(solution)/shard_map/sum_round/pallas_call | solution.py:720
  188.6 7.0 %attn_weight_grads.1 = (f32[2,192,1536]{2,1,0:T(8,128)}, bf16[2,192,1536]{2,1,0:T(8,128)(2,1)}, f32[2,192,1792]{2,1,0:T(8,128)}, bf16[2,192,1792]{2,1,0:T(8,128)(2,1)}) custom-call(s32[2]{0:T(128)} %pad_add_fusion.refs_0_.spot_ref, bf16[512,768]{1,0:T(8,128)(2,1)} %get-tuple-element.252.refs_1_, bf16[512,2304]{1,0:T(8,128)(2,1)} %get-tuple-element.273.refs_2_.refs_1_, ...), custom_call_target="tpu_custom_call" | custom-call | tf_op jit(solution)/shard_map/attn_weight_grads/pallas_call | solution.py:630
  196.5 3.5 %sum_round.17 = (f32[1,48,3072]{2,1,0:T(8,128)}, bf16[1,48,3072]{2,1,0:T(8,128)(2,1)}, bf16[1,384,768]{2,1,0:T(8,128)(2,1)}) custom-call(s32[2]{0:T(128)} %pad_add_fusion.refs_0_.spot_ref, f32[1,96,1536]{2,1,0:T(8,128)} %get-tuple-element.265.refs_0_.refs_1_, f32[1,96,1536]{2,1,0:T(8,128)} %get-tuple-element.265.refs_0_.refs_1_, ...), custom_call_target="tpu_custom_call" | custom-call | tf_op jit(solution)/shard_map/sum_round/pallas_call | solution.py:720
  201.0 8.0 %qkv_bwd.1 = (f32[512,768]{1,0:T(8,128)}, bf16[2,5376]{1,0:T(2,128)(2,1)}) custom-call(s32[2]{0:T(128)} %pad_add_fusion.refs_0_.spot_ref, bf16[512,2304]{1,0:T(8,128)(2,1)} %get-tuple-element.273.refs_2_.refs_1_, bf16[512,768]{1,0:T(8,128)(2,1)} %refs_2_.5, f32[512,768]{1,0:T(8,128)} %get-tuple-element.274.refs_3_, ...), custom_call_target="tpu_custom_call" | custom-call | tf_op jit(solution)/shard_map/qkv_bwd/pallas_call | solution.py:540
  209.2 6.0 %collective-permute-done.36.refs_1_ = bf16[1,384,768]{2,1,0:T(8,128)(2,1)S(1)} collective-permute-done((bf16[1,384,768]{2,1,0:T(8,128)(2,1)}, bf16[1,384,768]{2,1,0:T(8,128)(2,1)S(1)}, u32[]{:S(2)}, u32[]{:S(2)}) %collective-permute-start.36) | collective-permute-done | bytes 589856 | tf_op jit(solution)/shard_map/ppermute | solution.py:847
  216.7 6.2 %sum_round.18 = (f32[1,192,1536]{2,1,0:T(8,128)}, bf16[1,192,1536]{2,1,0:T(8,128)(2,1)}, f32[2,96,1792]{2,1,0:T(8,128)}, bf16[2,96,1792]{2,1,0:T(8,128)(2,1)}, bf16[1,48,3072]{2,1,0:T(8,128)(2,1)}) custom-call(s32[2]{0:T(128)} %pad_add_fusion.refs_0_.spot_ref, f32[2,192,1536]{2,1,0:T(8,128)} %get-tuple-element.280.refs_0_.refs_1_, ...), custom_call_target="tpu_custom_call" | custom-call | tf_op jit(solution)/shard_map/sum_round/pallas_call | solution.py:720
  227.5 11.3 %collective-permute-done.39.refs_9_ = bf16[1,48,3072]{2,1,0:T(8,128)(2,1)S(1)} collective-permute-done((bf16[1,48,3072]{2,1,0:T(8,128)(2,1)}, bf16[1,48,3072]{2,1,0:T(8,128)(2,1)S(1)}, u32[]{:S(2)}, u32[]{:S(2)}) %collective-permute-start.39) | collective-permute-done | bytes 294944 | tf_op jit(solution)/shard_map/ppermute | solution.py:847
  240.3 4.1 %sum_round.19 = (f32[1,96,1536]{2,1,0:T(8,128)}, bf16[1,96,1536]{2,1,0:T(8,128)(2,1)}, f32[1,96,1792]{2,1,0:T(8,128)}, bf16[1,96,1792]{2,1,0:T(8,128)(2,1)}, bf16[1,48,3072]{2,1,0:T(8,128)(2,1)}) custom-call(s32[2]{0:T(128)} %pad_add_fusion.refs_0_.spot_ref, f32[1,192,1536]{2,1,0:T(8,128)} %get-tuple-element.290.refs_0_.refs_1_, ...), custom_call_target="tpu_custom_call" | custom-call | tf_op jit(solution)/shard_map/sum_round/pallas_call | solution.py:720
  248.0 8.4 %collective-permute-done.44 = bf16[4,5376]{1,0:T(4,128)(2,1)S(1)} collective-permute-done((bf16[4,5376]{1,0:T(4,128)(2,1)S(1)}, bf16[4,5376]{1,0:T(4,128)(2,1)S(1)}, u32[]{:S(2)}, u32[]{:S(2)}) %collective-permute-start.44) | collective-permute-done | bytes 43040 | tf_op jit(solution)/shard_map/ppermute | solution.py:847
  281.2 8.0 %collective-permute-done.49.refs_1_ = bf16[1,48,1536]{2,1,0:T(8,128)(2,1)S(1)} collective-permute-done((bf16[1,48,1536]{2,1,0:T(8,128)(2,1)}, bf16[1,48,1536]{2,1,0:T(8,128)(2,1)S(1)}, u32[]{:S(2)}, u32[]{:S(2)}) %collective-permute-start.49) | collective-permute-done | bytes 147488 | tf_op jit(solution)/shard_map/ppermute | solution.py:847
  (257 shorter events, 137.4 us)
Async XLA Ops:
  6.3 28.2 %collective-permute-start.4 = (bf16[192,2304]{1,0:T(8,128)(2,1)}, bf16[192,2304]{1,0:T(8,128)(2,1)}, u32[]{:S(2)}, u32[]{:S(2)}) collective-permute-start(bf16[192,2304]{1,0:T(8,128)(2,1)} %refs_8_.3), channel_id=1, source_target_pairs={{0,2},{1,3},{2,0},{3,1},{4,6},{5,7},{6,4},{7,5},{8,10},{9,11},{10,... | collective-permute-start | bytes 2654216 | tf_op jit(solution)/shard_map/ppermute | solution.py:847
  12.5 19.7 %collective-permute-start.2 = (f32[5,4608]{1,0:T(8,128)S(1)}, f32[5,4608]{1,0:T(8,128)S(1)}, u32[]{:S(2)}, u32[]{:S(2)}) collective-permute-start(f32[5,4608]{1,0:T(8,128)S(1)} %pad_maximum_fusion.1), channel_id=1, source_target_pairs={{0,2},{1,3},{2,0},{3,1},{4,6},{5,7},{6,4},{7,5},{8,10},{9,11},{10,... | collective-permute-start | bytes 276488 | tf_op jit(solution)/shard_map/ppermute | solution.py:847
  12.7 25.9 %collective-permute-start.8 = (bf16[192,768]{1,0:T(8,128)(2,1)}, bf16[192,768]{1,0:T(8,128)(2,1)}, u32[]{:S(2)}, u32[]{:S(2)}) collective-permute-start(bf16[192,768]{1,0:T(8,128)(2,1)} %refs_2_.4), channel_id=1, source_target_pairs={{0,2},{1,3},{2,0},{3,1},{4,6},{5,7},{6,4},{7,5},{8,10},{9,11},{10,... | collective-permute-start | bytes 884744 | tf_op jit(solution)/shard_map/ppermute | solution.py:847
  14.6 25.5 %collective-permute-start.5 = (bf16[192,2304]{1,0:T(8,128)(2,1)}, bf16[192,2304]{1,0:T(8,128)(2,1)}, u32[]{:S(2)}, u32[]{:S(2)}) collective-permute-start(bf16[192,2304]{1,0:T(8,128)(2,1)} %refs_8_.3), channel_id=1, source_target_pairs={{0,1},{1,0},{2,3},{3,2},{4,5},{5,4},{6,7},{7,6},{8,9},{9,8},{10,11... | collective-permute-start | bytes 2654216 | tf_op jit(solution)/shard_map/ppermute | solution.py:847
  35.4 16.3 %collective-permute-start.7 = (bf16[96,3072]{1,0:T(8,128)(2,1)}, bf16[96,3072]{1,0:T(8,128)(2,1)S(1)}, u32[]{:S(2)}, u32[]{:S(2)}) collective-permute-start(bf16[96,3072]{1,0:T(8,128)(2,1)} %constant_dynamic-slice_fusion.1), channel_id=1, source_target_pairs={{0,2},{1,3},{2,0},{3,1},{4,6},{5,7},{6,4},{7,5},{8,10},{9,11},{10,... | collective-permute-start | bytes 1769480 | tf_op jit(solution)/shard_map/ppermute | solution.py:847
  38.6 29.4 %collective-permute-start.11 = (bf16[384,768]{1,0:T(8,128)(2,1)}, bf16[384,768]{1,0:T(8,128)(2,1)}, u32[]{:S(2)}, u32[]{:S(2)}) collective-permute-start(bf16[384,768]{1,0:T(8,128)(2,1)} %constant_dynamic-slice_fusion), channel_id=1, source_target_pairs={{0,2},{1,3},{2,0},{3,1},{4,6},{5,7},{6,4},{7,5},{8,10},{9,11},{10,... | collective-permute-start | bytes 1769480 | tf_op jit(solution)/shard_map/ppermute | solution.py:847
  51.7 16.2 %collective-permute-start.12 = (bf16[96,3072]{1,0:T(8,128)(2,1)S(1)}, bf16[96,3072]{1,0:T(8,128)(2,1)}, u32[]{:S(2)}, u32[]{:S(2)}) collective-permute-start(bf16[96,3072]{1,0:T(8,128)(2,1)S(1)} %collective-permute-done.7.refs_4_.refs_8_), channel_id=1, source_target_pairs={{0,4},{4,0},{8,12},{12,8},{16,20},{20,16},{24,28},{28,24},{1,5},{5... | collective-permute-start | bytes 1769480 | tf_op jit(solution)/shard_map/ppermute | solution.py:847
  53.6 16.5 %collective-permute-start.14 = (bf16[192,3072]{1,0:T(8,128)(2,1)}, bf16[192,3072]{1,0:T(8,128)(2,1)}, u32[]{:S(2)}, u32[]{:S(2)}) collective-permute-start(bf16[192,3072]{1,0:T(8,128)(2,1)} %refs_7_.2), channel_id=1, source_target_pairs={{0,1},{1,0},{2,3},{3,2},{4,5},{5,4},{6,7},{7,6},{8,9},{9,8},{10,11... | collective-permute-start | bytes 3538952 | tf_op jit(solution)/shard_map/ppermute | solution.py:847
  68.1 15.9 %collective-permute-start.16 = (bf16[384,768]{1,0:T(8,128)(2,1)}, bf16[384,768]{1,0:T(8,128)(2,1)S(1)}, u32[]{:S(2)}, u32[]{:S(2)}) collective-permute-start(bf16[384,768]{1,0:T(8,128)(2,1)} %collective-permute-done.11.refs_9_.refs_14_), channel_id=1, source_target_pairs={{0,4},{4,0},{8,12},{12,8},{16,20},{20,16},{24,28},{28,24},{1,5},{5... | collective-permute-start | bytes 1769480 | tf_op jit(solution)/shard_map/ppermute | solution.py:847
  68.2 22.4 %collective-permute-start.17 = (bf16[768,768]{1,0:T(8,128)(2,1)S(1)}, bf16[768,768]{1,0:T(8,128)(2,1)S(1)}, u32[]{:S(2)}, u32[]{:S(2)}) collective-permute-start(bf16[768,768]{1,0:T(8,128)(2,1)S(1)} %copy-done.2), channel_id=1, source_target_pairs={{0,1},{1,0},{2,3},{3,2},{4,5},{5,4},{6,7},{7,6},{8,9},{9,8},{10,11... | collective-permute-start | bytes 3538952 | tf_op jit(solution)/shard_map/ppermute | solution.py:847
  69.9 20.6 %collective-permute-start.18 = (bf16[384,768]{1,0:T(8,128)(2,1)}, bf16[384,768]{1,0:T(8,128)(2,1)S(1)}, u32[]{:S(2)}, u32[]{:S(2)}) collective-permute-start(bf16[384,768]{1,0:T(8,128)(2,1)} %collective-permute-done.11.refs_9_.refs_14_), channel_id=1, source_target_pairs={{0,1},{1,0},{2,3},{3,2},{4,5},{5,4},{6,7},{7,6},{8,9},{9,8},{10,11... | collective-permute-start | bytes 1769480 | tf_op jit(solution)/shard_map/ppermute | solution.py:847
  107.9 20.1 %collective-permute-start.21 = (bf16[1,768,384]{2,1,0:T(8,128)(2,1)}, bf16[1,768,384]{2,1,0:T(8,128)(2,1)S(1)}, u32[]{:S(2)}, u32[]{:S(2)}) collective-permute-start(bf16[1,768,384]{2,1,0:T(8,128)(2,1)} %get-tuple-element.210), channel_id=1, source_target_pairs={{0,2},{1,3},{2,0},{3,1},{4,6},{5,7},{6,4},{7,5},{8,10},{9,11},{10,... | collective-permute-start | bytes 1769480 | tf_op jit(solution)/shard_map/ppermute | solution.py:847
  109.4 18.6 %collective-permute-start.22 = (bf16[2,384,384]{2,1,0:T(8,128)(2,1)}, bf16[2,384,384]{2,1,0:T(8,128)(2,1)S(1)}, u32[]{:S(2)}, u32[]{:S(2)}) collective-permute-start(bf16[2,384,384]{2,1,0:T(8,128)(2,1)} %get-tuple-element.211), channel_id=1, source_target_pairs={{0,4},{4,0},{8,12},{12,8},{16,20},{20,16},{24,28},{28,24},{1,5},{5... | collective-permute-start | bytes 1769480 | tf_op jit(solution)/shard_map/ppermute | solution.py:847
  162.7 16.1 %collective-permute-start.27 = (bf16[1,192,1536]{2,1,0:T(8,128)(2,1)}, bf16[1,192,1536]{2,1,0:T(8,128)(2,1)S(1)}, u32[]{:S(2)}, u32[]{:S(2)}) collective-permute-start(bf16[1,192,1536]{2,1,0:T(8,128)(2,1)} %get-tuple-element.238), channel_id=1, source_target_pairs={{0,2},{1,3},{2,0},{3,1},{4,6},{5,7},{6,4},{7,5},{8,10},{9,11},{10,... | collective-permute-start | bytes 1769480 | tf_op jit(solution)/shard_map/ppermute | solution.py:847
  163.3 15.6 %collective-permute-start.28 = (bf16[2,96,1536]{2,1,0:T(8,128)(2,1)}, bf16[2,96,1536]{2,1,0:T(8,128)(2,1)S(1)}, u32[]{:S(2)}, u32[]{:S(2)}) collective-permute-start(bf16[2,96,1536]{2,1,0:T(8,128)(2,1)} %get-tuple-element.239), channel_id=1, source_target_pairs={{0,4},{4,0},{8,12},{12,8},{16,20},{20,16},{24,28},{28,24},{1,5},{5... | collective-permute-start | bytes 1769480 | tf_op jit(solution)/shard_map/ppermute | solution.py:847
  163.8 15.0 %collective-permute-start.29 = (bf16[1,192,768]{2,1,0:T(8,128)(2,1)}, bf16[1,192,768]{2,1,0:T(8,128)(2,1)S(1)}, u32[]{:S(2)}, u32[]{:S(2)}) collective-permute-start(bf16[1,192,768]{2,1,0:T(8,128)(2,1)} %get-tuple-element.240.refs_8_), channel_id=1, source_target_pairs={{0,16},{4,20},{8,24},{12,28},{16,0},{20,4},{24,8},{28,12},{1,17},{... | collective-permute-start | bytes 884744 | tf_op jit(solution)/shard_map/ppermute | solution.py:847
  195.6 19.6 %collective-permute-start.34 = (bf16[2,192,1792]{2,1,0:T(8,128)(2,1)}, bf16[2,192,1792]{2,1,0:T(8,128)(2,1)S(1)}, u32[]{:S(2)}, u32[]{:S(2)}) collective-permute-start(bf16[2,192,1792]{2,1,0:T(8,128)(2,1)} %get-tuple-element.264), channel_id=1, source_target_pairs={{0,1},{1,0},{2,3},{3,2},{4,5},{5,4},{6,7},{7,6},{8,9},{9,8},{10,11... | collective-permute-start | bytes 4128776 | tf_op jit(solution)/shard_map/ppermute | solution.py:847
  195.7 19.5 %collective-permute-start.33 = (bf16[2,192,1536]{2,1,0:T(8,128)(2,1)}, bf16[2,192,1536]{2,1,0:T(8,128)(2,1)S(1)}, u32[]{:S(2)}, u32[]{:S(2)}) collective-permute-start(bf16[2,192,1536]{2,1,0:T(8,128)(2,1)} %get-tuple-element.263), channel_id=1, source_target_pairs={{0,1},{1,0},{2,3},{3,2},{4,5},{5,4},{6,7},{7,6},{8,9},{9,8},{10,11... | collective-permute-start | bytes 3538952 | tf_op jit(solution)/shard_map/ppermute | solution.py:847
  200.0 15.2 %collective-permute-start.36 = (bf16[1,384,768]{2,1,0:T(8,128)(2,1)}, bf16[1,384,768]{2,1,0:T(8,128)(2,1)S(1)}, u32[]{:S(2)}, u32[]{:S(2)}) collective-permute-start(bf16[1,384,768]{2,1,0:T(8,128)(2,1)} %get-tuple-element.271.refs_0_), channel_id=1, source_target_pairs={{0,4},{4,0},{8,12},{12,8},{16,20},{20,16},{24,28},{28,24},{1,5},{5... | collective-permute-start | bytes 1769480 | tf_op jit(solution)/shard_map/ppermute | solution.py:847
  222.9 16.5 %collective-permute-start.38 = (bf16[2,96,1792]{2,1,0:T(8,128)(2,1)}, bf16[2,96,1792]{2,1,0:T(8,128)(2,1)S(1)}, u32[]{:S(2)}, u32[]{:S(2)}) collective-permute-start(bf16[2,96,1792]{2,1,0:T(8,128)(2,1)} %get-tuple-element.287), channel_id=1, source_target_pairs={{0,4},{4,0},{8,12},{12,8},{16,20},{20,16},{24,28},{28,24},{1,5},{5... | collective-permute-start | bytes 2064392 | tf_op jit(solution)/shard_map/ppermute | solution.py:847
  223.6 15.2 %collective-permute-start.37 = (bf16[1,192,1536]{2,1,0:T(8,128)(2,1)}, bf16[1,192,1536]{2,1,0:T(8,128)(2,1)S(1)}, u32[]{:S(2)}, u32[]{:S(2)}) collective-permute-start(bf16[1,192,1536]{2,1,0:T(8,128)(2,1)} %get-tuple-element.286), channel_id=1, source_target_pairs={{0,2},{1,3},{2,0},{3,1},{4,6},{5,7},{6,4},{7,5},{8,10},{9,11},{10,... | collective-permute-start | bytes 1769480 | tf_op jit(solution)/shard_map/ppermute | solution.py:847
  266.0 35.6 %collective-permute-start.58 = (bf16[1,96,3072]{2,1,0:T(8,128)(2,1)S(1)}, bf16[1,96,3072]{2,1,0:T(8,128)(2,1)S(1)}, u32[]{:S(2)}, u32[]{:S(2)}) collective-permute-start(bf16[1,96,3072]{2,1,0:T(8,128)(2,1)S(1)} %copy-done.26), channel_id=1, source_target_pairs={{0,4},{4,0},{8,12},{12,8},{16,20},{20,16},{24,28},{28,24},{1,5},{5... | collective-permute-start | bytes 1769480 | tf_op jit(solution)/shard_map/ppermute | solution.py:847
  271.4 17.9 %collective-permute-start.51 = (bf16[16,5376]{1,0:T(8,128)(2,1)S(1)}, bf16[16,5376]{1,0:T(8,128)(2,1)S(1)}, u32[]{:S(2)}, u32[]{:S(2)}) collective-permute-start(bf16[16,5376]{1,0:T(8,128)(2,1)S(1)} %pad_maximum_fusion), channel_id=1, source_target_pairs={{0,8},{4,12},{8,0},{12,4},{16,24},{20,28},{24,16},{28,20},{1,9},{5... | collective-permute-start | bytes 516104 | tf_op jit(solution)/shard_map/ppermute | solution.py:847
  274.6 15.4 %collective-permute-start.50 = (bf16[1,48,1792]{2,1,0:T(8,128)(2,1)}, bf16[1,48,1792]{2,1,0:T(8,128)(2,1)S(1)}, u32[]{:S(2)}, u32[]{:S(2)}) collective-permute-start(bf16[1,48,1792]{2,1,0:T(8,128)(2,1)} %get-tuple-element.312.refs_2_), channel_id=1, source_target_pairs={{0,16},{4,20},{8,24},{12,28},{16,0},{20,4},{24,8},{28,12},{1,17},{... | collective-permute-start | bytes 516104 | tf_op jit(solution)/shard_map/ppermute | solution.py:847
  (77 other events, 424.5 us)

commit v4 on v3

--- a/solution.py
+++ b/solution.py
@@ -180,7 +180,8 @@
     normed, _ = row_norm(tok_ref[...].astype(F32) + mod_part(mod, 0, 2, width) * branch)
     scale = 1.0 + mod_part(mod, 0, 4, width)
     hidden_ref[...] = (normed * scale + mod_part(mod, 0, 3, width)).astype(BF16)
-    low_ref[...] = (mod_part(mod, 0, 5, width) * cot_ref[...].astype(F32)).astype(BF16)
+    cot = jnp.where(spot_ref[2] > pl.program_id(0), cot_ref[...].astype(F32), 0.0)
+    low_ref[...] = (mod_part(mod, 0, 5, width) * cot).astype(BF16)
 
 
 def attn_call(spot, qkv, tokens, cot, modulation, bias, weight, slots):
@@ -274,9 +275,9 @@
 
 def out_kernel(offsets, slots, *refs):
     count = len(offsets)
-    spot_ref, live_ref, act_ref, tok_ref, branch_ref, cot_ref, mod_ref, bias_ref = refs[:8]
-    pieces = refs[8 : 8 + count]
-    block_ref, gate_ref, whole, sems = refs[8 + count :]
+    spot_ref, act_ref, tok_ref, branch_ref, cot_ref, mod_ref, bias_ref = refs[:7]
+    pieces = refs[7 : 7 + count]
+    block_ref, gate_ref, whole, sems = refs[7 + count :]
     copies = piece_copies(pieces, offsets, spot_ref, whole, sems)
     for copy in copies:
         copy.start()
@@ -287,21 +288,21 @@
     for slot in range(slots):
         at = pl.ds(slot * seq, seq)
         branch_two = dot_nn(act_ref[at, :], whole[...]) + bias_ref[...]
-        gate_ref[slot : slot + 1, :] = jnp.sum(
-            cot_ref[at, :].astype(F32) * branch_two, axis=0, keepdims=True
-        )
+        live = spot_ref[2] > slot
+        cot = jnp.where(live, cot_ref[at, :].astype(F32), 0.0)
+        gate_ref[slot : slot + 1, :] = jnp.sum(cot * branch_two, axis=0, keepdims=True)
         mid = tok_ref[at, :].astype(F32) + mod_part(mod_ref, slot, 2, width) * branch_ref[at, :]
         block = mid + mod_part(mod_ref, slot, 5, width) * branch_two
-        block_ref[at, :] = jnp.where(live_ref[0] > slot, block, 0.0).astype(BF16)
-
-
-def out_call(spot, counts, act_low, tokens, branch_one, cot, modulation, bias, weight, slots):
+        block_ref[at, :] = jnp.where(live, block, 0.0).astype(BF16)
+
+
+def out_call(spot, act_low, tokens, branch_one, cot, modulation, bias, weight, slots):
     rows, width = tokens.shape
     hidden_units = act_low.shape[1]
     pieces, offsets = weight
     return pl.pallas_call(
         functools.partial(out_kernel, offsets, slots),
-        in_specs=specs(2, pltpu.SMEM) + specs(6) + specs(len(pieces), pl.ANY),
+        in_specs=specs(1, pltpu.SMEM) + specs(6) + specs(len(pieces), pl.ANY),
         out_specs=specs(2),
         out_shape=[shape((rows, width), BF16), shape((slots, width), F32)],
         scratch_shapes=[
@@ -310,7 +311,7 @@
         ],
         name="fc2_fwd",
         **params(2 * rows * width * hidden_units, 2 * (rows + width) * hidden_units),
-    )(spot, counts, act_low, tokens, branch_one, cot, modulation, bias, *pieces)
+    )(spot, act_low, tokens, branch_one, cot, modulation, bias, *pieces)
 
 
 def mlp_bwd_kernel(one_offsets, two_offsets, slots, *refs):
@@ -353,7 +354,7 @@
         for slot in range(slots):
             at = pl.ds(slot * seq, seq)
             branch = branch_ref[at, :]
-            cot = cot_ref[at, :].astype(F32)
+            cot = jnp.where(spot_ref[2] > slot, cot_ref[at, :].astype(F32), 0.0)
             gate_one = mod_part(mod_ref, slot, 2, width)
             normed, inv_std = row_norm(tok_ref[at, :].astype(F32) + gate_one * branch)
             grad_hidden = acc[at, :]
@@ -666,8 +667,11 @@
             out[:, rows:, :] = args[1][...]
 
 
+SMALL_ROUND = 1 << 20
+
+
 def round_call(spot, jobs):
-    split = 2
+    split = 2 if sum(value.size for job in jobs for value in job["args"]) > SMALL_ROUND else 1
     for job in jobs:
         cols = job["args"][0].shape[2] // (1 if job.get("part") is None else 2)
         if job["kind"] == "merge" or cols % 256:
@@ -785,7 +789,7 @@
     row = 0
     for count, out in zip(biases, bias_outs):
         for start, size in bias_rows(count):
-            out[:, start : start + size] = head[row : row + 1, :size]
+            out[start : start + size] = head[row, :size]
             row += 1
 
 
@@ -796,7 +800,7 @@
         in_specs=specs(1, pltpu.SMEM) + specs(2 * parts),
         out_specs=specs(2 + len(biases)),
         out_shape=[shape((rows, 3 * width), F32), shape((rows, width), F32)]
-        + [shape((1, count), F32) for count in biases],
+        + [shape((count,), F32) for count in biases],
         scratch_shapes=[pltpu.VMEM((rows, EXTRA), F32)],
         name="place_attn",
         **params(0, rows * width * 24),
@@ -1128,7 +1132,7 @@
     silu_group = jax.nn.silu(slots_here.astype(F32)).astype(BF16)
     my_cols = lax.dynamic_slice_in_dim(silu_group, shard.index * depth, depth, 1)
     ada_late, counts, *bias_list = lax.optimization_barrier(
-        (ada_bias, counts, qv_bias, proj_bias, fc1_bias, fc2_bias, arrived[0])
+        (ada_bias, counts, qv_bias, proj_bias, fc1_bias, fc2_bias, slots_here)
     )[:-1]
     own_bias = lax.dynamic_update_slice(
         jnp.zeros((6 * width,), F32), ada_late.astype(F32), (shard.index * ada_bias.shape[0],)
@@ -1137,14 +1141,18 @@
 
     packed = jnp.concatenate(bias_list).astype(F32)
     packed = jnp.pad(packed, (0, 6 * width - packed.shape[0]))[None]
-    qkv_gather = Gather(qkv_weight, shard, rep, None)
+    qkv_gather = Gather(qkv_weight, shard, rep, condition)
     near = qkv_gather.near(arrived[0])
+    qkv_gather.far()
     qkv_gather.swap_own(slots_here)
     queued = []
+    partial = []
     for bit in reversed(shard.bits):
         half = modulation.shape[0] // 2
-        queued.append(jnp.concatenate([modulation[half:], packed], 0))
+        send = jnp.concatenate([modulation[half:], packed], 0)
+        queued.append(send if queued else after(send, near))
         came = shard.swap(queued[-1], bit)
+        partial.append(came)
         modulation = modulation[:half] + came[:half]
         other, high = came[half:], shard.high(bit)
         packed = jnp.stack([jnp.where(high, other, packed), jnp.where(high, packed, other)], 1)
@@ -1154,7 +1162,7 @@
     proj_gather.swap_own(slots_here)
     fc1_gather = Gather(fc1_weight, shard, rep, queued[0])
     fc2_gather = Gather(fc2_weight, shard, rep, queued[0])
-    near_one = fc1_gather.near(near)
+    near_one = fc1_gather.near(partial[0])
     near_two = fc2_gather.near(near_proj)
     wide = []
     start = 0
@@ -1163,10 +1171,11 @@
         start += bias.shape[0]
     qv_b, proj_b, fc1_b, fc2_b = wide
 
-    live_rows = lax.broadcasted_iota(jnp.int32, (rows, 1), 0) < counts[0] * seq
-    cot = jnp.where(live_rows, cotangent, jnp.zeros_like(cotangent))
+    spot = jnp.concatenate([spot, counts])
+    cot = cotangent
 
     qkv_gather.swap_near()
+    qkv_gather.swap_far()
     proj_gather.swap_near()
     qkv_w = qkv_gather.pieces()
     proj_w = proj_gather.pieces()
@@ -1192,8 +1201,8 @@
     high_bits = [(rep, bit) for bit in rep.bits[1:]]
     keep, send = wide_grad(spot, act_low, after(low_two, far_two), shard.size, "fc2_grad")
     fc2_sum = two_way((keep, after(send, *fc2_w[0])), shard, rep)
-    block_out, gate_sums = out_call(spot,
-        counts, launched(act_low, fc2_sum), tokens, branch_one, cot, modulation, fc2_b, fc2_w, slots
+    block_out, gate_sums = out_call(
+        spot, launched(act_low, fc2_sum), tokens, branch_one, cot, modulation, fc2_b, fc2_w, slots
     )
     block_out, gate_sums = together(spot, [fc2_sum], block_out, gate_sums)
     low_pre, grad_fc1_b, grad_mid, low_one, sums = mlp_bwd_call(spot,
@@ -1233,7 +1242,7 @@
         qkv_w,
         slots,
     )
-    sums_list = [first_sum, second_sum, fc1_sum, fc2_sum]
+    sums_list = [first_sum, second_sum, fc1_sum] + ([fc2_sum] if fc2_sum.running() else [])
     grad_tokens, slot_values = together(spot, sums_list, grad_tokens, slot_values)
 
     def append(mine, other):
@@ -1263,7 +1272,6 @@
     grad_qkv_w, grad_proj_w, *bias_out = place_attn(
         spot, first_sum.finish(), second_sum.finish(), depth, width, bias_sizes
     )
-    bias_out = [value.reshape(-1) for value in bias_out]
 
     return (
         block_out,

time: 326 us -> 313 us (0.960)
  waiting for transfers between devices: 73.9 us -> 57.2 us
  starting transfers between devices: 52.6 us -> 57.3 us
  other arithmetic: 8.13 us -> 4.64 us
    ppermute x59 -> x61, waiting for transfers between devices: 73.9 us -> 57.2 us  [swap(): lax.ppermute(value, self.name, [(i, i ^ bit) for i in range(self.size)])]
    ppermute x59 -> x61, starting transfers between devices: 52.6 us -> 57.3 us  [swap(): lax.ppermute(value, self.name, [(i, i ^ bit) for i in range(self.size)])]
    unnamed x88 -> x86, local copies, waits for them, and re-layouts: 14.6 us -> 15.1 us
  transfers between devices with their start and end apart: 59 -> 61, of which waited for: 22 -> 21; matrix products, arithmetic and copies ran while one was open for 7% -> 8% of each run, Pallas kernels for 37% -> 39%
where the time goes in v4:
time: 313 us; the launch traced here: 312 us
  Pallas kernels  155 us (50%)
  starting transfers between devices  57.3 us (18%)
  waiting for transfers between devices  57.2 us (18%)
  local copies, waits for them, and re-layouts  32.3 us (10%)
  other arithmetic  4.64 us (1%)
  matrix products  3.45 us (1%)
    ppermute x61, starting transfers between devices, swap(): lax.ppermute(value, self.name, [(i, i ^ bit) for i in range(self.size)])  57.3 us
    ppermute x61, waiting for transfers between devices, swap(): lax.ppermute(value, self.name, [(i, i ^ bit) for i in range(self.size)])  57.2 us
    pallas_call x12, Pallas kernels, round_call(): pl.pallas_call(functools.partial(round_kernel, kinds), grid_spec=pltpu.Pr...  47.4 us
    pallas_call x1, Pallas kernels, mlp_bwd_call(): pl.pallas_call(functools.partial(mlp_bwd_kernel, one[1], two[1], slots),...  18 us
    unnamed x86, local copies, waits for them, and re-layouts  15.1 us
    pallas_call x2, Pallas kernels, wide_grad(): pl.pallas_call(wide_grad_kernel, grid=(shards // 2 // per_step, out_dim /...  12.7 us
    pallas_call x1, Pallas kernels, attn_bwd_call(): pl.pallas_call(attn_bwd_kernel, grid=(slots,), in_specs=[pl.BlockSpec((se...  12.4 us
    pallas_call x1, Pallas kernels, gelu_call(): pl.pallas_call(functools.partial(gelu_kernel, offsets), grid=(hidden_unit...  10.5 us
  transfers between devices with their start and end apart: 61, of which 21 were waited for; matrix products, arithmetic and copies ran while one was open for 8% of the time, Pallas kernels for 39%

profile of v4, /device:TPU:0, one launch (start us, length us, event | category | flops | bytes accessed | tf_op | source)
XLA Modules:
  0.0 311.8 jit_solution(16580612232142564203)
XLA Ops:
  13.4 6.4 %collective-permute-done.2.refs_5_.refs_9_ = bf16[96,2304]{1,0:T(8,128)(2,1)} collective-permute-done((bf16[96,2304]{1,0:T(8,128)(2,1)S(1)}, bf16[96,2304]{1,0:T(8,128)(2,1)}, u32[]{:S(2)}, u32[]{:S(2)}) %collective-permute-start.2) | collective-permute-done | bytes 442400 | tf_op jit(solution)/shard_map/ppermute | solution.py:851
  37.8 6.6 %qkv_fwd.1 = (bf16[512,768]{1,0:T(8,128)(2,1)}, bf16[512,2304]{1,0:T(8,128)(2,1)}) custom-call(s32[3]{0:T(128)} %pad_add_fusion.refs_0_.spot_ref, bf16[512,768]{1,0:T(8,128)(2,1)} %refs_2_.7, f32[2,4608]{1,0:T(2,128)} %get-tuple-element.341.refs_2_.refs_5_.refs_6_.refs_4_, f32[1,2304]{1,0:T(1,128)} %fusion.7.refs_3_, bf16[192,2304]{1,0:T(8,128)(2,1)} %refs_8_.1, ...), custom_call_target="tpu_custom_call" | custom-call | tf_op jit(solution)/shard_map/qkv_fwd/pallas_call | solution.py:124
  52.2 9.5 %attn_fwd.1 = (bf16[512,768]{1,0:T(8,128)(2,1)}, f32[512,768]{1,0:T(8,128)}, bf16[512,768]{1,0:T(8,128)(2,1)}, bf16[512,768]{1,0:T(8,128)(2,1)}) custom-call(s32[3]{0:T(128)} %pad_add_fusion.refs_0_.spot_ref, bf16[512,2304]{1,0:T(8,128)(2,1)} %get-tuple-element.187.refs_1_.qkv_ref, bf16[512,768]{1,0:T(8,128)(2,1)} %refs_2_.7, bf16[512,768]{1,0:T(8,128)(2,1)} %refs_5_.1, ...), custom_call_target="tpu_custom_call" | custom-call | tf_op jit(solution)/shard_map/attn_fwd/pallas_call | solution.py:192
  67.4 10.5 %fc1_gelu.1 = (bf16[512,3072]{1,0:T(8,128)(2,1)}, f32[512,3072]{1,0:T(8,128)}) custom-call(s32[3]{0:T(128)} %pad_add_fusion.refs_0_.spot_ref, bf16[512,768]{1,0:T(8,128)(2,1)} %get-tuple-element.193.refs_1_.left_ref, f32[1,3072]{1,0:T(1,128)} %bitcast.36, bf16[192,3072]{1,0:T(8,128)(2,1)} %refs_7_.4, bf16[96,3072]{1,0:T(8,128)(2,1)} %copy-done.7, ...), custom_call_target="tpu_custom_call" | custom-call | tf_op jit(solution)/shard_map/fc1_gelu/pallas_call | solution.py:254
  78.2 6.4 %fc2_grad.1 = (f32[2,768,768]{2,1,0:T(8,128)}, bf16[2,768,768]{2,1,0:T(8,128)(2,1)}) custom-call(s32[3]{0:T(128)} %pad_add_fusion.refs_0_.spot_ref, bf16[512,3072]{1,0:T(8,128)(2,1)} %get-tuple-element.205.left_ref.refs_1_, bf16[512,768]{1,0:T(8,128)(2,1)} %get-tuple-element.215.right_ref.refs_1_), custom_call_target="tpu_custom_call" | custom-call | tf_op jit(solution)/shard_map/fc2_grad/pallas_call | solution.py:576
  87.5 8.9 %fc2_fwd.1 = (bf16[512,768]{1,0:T(8,128)(2,1)}, f32[2,768]{1,0:T(2,128)}) custom-call(s32[3]{0:T(128)} %pad_add_fusion.refs_0_.spot_ref, bf16[512,3072]{1,0:T(8,128)(2,1)} %get-tuple-element.205.left_ref.refs_1_, bf16[512,768]{1,0:T(8,128)(2,1)} %refs_2_.7, f32[512,768]{1,0:T(8,128)} %get-tuple-element.206.refs_3_.refs_4_, bf16[512,768]{1,0:T(8,128)(2,1)} %refs_5_.1, ...), custom_call_target="tpu_custom_call" | custom-call | tf_op jit(solution)/shard_map/fc2_fwd/pallas_call | solution.py:303
  96.4 5.6 %sum_round.12 = (f32[1,768,384]{2,1,0:T(8,128)}, bf16[1,768,384]{2,1,0:T(8,128)(2,1)}, f32[2,384,384]{2,1,0:T(8,128)}, bf16[2,384,384]{2,1,0:T(8,128)(2,1)}) custom-call(s32[3]{0:T(128)} %pad_add_fusion.refs_0_.spot_ref, f32[2,768,768]{2,1,0:T(8,128)} %get-tuple-element.210.refs_0_.refs_1_.refs_4_.refs_5_, ...), custom_call_target="tpu_custom_call" | custom-call | tf_op jit(solution)/shard_map/sum_round/pallas_call | solution.py:724
  105.2 18.0 %mlp_bwd.1 = (bf16[512,3072]{1,0:T(8,128)(2,1)}, f32[1,3072]{1,0:T(1,128)}, f32[512,768]{1,0:T(8,128)}, bf16[512,768]{1,0:T(8,128)(2,1)}, f32[5,2,768]{2,1,0:T(2,128)}) custom-call(s32[3]{0:T(128)} %pad_add_fusion.refs_0_.spot_ref, bf16[512,768]{1,0:T(8,128)(2,1)} %get-tuple-element.215.right_ref.refs_1_, f32[512,3072]{1,0:T(8,128)} %get-tuple-element.216.refs_2_, ...), custom_call_target="tpu_custom_call" | custom-call | tf_op jit(solution)/shard_map/mlp_bwd/pallas_call | solution.py:382
  124.3 3.9 %sum_round.13 = (f32[1,384,384]{2,1,0:T(8,128)}, bf16[1,384,384]{2,1,0:T(8,128)(2,1)}, f32[1,384,384]{2,1,0:T(8,128)}, bf16[1,384,384]{2,1,0:T(8,128)(2,1)}) custom-call(s32[3]{0:T(128)} %pad_add_fusion.refs_0_.spot_ref, f32[1,768,384]{2,1,0:T(8,128)} %get-tuple-element.212.refs_0_.refs_1_, f32[1,768,384]{2,1,0:T(8,128)} %get-tuple-element.212.refs_0_.refs_1_, ...), custom_call_target="tpu_custom_call" | custom-call | tf_op jit(solution)/shard_map/sum_round/pallas_call | solution.py:724
  129.1 6.3 %fc1_grad.1 = (f32[2,192,3072]{2,1,0:T(8,128)}, bf16[2,192,3072]{2,1,0:T(8,128)(2,1)}) custom-call(s32[3]{0:T(128)} %pad_add_fusion.refs_0_.spot_ref, bf16[512,768]{1,0:T(8,128)(2,1)} %get-tuple-element.193.refs_1_.left_ref, bf16[512,3072]{1,0:T(8,128)(2,1)} %get-tuple-element.224.right_ref), custom_call_target="tpu_custom_call" | custom-call | tf_op jit(solution)/shard_map/fc1_grad/pallas_call | solution.py:576
  142.7 4.1 %proj_bwd.1.grad_ref = bf16[512,768]{1,0:T(8,128)(2,1)} custom-call(s32[3]{0:T(128)} %pad_add_fusion.refs_0_.spot_ref, bf16[512,768]{1,0:T(8,128)(2,1)} %get-tuple-element.236.refs_1_.refs_4_, bf16[192,768]{1,0:T(8,128)(2,1)} %refs_2_.6, bf16[192,768]{1,0:T(8,128)(2,1)} %collective-permute-done.10.refs_7_.refs_3_, ...), custom_call_target="tpu_custom_call" | custom-call | tf_op jit(solution)/shard_map/proj_bwd/pallas_call | solution.py:492
  151.5 5.7 %sum_round.15 = (f32[1,192,1536]{2,1,0:T(8,128)}, bf16[1,192,1536]{2,1,0:T(8,128)(2,1)}, f32[2,96,1536]{2,1,0:T(8,128)}, bf16[2,96,1536]{2,1,0:T(8,128)(2,1)}, bf16[1,192,768]{2,1,0:T(8,128)(2,1)}) custom-call(s32[3]{0:T(128)} %pad_add_fusion.refs_0_.spot_ref, f32[2,192,3072]{2,1,0:T(8,128)} %get-tuple-element.228.refs_0_.refs_1_.refs_4_.refs_5_, ...), custom_call_target="tpu_custom_call" | custom-call | tf_op jit(solution)/shard_map/sum_round/pallas_call | solution.py:724
  161.9 12.4 %attn_bwd.1 = (bf16[512,2304]{1,0:T(8,128)(2,1)}, f32[2,1,1536]{2,1,0:T(1,128)}) custom-call(bf16[512,2304]{1,0:T(8,128)(2,1)} %get-tuple-element.187.refs_1_.qkv_ref, bf16[512,768]{1,0:T(8,128)(2,1)} %proj_bwd.1.grad_ref), custom_call_target="tpu_custom_call" | custom-call | tf_op jit(solution)/shard_map/attn_bwd/pallas_call | solution.py:456
  175.4 4.0 %sum_round.16 = (f32[1,96,1536]{2,1,0:T(8,128)}, bf16[1,96,1536]{2,1,0:T(8,128)(2,1)}, f32[1,96,1536]{2,1,0:T(8,128)}, bf16[1,96,1536]{2,1,0:T(8,128)(2,1)}, bf16[1,192,768]{2,1,0:T(8,128)(2,1)}) custom-call(s32[3]{0:T(128)} %pad_add_fusion.refs_0_.spot_ref, f32[1,192,1536]{2,1,0:T(8,128)} %get-tuple-element.240.refs_0_.refs_1_, ...), custom_call_target="tpu_custom_call" | custom-call | tf_op jit(solution)/shard_map/sum_round/pallas_call | solution.py:724
  183.2 7.0 %attn_weight_grads.1 = (f32[2,192,1536]{2,1,0:T(8,128)}, bf16[2,192,1536]{2,1,0:T(8,128)(2,1)}, f32[2,192,1792]{2,1,0:T(8,128)}, bf16[2,192,1792]{2,1,0:T(8,128)(2,1)}) custom-call(s32[3]{0:T(128)} %pad_add_fusion.refs_0_.spot_ref, bf16[512,768]{1,0:T(8,128)(2,1)} %get-tuple-element.255.refs_1_, bf16[512,2304]{1,0:T(8,128)(2,1)} %get-tuple-element.276.refs_2_.refs_1_, ...), custom_call_target="tpu_custom_call" | custom-call | tf_op jit(solution)/shard_map/attn_weight_grads/pallas_call | solution.py:631
  191.0 3.5 %sum_round.17 = (f32[1,48,3072]{2,1,0:T(8,128)}, bf16[1,48,3072]{2,1,0:T(8,128)(2,1)}, bf16[1,384,768]{2,1,0:T(8,128)(2,1)}) custom-call(s32[3]{0:T(128)} %pad_add_fusion.refs_0_.spot_ref, f32[1,96,1536]{2,1,0:T(8,128)} %get-tuple-element.268.refs_0_.refs_1_, f32[1,96,1536]{2,1,0:T(8,128)} %get-tuple-element.268.refs_0_.refs_1_, ...), custom_call_target="tpu_custom_call" | custom-call | tf_op jit(solution)/shard_map/sum_round/pallas_call | solution.py:724
  195.0 8.0 %qkv_bwd.1 = (f32[512,768]{1,0:T(8,128)}, bf16[2,5376]{1,0:T(2,128)(2,1)}) custom-call(s32[3]{0:T(128)} %pad_add_fusion.refs_0_.spot_ref, bf16[512,2304]{1,0:T(8,128)(2,1)} %get-tuple-element.276.refs_2_.refs_1_, bf16[512,768]{1,0:T(8,128)(2,1)} %refs_2_.7, f32[512,768]{1,0:T(8,128)} %get-tuple-element.277.refs_3_, ...), custom_call_target="tpu_custom_call" | custom-call | tf_op jit(solution)/shard_map/qkv_bwd/pallas_call | solution.py:541
  205.0 6.2 %sum_round.18 = (f32[1,192,1536]{2,1,0:T(8,128)}, bf16[1,192,1536]{2,1,0:T(8,128)(2,1)}, f32[2,96,1792]{2,1,0:T(8,128)}, bf16[2,96,1792]{2,1,0:T(8,128)(2,1)}, bf16[1,48,3072]{2,1,0:T(8,128)(2,1)}) custom-call(s32[3]{0:T(128)} %pad_add_fusion.refs_0_.spot_ref, f32[2,192,1536]{2,1,0:T(8,128)} %get-tuple-element.283.refs_0_.refs_1_, ...), custom_call_target="tpu_custom_call" | custom-call | tf_op jit(solution)/shard_map/sum_round/pallas_call | solution.py:724
  217.1 11.5 %collective-permute-done.40.refs_9_ = bf16[1,48,3072]{2,1,0:T(8,128)(2,1)S(1)} collective-permute-done((bf16[1,48,3072]{2,1,0:T(8,128)(2,1)}, bf16[1,48,3072]{2,1,0:T(8,128)(2,1)S(1)}, u32[]{:S(2)}, u32[]{:S(2)}) %collective-permute-start.40) | collective-permute-done | bytes 294944 | tf_op jit(solution)/shard_map/ppermute | solution.py:851
  229.8 4.1 %sum_round.19 = (f32[1,96,1536]{2,1,0:T(8,128)}, bf16[1,96,1536]{2,1,0:T(8,128)(2,1)}, f32[1,96,1792]{2,1,0:T(8,128)}, bf16[1,96,1792]{2,1,0:T(8,128)(2,1)}, bf16[1,48,3072]{2,1,0:T(8,128)(2,1)}) custom-call(s32[3]{0:T(128)} %pad_add_fusion.refs_0_.spot_ref, f32[1,192,1536]{2,1,0:T(8,128)} %get-tuple-element.293.refs_0_.refs_1_, ...), custom_call_target="tpu_custom_call" | custom-call | tf_op jit(solution)/shard_map/sum_round/pallas_call | solution.py:724
  238.1 7.0 %collective-permute-done.45 = bf16[4,5376]{1,0:T(4,128)(2,1)S(1)} collective-permute-done((bf16[4,5376]{1,0:T(4,128)(2,1)S(1)}, bf16[4,5376]{1,0:T(4,128)(2,1)S(1)}, u32[]{:S(2)}, u32[]{:S(2)}) %collective-permute-start.45) | collective-permute-done | bytes 43040 | tf_op jit(solution)/shard_map/ppermute | solution.py:851
  247.6 3.5 %sum_round.20 = (f32[1,48,1536]{2,1,0:T(8,128)}, bf16[1,48,1536]{2,1,0:T(8,128)(2,1)}, f32[1,48,1792]{2,1,0:T(8,128)}, bf16[1,48,1792]{2,1,0:T(8,128)(2,1)}, bf16[1,96,3072]{2,1,0:T(8,128)(2,1)}) custom-call(s32[3]{0:T(128)} %pad_add_fusion.refs_0_.spot_ref, f32[1,96,1536]{2,1,0:T(8,128)} %get-tuple-element.302.refs_0_.refs_1_, ...), custom_call_target="tpu_custom_call" | custom-call | tf_op jit(solution)/shard_map/sum_round/pallas_call | solution.py:724
  269.2 8.0 %collective-permute-done.50.refs_1_ = bf16[1,48,1536]{2,1,0:T(8,128)(2,1)S(1)} collective-permute-done((bf16[1,48,1536]{2,1,0:T(8,128)(2,1)}, bf16[1,48,1536]{2,1,0:T(8,128)(2,1)S(1)}, u32[]{:S(2)}, u32[]{:S(2)}) %collective-permute-start.50) | collective-permute-done | bytes 147488 | tf_op jit(solution)/shard_map/ppermute | solution.py:851
  303.3 4.3 %collective-permute-done.57.refs_1_ = bf16[1,96,1536]{2,1,0:T(8,128)(2,1)S(1)} collective-permute-done((bf16[1,96,1536]{2,1,0:T(8,128)(2,1)}, bf16[1,96,1536]{2,1,0:T(8,128)(2,1)S(1)}, u32[]{:S(2)}, u32[]{:S(2)}) %collective-permute-start.57) | collective-permute-done | bytes 294944 | tf_op jit(solution)/shard_map/ppermute | solution.py:851
  (256 shorter events, 138.5 us)
Async XLA Ops:
  13.1 22.6 %collective-permute-start.6 = (bf16[192,2304]{1,0:T(8,128)(2,1)}, bf16[192,2304]{1,0:T(8,128)(2,1)}, u32[]{:S(2)}, u32[]{:S(2)}) collective-permute-start(bf16[192,2304]{1,0:T(8,128)(2,1)} %refs_8_.1), channel_id=1, source_target_pairs={{0,1},{1,0},{2,3},{3,2},{4,5},{5,4},{6,7},{7,6},{8,9},{9,8},{10,11... | collective-permute-start | bytes 2654216 | tf_op jit(solution)/shard_map/ppermute | solution.py:851
  19.8 15.8 %collective-permute-start.7 = (bf16[96,2304]{1,0:T(8,128)(2,1)}, bf16[96,2304]{1,0:T(8,128)(2,1)}, u32[]{:S(2)}, u32[]{:S(2)}) collective-permute-start(bf16[96,2304]{1,0:T(8,128)(2,1)} %collective-permute-done.2.refs_5_.refs_9_), channel_id=1, source_target_pairs={{0,1},{1,0},{2,3},{3,2},{4,5},{5,4},{6,7},{7,6},{8,9},{9,8},{10,11... | collective-permute-start | bytes 1327112 | tf_op jit(solution)/shard_map/ppermute | solution.py:851
  19.8 15.1 %collective-permute-start.5 = (bf16[96,2304]{1,0:T(8,128)(2,1)}, bf16[96,2304]{1,0:T(8,128)(2,1)}, u32[]{:S(2)}, u32[]{:S(2)}) collective-permute-start(bf16[96,2304]{1,0:T(8,128)(2,1)} %collective-permute-done.2.refs_5_.refs_9_), channel_id=1, source_target_pairs={{0,4},{4,0},{8,12},{12,8},{16,20},{20,16},{24,28},{28,24},{1,5},{5... | collective-permute-start | bytes 1327112 | tf_op jit(solution)/shard_map/ppermute | solution.py:851
  29.8 16.7 %collective-permute-start.9 = (bf16[96,3072]{1,0:T(8,128)(2,1)}, bf16[96,3072]{1,0:T(8,128)(2,1)S(1)}, u32[]{:S(2)}, u32[]{:S(2)}) collective-permute-start(bf16[96,3072]{1,0:T(8,128)(2,1)} %constant_dynamic-slice_fusion.1), channel_id=1, source_target_pairs={{0,2},{1,3},{2,0},{3,1},{4,6},{5,7},{6,4},{7,5},{8,10},{9,11},{10,... | collective-permute-start | bytes 1769480 | tf_op jit(solution)/shard_map/ppermute | solution.py:851
  46.5 15.2 %collective-permute-start.14 = (bf16[96,3072]{1,0:T(8,128)(2,1)S(1)}, bf16[96,3072]{1,0:T(8,128)(2,1)}, u32[]{:S(2)}, u32[]{:S(2)}) collective-permute-start(bf16[96,3072]{1,0:T(8,128)(2,1)S(1)} %collective-permute-done.9.refs_4_.refs_8_), channel_id=1, source_target_pairs={{0,4},{4,0},{8,12},{12,8},{16,20},{20,16},{24,28},{28,24},{1,5},{5... | collective-permute-start | bytes 1769480 | tf_op jit(solution)/shard_map/ppermute | solution.py:851
  46.8 19.7 %collective-permute-start.16 = (bf16[192,3072]{1,0:T(8,128)(2,1)}, bf16[192,3072]{1,0:T(8,128)(2,1)}, u32[]{:S(2)}, u32[]{:S(2)}) collective-permute-start(bf16[192,3072]{1,0:T(8,128)(2,1)} %refs_7_.4), channel_id=1, source_target_pairs={{0,1},{1,0},{2,3},{3,2},{4,5},{5,4},{6,7},{7,6},{8,9},{9,8},{10,11... | collective-permute-start | bytes 3538952 | tf_op jit(solution)/shard_map/ppermute | solution.py:851
  46.8 16.1 %collective-permute-start.13 = (bf16[384,768]{1,0:T(8,128)(2,1)}, bf16[384,768]{1,0:T(8,128)(2,1)}, u32[]{:S(2)}, u32[]{:S(2)}) collective-permute-start(bf16[384,768]{1,0:T(8,128)(2,1)} %constant_dynamic-slice_fusion), channel_id=1, source_target_pairs={{0,2},{1,3},{2,0},{3,1},{4,6},{5,7},{6,4},{7,5},{8,10},{9,11},{10,... | collective-permute-start | bytes 1769480 | tf_op jit(solution)/shard_map/ppermute | solution.py:851
  51.9 14.1 %collective-permute-start.15 = (bf16[96,3072]{1,0:T(8,128)(2,1)S(1)}, bf16[96,3072]{1,0:T(8,128)(2,1)S(1)}, u32[]{:S(2)}, u32[]{:S(2)}) collective-permute-start(bf16[96,3072]{1,0:T(8,128)(2,1)S(1)} %collective-permute-done.9.refs_4_.refs_8_), channel_id=1, source_target_pairs={{0,1},{1,0},{2,3},{3,2},{4,5},{5,4},{6,7},{7,6},{8,9},{9,8},{10,11... | collective-permute-start | bytes 1769480 | tf_op jit(solution)/shard_map/ppermute | solution.py:851
  62.9 15.2 %collective-permute-start.18 = (bf16[384,768]{1,0:T(8,128)(2,1)}, bf16[384,768]{1,0:T(8,128)(2,1)S(1)}, u32[]{:S(2)}, u32[]{:S(2)}) collective-permute-start(bf16[384,768]{1,0:T(8,128)(2,1)} %collective-permute-done.13.refs_8_.refs_14_), channel_id=1, source_target_pairs={{0,4},{4,0},{8,12},{12,8},{16,20},{20,16},{24,28},{28,24},{1,5},{5... | collective-permute-start | bytes 1769480 | tf_op jit(solution)/shard_map/ppermute | solution.py:851
  64.6 20.0 %collective-permute-start.19 = (bf16[768,768]{1,0:T(8,128)(2,1)S(1)}, bf16[768,768]{1,0:T(8,128)(2,1)S(1)}, u32[]{:S(2)}, u32[]{:S(2)}) collective-permute-start(bf16[768,768]{1,0:T(8,128)(2,1)S(1)} %copy-done.2), channel_id=1, source_target_pairs={{0,1},{1,0},{2,3},{3,2},{4,5},{5,4},{6,7},{7,6},{8,9},{9,8},{10,11... | collective-permute-start | bytes 3538952 | tf_op jit(solution)/shard_map/ppermute | solution.py:851
  66.0 18.6 %collective-permute-start.20 = (bf16[384,768]{1,0:T(8,128)(2,1)}, bf16[384,768]{1,0:T(8,128)(2,1)S(1)}, u32[]{:S(2)}, u32[]{:S(2)}) collective-permute-start(bf16[384,768]{1,0:T(8,128)(2,1)} %collective-permute-done.13.refs_8_.refs_14_), channel_id=1, source_target_pairs={{0,1},{1,0},{2,3},{3,2},{4,5},{5,4},{6,7},{7,6},{8,9},{9,8},{10,11... | collective-permute-start | bytes 1769480 | tf_op jit(solution)/shard_map/ppermute | solution.py:851
  102.0 21.3 %collective-permute-start.23 = (bf16[1,768,384]{2,1,0:T(8,128)(2,1)}, bf16[1,768,384]{2,1,0:T(8,128)(2,1)S(1)}, u32[]{:S(2)}, u32[]{:S(2)}) collective-permute-start(bf16[1,768,384]{2,1,0:T(8,128)(2,1)} %get-tuple-element.213), channel_id=1, source_target_pairs={{0,2},{1,3},{2,0},{3,1},{4,6},{5,7},{6,4},{7,5},{8,10},{9,11},{10,... | collective-permute-start | bytes 1769480 | tf_op jit(solution)/shard_map/ppermute | solution.py:851
  103.8 19.6 %collective-permute-start.24 = (bf16[2,384,384]{2,1,0:T(8,128)(2,1)}, bf16[2,384,384]{2,1,0:T(8,128)(2,1)S(1)}, u32[]{:S(2)}, u32[]{:S(2)}) collective-permute-start(bf16[2,384,384]{2,1,0:T(8,128)(2,1)} %get-tuple-element.214), channel_id=1, source_target_pairs={{0,4},{4,0},{8,12},{12,8},{16,20},{20,16},{24,28},{28,24},{1,5},{5... | collective-permute-start | bytes 1769480 | tf_op jit(solution)/shard_map/ppermute | solution.py:851
  157.3 17.0 %collective-permute-start.29 = (bf16[1,192,1536]{2,1,0:T(8,128)(2,1)}, bf16[1,192,1536]{2,1,0:T(8,128)(2,1)S(1)}, u32[]{:S(2)}, u32[]{:S(2)}) collective-permute-start(bf16[1,192,1536]{2,1,0:T(8,128)(2,1)} %get-tuple-element.241), channel_id=1, source_target_pairs={{0,2},{1,3},{2,0},{3,1},{4,6},{5,7},{6,4},{7,5},{8,10},{9,11},{10,... | collective-permute-start | bytes 1769480 | tf_op jit(solution)/shard_map/ppermute | solution.py:851
  157.8 16.5 %collective-permute-start.30 = (bf16[2,96,1536]{2,1,0:T(8,128)(2,1)}, bf16[2,96,1536]{2,1,0:T(8,128)(2,1)S(1)}, u32[]{:S(2)}, u32[]{:S(2)}) collective-permute-start(bf16[2,96,1536]{2,1,0:T(8,128)(2,1)} %get-tuple-element.242), channel_id=1, source_target_pairs={{0,4},{4,0},{8,12},{12,8},{16,20},{20,16},{24,28},{28,24},{1,5},{5... | collective-permute-start | bytes 1769480 | tf_op jit(solution)/shard_map/ppermute | solution.py:851
  159.3 15.0 %collective-permute-start.31 = (bf16[1,192,768]{2,1,0:T(8,128)(2,1)}, bf16[1,192,768]{2,1,0:T(8,128)(2,1)S(1)}, u32[]{:S(2)}, u32[]{:S(2)}) collective-permute-start(bf16[1,192,768]{2,1,0:T(8,128)(2,1)} %get-tuple-element.243.refs_8_), channel_id=1, source_target_pairs={{0,16},{4,20},{8,24},{12,28},{16,0},{20,4},{24,8},{28,12},{1,17},{... | collective-permute-start | bytes 884744 | tf_op jit(solution)/shard_map/ppermute | solution.py:851
  190.2 13.3 %collective-permute-start.36 = (bf16[2,192,1792]{2,1,0:T(8,128)(2,1)}, bf16[2,192,1792]{2,1,0:T(8,128)(2,1)S(1)}, u32[]{:S(2)}, u32[]{:S(2)}) collective-permute-start(bf16[2,192,1792]{2,1,0:T(8,128)(2,1)} %get-tuple-element.267), channel_id=1, source_target_pairs={{0,1},{1,0},{2,3},{3,2},{4,5},{5,4},{6,7},{7,6},{8,9},{9,8},{10,11... | collective-permute-start | bytes 4128776 | tf_op jit(solution)/shard_map/ppermute | solution.py:851
  211.2 17.4 %collective-permute-start.39 = (bf16[2,96,1792]{2,1,0:T(8,128)(2,1)}, bf16[2,96,1792]{2,1,0:T(8,128)(2,1)S(1)}, u32[]{:S(2)}, u32[]{:S(2)}) collective-permute-start(bf16[2,96,1792]{2,1,0:T(8,128)(2,1)} %get-tuple-element.290), channel_id=1, source_target_pairs={{0,4},{4,0},{8,12},{12,8},{16,20},{20,16},{24,28},{28,24},{1,5},{5... | collective-permute-start | bytes 2064392 | tf_op jit(solution)/shard_map/ppermute | solution.py:851
  212.7 15.9 %collective-permute-start.38 = (bf16[1,192,1536]{2,1,0:T(8,128)(2,1)}, bf16[1,192,1536]{2,1,0:T(8,128)(2,1)S(1)}, u32[]{:S(2)}, u32[]{:S(2)}) collective-permute-start(bf16[1,192,1536]{2,1,0:T(8,128)(2,1)} %get-tuple-element.289), channel_id=1, source_target_pairs={{0,2},{1,3},{2,0},{3,1},{4,6},{5,7},{6,4},{7,5},{8,10},{9,11},{10,... | collective-permute-start | bytes 1769480 | tf_op jit(solution)/shard_map/ppermute | solution.py:851
  213.2 15.4 %collective-permute-start.40 = (bf16[1,48,3072]{2,1,0:T(8,128)(2,1)}, bf16[1,48,3072]{2,1,0:T(8,128)(2,1)S(1)}, u32[]{:S(2)}, u32[]{:S(2)}) collective-permute-start(bf16[1,48,3072]{2,1,0:T(8,128)(2,1)} %get-tuple-element.291.refs_8_), channel_id=1, source_target_pairs={{0,16},{4,20},{8,24},{12,28},{16,0},{20,4},{24,8},{28,12},{1,17},{... | collective-permute-start | bytes 884744 | tf_op jit(solution)/shard_map/ppermute | solution.py:851
  253.7 30.8 %collective-permute-start.60 = (bf16[1,384,768]{2,1,0:T(8,128)(2,1)S(1)}, bf16[1,384,768]{2,1,0:T(8,128)(2,1)}, u32[]{:S(2)}, u32[]{:S(2)}) collective-permute-start(bf16[1,384,768]{2,1,0:T(8,128)(2,1)S(1)} %copy-done.25), channel_id=1, source_target_pairs={{0,4},{4,0},{8,12},{12,8},{16,20},{20,16},{24,28},{28,24},{1,5},{5... | collective-permute-start | bytes 1769480 | tf_op jit(solution)/shard_map/ppermute | solution.py:851
  255.3 34.2 %collective-permute-start.59 = (bf16[1,96,3072]{2,1,0:T(8,128)(2,1)S(1)}, bf16[1,96,3072]{2,1,0:T(8,128)(2,1)}, u32[]{:S(2)}, u32[]{:S(2)}) collective-permute-start(bf16[1,96,3072]{2,1,0:T(8,128)(2,1)S(1)} %copy-done.26), channel_id=1, source_target_pairs={{0,4},{4,0},{8,12},{12,8},{16,20},{20,16},{24,28},{28,24},{1,5},{5... | collective-permute-start | bytes 1769480 | tf_op jit(solution)/shard_map/ppermute | solution.py:851
  258.5 18.7 %collective-permute-start.52 = (bf16[16,5376]{1,0:T(8,128)(2,1)S(1)}, bf16[16,5376]{1,0:T(8,128)(2,1)S(1)}, u32[]{:S(2)}, u32[]{:S(2)}) collective-permute-start(bf16[16,5376]{1,0:T(8,128)(2,1)S(1)} %pad_maximum_fusion), channel_id=1, source_target_pairs={{0,8},{4,12},{8,0},{12,4},{16,24},{20,28},{24,16},{28,20},{1,9},{5... | collective-permute-start | bytes 516104 | tf_op jit(solution)/shard_map/ppermute | solution.py:851
  262.5 15.3 %collective-permute-start.51 = (bf16[1,48,1792]{2,1,0:T(8,128)(2,1)}, bf16[1,48,1792]{2,1,0:T(8,128)(2,1)S(1)}, u32[]{:S(2)}, u32[]{:S(2)}) collective-permute-start(bf16[1,48,1792]{2,1,0:T(8,128)(2,1)} %get-tuple-element.315.refs_2_), channel_id=1, source_target_pairs={{0,16},{4,20},{8,24},{12,28},{16,0},{20,4},{24,8},{28,12},{1,17},{... | collective-permute-start | bytes 516104 | tf_op jit(solution)/shard_map/ppermute | solution.py:851
  (78 other events, 401.1 us)

commit v5 on v4

--- a/solution.py
+++ b/solution.py
@@ -278,32 +278,52 @@
     spot_ref, act_ref, tok_ref, branch_ref, cot_ref, mod_ref, bias_ref = refs[:7]
     pieces = refs[7 : 7 + count]
     block_ref, gate_ref, whole, sems = refs[7 + count :]
-    copies = piece_copies(pieces, offsets, spot_ref, whole, sems)
-    for copy in copies:
-        copy.start()
-    for copy in copies:
-        copy.wait()
-    rows, width = tok_ref.shape
-    seq = rows // slots
-    for slot in range(slots):
-        at = pl.ds(slot * seq, seq)
-        branch_two = dot_nn(act_ref[at, :], whole[...]) + bias_ref[...]
-        live = spot_ref[2] > slot
-        cot = jnp.where(live, cot_ref[at, :].astype(F32), 0.0)
-        gate_ref[slot : slot + 1, :] = jnp.sum(cot * branch_two, axis=0, keepdims=True)
-        mid = tok_ref[at, :].astype(F32) + mod_part(mod_ref, slot, 2, width) * branch_ref[at, :]
-        block = mid + mod_part(mod_ref, slot, 5, width) * branch_two
-        block_ref[at, :] = jnp.where(live, block, 0.0).astype(BF16)
+    slot = pl.program_id(0)
+    width = tok_ref.shape[1]
+
+    @pl.when(slot == 0)
+    def _():
+        copies = piece_copies(pieces, offsets, spot_ref, whole, sems)
+        for copy in copies:
+            copy.start()
+        for copy in copies:
+            copy.wait()
+
+    mod = mod_ref[0]
+    branch_two = dot_nn(act_ref[...], whole[...]) + bias_ref[...]
+    live = spot_ref[2] > slot
+    cot = jnp.where(live, cot_ref[...].astype(F32), 0.0)
+    gate = jnp.sum(cot * branch_two, axis=0, keepdims=True)
+    for place in range(slots):
+
+        @pl.when(slot == place)
+        def _():
+            gate_ref[place : place + 1, :] = gate
+
+    mid = tok_ref[...].astype(F32) + mod_part(mod, 0, 2, width) * branch_ref[...]
+    block = mid + mod_part(mod, 0, 5, width) * branch_two
+    block_ref[...] = jnp.where(live, block, 0.0).astype(BF16)
 
 
 def out_call(spot, act_low, tokens, branch_one, cot, modulation, bias, weight, slots):
     rows, width = tokens.shape
     hidden_units = act_low.shape[1]
     pieces, offsets = weight
+    by_slot = pl.BlockSpec((rows // slots, width), lambda s: (s, 0))
     return pl.pallas_call(
         functools.partial(out_kernel, offsets, slots),
-        in_specs=specs(1, pltpu.SMEM) + specs(6) + specs(len(pieces), pl.ANY),
-        out_specs=specs(2),
+        grid=(slots,),
+        in_specs=specs(1, pltpu.SMEM)
+        + [
+            pl.BlockSpec((rows // slots, hidden_units), lambda s: (s, 0)),
+            by_slot,
+            by_slot,
+            by_slot,
+            pl.BlockSpec((1, 1, 6 * width), lambda s: (s, 0, 0)),
+            pl.BlockSpec((1, width), lambda s: (0, 0)),
+        ]
+        + specs(len(pieces), pl.ANY),
+        out_specs=[by_slot, pl.BlockSpec((slots, width), lambda s: (0, 0))],
         out_shape=[shape((rows, width), BF16), shape((slots, width), F32)],
         scratch_shapes=[
             pltpu.VMEM((hidden_units, width), BF16),
@@ -311,7 +331,7 @@
         ],
         name="fc2_fwd",
         **params(2 * rows * width * hidden_units, 2 * (rows + width) * hidden_units),
-    )(spot, act_low, tokens, branch_one, cot, modulation, bias, *pieces)
+    )(spot, act_low, tokens, branch_one, cot, modulation[:, None, :], bias, *pieces)
 
 
 def mlp_bwd_kernel(one_offsets, two_offsets, slots, *refs):

time: 313 us -> 313 us (level)
  transfers between devices with their start and end apart: 61 -> 61, of which waited for: 21 -> 21; matrix products, arithmetic and copies ran while one was open for 8% -> 8% of each run, Pallas kernels for 39% -> 38%
where the time goes in v5:
time: 313 us; the launch traced here: 312 us
  Pallas kernels  155 us (50%)
  starting transfers between devices  57.4 us (18%)
  waiting for transfers between devices  57.1 us (18%)
  local copies, waits for them, and re-layouts  32.3 us (10%)
  other arithmetic  4.64 us (1%)
  matrix products  3.45 us (1%)
    ppermute x61, starting transfers between devices, swap(): lax.ppermute(value, self.name, [(i, i ^ bit) for i in range(self.size)])  57.4 us
    ppermute x61, waiting for transfers between devices, swap(): lax.ppermute(value, self.name, [(i, i ^ bit) for i in range(self.size)])  57.1 us
    pallas_call x12, Pallas kernels, round_call(): pl.pallas_call(functools.partial(round_kernel, kinds), grid_spec=pltpu.Pr...  47.4 us
    pallas_call x1, Pallas kernels, mlp_bwd_call(): pl.pallas_call(functools.partial(mlp_bwd_kernel, one[1], two[1], slots),...  18 us
    unnamed x86, local copies, waits for them, and re-layouts  15.1 us
    pallas_call x2, Pallas kernels, wide_grad(): pl.pallas_call(wide_grad_kernel, grid=(shards // 2 // per_step, out_dim /...  12.7 us
    pallas_call x1, Pallas kernels, attn_bwd_call(): pl.pallas_call(attn_bwd_kernel, grid=(slots,), in_specs=[pl.BlockSpec((se...  12.4 us
    pallas_call x1, Pallas kernels, gelu_call(): pl.pallas_call(functools.partial(gelu_kernel, offsets), grid=(hidden_unit...  10.5 us
  transfers between devices with their start and end apart: 61, of which 21 were waited for; matrix products, arithmetic and copies ran while one was open for 8% of the time, Pallas kernels for 38%

profile of v5, /device:TPU:0, one launch (start us, length us, event | category | flops | bytes accessed | tf_op | source)
XLA Modules:
  0.0 311.8 jit_solution(17336149674996727458)
XLA Ops:
  13.4 6.4 %collective-permute-done.2.refs_5_.refs_9_ = bf16[96,2304]{1,0:T(8,128)(2,1)} collective-permute-done((bf16[96,2304]{1,0:T(8,128)(2,1)S(1)}, bf16[96,2304]{1,0:T(8,128)(2,1)}, u32[]{:S(2)}, u32[]{:S(2)}) %collective-permute-start.2) | collective-permute-done | bytes 442400 | tf_op jit(solution)/shard_map/ppermute | solution.py:871
  37.8 6.6 %qkv_fwd.1 = (bf16[512,768]{1,0:T(8,128)(2,1)}, bf16[512,2304]{1,0:T(8,128)(2,1)}) custom-call(s32[3]{0:T(128)} %pad_add_fusion.refs_0_.spot_ref, bf16[512,768]{1,0:T(8,128)(2,1)} %refs_2_.7, f32[2,4608]{1,0:T(2,128)} %get-tuple-element.341.refs_2_.refs_6_.refs_4_, f32[1,2304]{1,0:T(1,128)} %fusion.7.refs_3_, bf16[192,2304]{1,0:T(8,128)(2,1)} %refs_8_.1, ...), custom_call_target="tpu_custom_call" | custom-call | tf_op jit(solution)/shard_map/qkv_fwd/pallas_call | solution.py:124
  52.2 9.5 %attn_fwd.1 = (bf16[512,768]{1,0:T(8,128)(2,1)}, f32[512,768]{1,0:T(8,128)}, bf16[512,768]{1,0:T(8,128)(2,1)}, bf16[512,768]{1,0:T(8,128)(2,1)}) custom-call(s32[3]{0:T(128)} %pad_add_fusion.refs_0_.spot_ref, bf16[512,2304]{1,0:T(8,128)(2,1)} %get-tuple-element.187.refs_1_.qkv_ref, bf16[512,768]{1,0:T(8,128)(2,1)} %refs_2_.7, bf16[512,768]{1,0:T(8,128)(2,1)} %refs_5_.1, ...), custom_call_target="tpu_custom_call" | custom-call | tf_op jit(solution)/shard_map/attn_fwd/pallas_call | solution.py:192
  67.4 10.5 %fc1_gelu.1 = (bf16[512,3072]{1,0:T(8,128)(2,1)}, f32[512,3072]{1,0:T(8,128)}) custom-call(s32[3]{0:T(128)} %pad_add_fusion.refs_0_.spot_ref, bf16[512,768]{1,0:T(8,128)(2,1)} %get-tuple-element.193.refs_1_.left_ref, f32[1,3072]{1,0:T(1,128)} %bitcast.36, bf16[192,3072]{1,0:T(8,128)(2,1)} %refs_7_.4, bf16[96,3072]{1,0:T(8,128)(2,1)} %copy-done.7, ...), custom_call_target="tpu_custom_call" | custom-call | tf_op jit(solution)/shard_map/fc1_gelu/pallas_call | solution.py:254
  78.2 6.4 %fc2_grad.1 = (f32[2,768,768]{2,1,0:T(8,128)}, bf16[2,768,768]{2,1,0:T(8,128)(2,1)}) custom-call(s32[3]{0:T(128)} %pad_add_fusion.refs_0_.spot_ref, bf16[512,3072]{1,0:T(8,128)(2,1)} %get-tuple-element.205.left_ref.refs_1_, bf16[512,768]{1,0:T(8,128)(2,1)} %get-tuple-element.215.right_ref.refs_1_), custom_call_target="tpu_custom_call" | custom-call | tf_op jit(solution)/shard_map/fc2_grad/pallas_call | solution.py:596
  87.5 8.8 %fc2_fwd.1 = (bf16[512,768]{1,0:T(8,128)(2,1)}, f32[2,768]{1,0:T(2,128)}) custom-call(s32[3]{0:T(128)} %pad_add_fusion.refs_0_.spot_ref, bf16[512,3072]{1,0:T(8,128)(2,1)} %get-tuple-element.205.left_ref.refs_1_, bf16[512,768]{1,0:T(8,128)(2,1)} %refs_2_.7, f32[512,768]{1,0:T(8,128)} %get-tuple-element.206.refs_3_.refs_4_, bf16[512,768]{1,0:T(8,128)(2,1)} %refs_5_.1, ...), custom_call_target="tpu_custom_call" | custom-call | tf_op jit(solution)/shard_map/fc2_fwd/pallas_call | solution.py:313
  96.3 5.6 %sum_round.12 = (f32[1,768,384]{2,1,0:T(8,128)}, bf16[1,768,384]{2,1,0:T(8,128)(2,1)}, f32[2,384,384]{2,1,0:T(8,128)}, bf16[2,384,384]{2,1,0:T(8,128)(2,1)}) custom-call(s32[3]{0:T(128)} %pad_add_fusion.refs_0_.spot_ref, f32[2,768,768]{2,1,0:T(8,128)} %get-tuple-element.210.refs_0_.refs_1_.refs_4_.refs_5_, ...), custom_call_target="tpu_custom_call" | custom-call | tf_op jit(solution)/shard_map/sum_round/pallas_call | solution.py:744
  105.2 18.0 %mlp_bwd.1 = (bf16[512,3072]{1,0:T(8,128)(2,1)}, f32[1,3072]{1,0:T(1,128)}, f32[512,768]{1,0:T(8,128)}, bf16[512,768]{1,0:T(8,128)(2,1)}, f32[5,2,768]{2,1,0:T(2,128)}) custom-call(s32[3]{0:T(128)} %pad_add_fusion.refs_0_.spot_ref, bf16[512,768]{1,0:T(8,128)(2,1)} %get-tuple-element.215.right_ref.refs_1_, f32[512,3072]{1,0:T(8,128)} %get-tuple-element.216.refs_2_, ...), custom_call_target="tpu_custom_call" | custom-call | tf_op jit(solution)/shard_map/mlp_bwd/pallas_call | solution.py:402
  124.2 3.9 %sum_round.13 = (f32[1,384,384]{2,1,0:T(8,128)}, bf16[1,384,384]{2,1,0:T(8,128)(2,1)}, f32[1,384,384]{2,1,0:T(8,128)}, bf16[1,384,384]{2,1,0:T(8,128)(2,1)}) custom-call(s32[3]{0:T(128)} %pad_add_fusion.refs_0_.spot_ref, f32[1,768,384]{2,1,0:T(8,128)} %get-tuple-element.212.refs_0_.refs_1_, f32[1,768,384]{2,1,0:T(8,128)} %get-tuple-element.212.refs_0_.refs_1_, ...), custom_call_target="tpu_custom_call" | custom-call | tf_op jit(solution)/shard_map/sum_round/pallas_call | solution.py:744
  129.0 6.3 %fc1_grad.1 = (f32[2,192,3072]{2,1,0:T(8,128)}, bf16[2,192,3072]{2,1,0:T(8,128)(2,1)}) custom-call(s32[3]{0:T(128)} %pad_add_fusion.refs_0_.spot_ref, bf16[512,768]{1,0:T(8,128)(2,1)} %get-tuple-element.193.refs_1_.left_ref, bf16[512,3072]{1,0:T(8,128)(2,1)} %get-tuple-element.224.right_ref), custom_call_target="tpu_custom_call" | custom-call | tf_op jit(solution)/shard_map/fc1_grad/pallas_call | solution.py:596
  142.6 4.1 %proj_bwd.1.grad_ref = bf16[512,768]{1,0:T(8,128)(2,1)} custom-call(s32[3]{0:T(128)} %pad_add_fusion.refs_0_.spot_ref, bf16[512,768]{1,0:T(8,128)(2,1)} %get-tuple-element.236.refs_1_.refs_4_, bf16[192,768]{1,0:T(8,128)(2,1)} %refs_2_.6, bf16[192,768]{1,0:T(8,128)(2,1)} %collective-permute-done.10.refs_7_.refs_3_, ...), custom_call_target="tpu_custom_call" | custom-call | tf_op jit(solution)/shard_map/proj_bwd/pallas_call | solution.py:512
  151.4 5.7 %sum_round.15 = (f32[1,192,1536]{2,1,0:T(8,128)}, bf16[1,192,1536]{2,1,0:T(8,128)(2,1)}, f32[2,96,1536]{2,1,0:T(8,128)}, bf16[2,96,1536]{2,1,0:T(8,128)(2,1)}, bf16[1,192,768]{2,1,0:T(8,128)(2,1)}) custom-call(s32[3]{0:T(128)} %pad_add_fusion.refs_0_.spot_ref, f32[2,192,3072]{2,1,0:T(8,128)} %get-tuple-element.228.refs_0_.refs_1_.refs_4_.refs_5_, ...), custom_call_target="tpu_custom_call" | custom-call | tf_op jit(solution)/shard_map/sum_round/pallas_call | solution.py:744
  161.8 12.4 %attn_bwd.1 = (bf16[512,2304]{1,0:T(8,128)(2,1)}, f32[2,1,1536]{2,1,0:T(1,128)}) custom-call(bf16[512,2304]{1,0:T(8,128)(2,1)} %get-tuple-element.187.refs_1_.qkv_ref, bf16[512,768]{1,0:T(8,128)(2,1)} %proj_bwd.1.grad_ref), custom_call_target="tpu_custom_call" | custom-call | tf_op jit(solution)/shard_map/attn_bwd/pallas_call | solution.py:476
  175.3 4.0 %sum_round.16 = (f32[1,96,1536]{2,1,0:T(8,128)}, bf16[1,96,1536]{2,1,0:T(8,128)(2,1)}, f32[1,96,1536]{2,1,0:T(8,128)}, bf16[1,96,1536]{2,1,0:T(8,128)(2,1)}, bf16[1,192,768]{2,1,0:T(8,128)(2,1)}) custom-call(s32[3]{0:T(128)} %pad_add_fusion.refs_0_.spot_ref, f32[1,192,1536]{2,1,0:T(8,128)} %get-tuple-element.240.refs_0_.refs_1_, ...), custom_call_target="tpu_custom_call" | custom-call | tf_op jit(solution)/shard_map/sum_round/pallas_call | solution.py:744
  183.1 7.0 %attn_weight_grads.1 = (f32[2,192,1536]{2,1,0:T(8,128)}, bf16[2,192,1536]{2,1,0:T(8,128)(2,1)}, f32[2,192,1792]{2,1,0:T(8,128)}, bf16[2,192,1792]{2,1,0:T(8,128)(2,1)}) custom-call(s32[3]{0:T(128)} %pad_add_fusion.refs_0_.spot_ref, bf16[512,768]{1,0:T(8,128)(2,1)} %get-tuple-element.255.refs_1_, bf16[512,2304]{1,0:T(8,128)(2,1)} %get-tuple-element.276.refs_2_.refs_1_, ...), custom_call_target="tpu_custom_call" | custom-call | tf_op jit(solution)/shard_map/attn_weight_grads/pallas_call | solution.py:651
  191.0 3.5 %sum_round.17 = (f32[1,48,3072]{2,1,0:T(8,128)}, bf16[1,48,3072]{2,1,0:T(8,128)(2,1)}, bf16[1,384,768]{2,1,0:T(8,128)(2,1)}) custom-call(s32[3]{0:T(128)} %pad_add_fusion.refs_0_.spot_ref, f32[1,96,1536]{2,1,0:T(8,128)} %get-tuple-element.268.refs_0_.refs_1_, f32[1,96,1536]{2,1,0:T(8,128)} %get-tuple-element.268.refs_0_.refs_1_, ...), custom_call_target="tpu_custom_call" | custom-call | tf_op jit(solution)/shard_map/sum_round/pallas_call | solution.py:744
  194.9 8.0 %qkv_bwd.1 = (f32[512,768]{1,0:T(8,128)}, bf16[2,5376]{1,0:T(2,128)(2,1)}) custom-call(s32[3]{0:T(128)} %pad_add_fusion.refs_0_.spot_ref, bf16[512,2304]{1,0:T(8,128)(2,1)} %get-tuple-element.276.refs_2_.refs_1_, bf16[512,768]{1,0:T(8,128)(2,1)} %refs_2_.7, f32[512,768]{1,0:T(8,128)} %get-tuple-element.277.refs_3_, ...), custom_call_target="tpu_custom_call" | custom-call | tf_op jit(solution)/shard_map/qkv_bwd/pallas_call | solution.py:561
  204.9 6.2 %sum_round.18 = (f32[1,192,1536]{2,1,0:T(8,128)}, bf16[1,192,1536]{2,1,0:T(8,128)(2,1)}, f32[2,96,1792]{2,1,0:T(8,128)}, bf16[2,96,1792]{2,1,0:T(8,128)(2,1)}, bf16[1,48,3072]{2,1,0:T(8,128)(2,1)}) custom-call(s32[3]{0:T(128)} %pad_add_fusion.refs_0_.spot_ref, f32[2,192,1536]{2,1,0:T(8,128)} %get-tuple-element.283.refs_0_.refs_1_, ...), custom_call_target="tpu_custom_call" | custom-call | tf_op jit(solution)/shard_map/sum_round/pallas_call | solution.py:744
  217.1 11.5 %collective-permute-done.40.refs_9_ = bf16[1,48,3072]{2,1,0:T(8,128)(2,1)S(1)} collective-permute-done((bf16[1,48,3072]{2,1,0:T(8,128)(2,1)}, bf16[1,48,3072]{2,1,0:T(8,128)(2,1)S(1)}, u32[]{:S(2)}, u32[]{:S(2)}) %collective-permute-start.40) | collective-permute-done | bytes 294944 | tf_op jit(solution)/shard_map/ppermute | solution.py:871
  229.7 4.1 %sum_round.19 = (f32[1,96,1536]{2,1,0:T(8,128)}, bf16[1,96,1536]{2,1,0:T(8,128)(2,1)}, f32[1,96,1792]{2,1,0:T(8,128)}, bf16[1,96,1792]{2,1,0:T(8,128)(2,1)}, bf16[1,48,3072]{2,1,0:T(8,128)(2,1)}) custom-call(s32[3]{0:T(128)} %pad_add_fusion.refs_0_.spot_ref, f32[1,192,1536]{2,1,0:T(8,128)} %get-tuple-element.293.refs_0_.refs_1_, ...), custom_call_target="tpu_custom_call" | custom-call | tf_op jit(solution)/shard_map/sum_round/pallas_call | solution.py:744
  238.0 7.0 %collective-permute-done.45 = bf16[4,5376]{1,0:T(4,128)(2,1)S(1)} collective-permute-done((bf16[4,5376]{1,0:T(4,128)(2,1)S(1)}, bf16[4,5376]{1,0:T(4,128)(2,1)S(1)}, u32[]{:S(2)}, u32[]{:S(2)}) %collective-permute-start.45) | collective-permute-done | bytes 43040 | tf_op jit(solution)/shard_map/ppermute | solution.py:871
  247.5 3.5 %sum_round.20 = (f32[1,48,1536]{2,1,0:T(8,128)}, bf16[1,48,1536]{2,1,0:T(8,128)(2,1)}, f32[1,48,1792]{2,1,0:T(8,128)}, bf16[1,48,1792]{2,1,0:T(8,128)(2,1)}, bf16[1,96,3072]{2,1,0:T(8,128)(2,1)}) custom-call(s32[3]{0:T(128)} %pad_add_fusion.refs_0_.spot_ref, f32[1,96,1536]{2,1,0:T(8,128)} %get-tuple-element.302.refs_0_.refs_1_, ...), custom_call_target="tpu_custom_call" | custom-call | tf_op jit(solution)/shard_map/sum_round/pallas_call | solution.py:744
  269.1 8.0 %collective-permute-done.50.refs_1_ = bf16[1,48,1536]{2,1,0:T(8,128)(2,1)S(1)} collective-permute-done((bf16[1,48,1536]{2,1,0:T(8,128)(2,1)}, bf16[1,48,1536]{2,1,0:T(8,128)(2,1)S(1)}, u32[]{:S(2)}, u32[]{:S(2)}) %collective-permute-start.50) | collective-permute-done | bytes 147488 | tf_op jit(solution)/shard_map/ppermute | solution.py:871
  303.2 4.3 %collective-permute-done.57.refs_1_ = bf16[1,96,1536]{2,1,0:T(8,128)(2,1)S(1)} collective-permute-done((bf16[1,96,1536]{2,1,0:T(8,128)(2,1)}, bf16[1,96,1536]{2,1,0:T(8,128)(2,1)S(1)}, u32[]{:S(2)}, u32[]{:S(2)}) %collective-permute-start.57) | collective-permute-done | bytes 294944 | tf_op jit(solution)/shard_map/ppermute | solution.py:871
  (256 shorter events, 138.5 us)
Async XLA Ops:
  13.1 22.6 %collective-permute-start.6 = (bf16[192,2304]{1,0:T(8,128)(2,1)}, bf16[192,2304]{1,0:T(8,128)(2,1)}, u32[]{:S(2)}, u32[]{:S(2)}) collective-permute-start(bf16[192,2304]{1,0:T(8,128)(2,1)} %refs_8_.1), channel_id=1, source_target_pairs={{0,1},{1,0},{2,3},{3,2},{4,5},{5,4},{6,7},{7,6},{8,9},{9,8},{10,11... | collective-permute-start | bytes 2654216 | tf_op jit(solution)/shard_map/ppermute | solution.py:871
  19.8 15.8 %collective-permute-start.7 = (bf16[96,2304]{1,0:T(8,128)(2,1)}, bf16[96,2304]{1,0:T(8,128)(2,1)}, u32[]{:S(2)}, u32[]{:S(2)}) collective-permute-start(bf16[96,2304]{1,0:T(8,128)(2,1)} %collective-permute-done.2.refs_5_.refs_9_), channel_id=1, source_target_pairs={{0,1},{1,0},{2,3},{3,2},{4,5},{5,4},{6,7},{7,6},{8,9},{9,8},{10,11... | collective-permute-start | bytes 1327112 | tf_op jit(solution)/shard_map/ppermute | solution.py:871
  19.8 15.1 %collective-permute-start.5 = (bf16[96,2304]{1,0:T(8,128)(2,1)}, bf16[96,2304]{1,0:T(8,128)(2,1)}, u32[]{:S(2)}, u32[]{:S(2)}) collective-permute-start(bf16[96,2304]{1,0:T(8,128)(2,1)} %collective-permute-done.2.refs_5_.refs_9_), channel_id=1, source_target_pairs={{0,4},{4,0},{8,12},{12,8},{16,20},{20,16},{24,28},{28,24},{1,5},{5... | collective-permute-start | bytes 1327112 | tf_op jit(solution)/shard_map/ppermute | solution.py:871
  29.8 16.7 %collective-permute-start.9 = (bf16[96,3072]{1,0:T(8,128)(2,1)}, bf16[96,3072]{1,0:T(8,128)(2,1)S(1)}, u32[]{:S(2)}, u32[]{:S(2)}) collective-permute-start(bf16[96,3072]{1,0:T(8,128)(2,1)} %constant_dynamic-slice_fusion.1), channel_id=1, source_target_pairs={{0,2},{1,3},{2,0},{3,1},{4,6},{5,7},{6,4},{7,5},{8,10},{9,11},{10,... | collective-permute-start | bytes 1769480 | tf_op jit(solution)/shard_map/ppermute | solution.py:871
  46.5 15.2 %collective-permute-start.14 = (bf16[96,3072]{1,0:T(8,128)(2,1)S(1)}, bf16[96,3072]{1,0:T(8,128)(2,1)}, u32[]{:S(2)}, u32[]{:S(2)}) collective-permute-start(bf16[96,3072]{1,0:T(8,128)(2,1)S(1)} %collective-permute-done.9.refs_4_.refs_8_), channel_id=1, source_target_pairs={{0,4},{4,0},{8,12},{12,8},{16,20},{20,16},{24,28},{28,24},{1,5},{5... | collective-permute-start | bytes 1769480 | tf_op jit(solution)/shard_map/ppermute | solution.py:871
  46.8 19.7 %collective-permute-start.16 = (bf16[192,3072]{1,0:T(8,128)(2,1)}, bf16[192,3072]{1,0:T(8,128)(2,1)}, u32[]{:S(2)}, u32[]{:S(2)}) collective-permute-start(bf16[192,3072]{1,0:T(8,128)(2,1)} %refs_7_.4), channel_id=1, source_target_pairs={{0,1},{1,0},{2,3},{3,2},{4,5},{5,4},{6,7},{7,6},{8,9},{9,8},{10,11... | collective-permute-start | bytes 3538952 | tf_op jit(solution)/shard_map/ppermute | solution.py:871
  46.8 16.1 %collective-permute-start.13 = (bf16[384,768]{1,0:T(8,128)(2,1)}, bf16[384,768]{1,0:T(8,128)(2,1)}, u32[]{:S(2)}, u32[]{:S(2)}) collective-permute-start(bf16[384,768]{1,0:T(8,128)(2,1)} %constant_dynamic-slice_fusion), channel_id=1, source_target_pairs={{0,2},{1,3},{2,0},{3,1},{4,6},{5,7},{6,4},{7,5},{8,10},{9,11},{10,... | collective-permute-start | bytes 1769480 | tf_op jit(solution)/shard_map/ppermute | solution.py:871
  51.9 14.1 %collective-permute-start.15 = (bf16[96,3072]{1,0:T(8,128)(2,1)S(1)}, bf16[96,3072]{1,0:T(8,128)(2,1)S(1)}, u32[]{:S(2)}, u32[]{:S(2)}) collective-permute-start(bf16[96,3072]{1,0:T(8,128)(2,1)S(1)} %collective-permute-done.9.refs_4_.refs_8_), channel_id=1, source_target_pairs={{0,1},{1,0},{2,3},{3,2},{4,5},{5,4},{6,7},{7,6},{8,9},{9,8},{10,11... | collective-permute-start | bytes 1769480 | tf_op jit(solution)/shard_map/ppermute | solution.py:871
  62.9 15.2 %collective-permute-start.18 = (bf16[384,768]{1,0:T(8,128)(2,1)}, bf16[384,768]{1,0:T(8,128)(2,1)S(1)}, u32[]{:S(2)}, u32[]{:S(2)}) collective-permute-start(bf16[384,768]{1,0:T(8,128)(2,1)} %collective-permute-done.13.refs_8_.refs_14_), channel_id=1, source_target_pairs={{0,4},{4,0},{8,12},{12,8},{16,20},{20,16},{24,28},{28,24},{1,5},{5... | collective-permute-start | bytes 1769480 | tf_op jit(solution)/shard_map/ppermute | solution.py:871
  64.6 20.0 %collective-permute-start.19 = (bf16[768,768]{1,0:T(8,128)(2,1)S(1)}, bf16[768,768]{1,0:T(8,128)(2,1)S(1)}, u32[]{:S(2)}, u32[]{:S(2)}) collective-permute-start(bf16[768,768]{1,0:T(8,128)(2,1)S(1)} %copy-done.2), channel_id=1, source_target_pairs={{0,1},{1,0},{2,3},{3,2},{4,5},{5,4},{6,7},{7,6},{8,9},{9,8},{10,11... | collective-permute-start | bytes 3538952 | tf_op jit(solution)/shard_map/ppermute | solution.py:871
  66.0 18.6 %collective-permute-start.20 = (bf16[384,768]{1,0:T(8,128)(2,1)}, bf16[384,768]{1,0:T(8,128)(2,1)S(1)}, u32[]{:S(2)}, u32[]{:S(2)}) collective-permute-start(bf16[384,768]{1,0:T(8,128)(2,1)} %collective-permute-done.13.refs_8_.refs_14_), channel_id=1, source_target_pairs={{0,1},{1,0},{2,3},{3,2},{4,5},{5,4},{6,7},{7,6},{8,9},{9,8},{10,11... | collective-permute-start | bytes 1769480 | tf_op jit(solution)/shard_map/ppermute | solution.py:871
  102.0 21.3 %collective-permute-start.23 = (bf16[1,768,384]{2,1,0:T(8,128)(2,1)}, bf16[1,768,384]{2,1,0:T(8,128)(2,1)S(1)}, u32[]{:S(2)}, u32[]{:S(2)}) collective-permute-start(bf16[1,768,384]{2,1,0:T(8,128)(2,1)} %get-tuple-element.213), channel_id=1, source_target_pairs={{0,2},{1,3},{2,0},{3,1},{4,6},{5,7},{6,4},{7,5},{8,10},{9,11},{10,... | collective-permute-start | bytes 1769480 | tf_op jit(solution)/shard_map/ppermute | solution.py:871
  103.7 19.6 %collective-permute-start.24 = (bf16[2,384,384]{2,1,0:T(8,128)(2,1)}, bf16[2,384,384]{2,1,0:T(8,128)(2,1)S(1)}, u32[]{:S(2)}, u32[]{:S(2)}) collective-permute-start(bf16[2,384,384]{2,1,0:T(8,128)(2,1)} %get-tuple-element.214), channel_id=1, source_target_pairs={{0,4},{4,0},{8,12},{12,8},{16,20},{20,16},{24,28},{28,24},{1,5},{5... | collective-permute-start | bytes 1769480 | tf_op jit(solution)/shard_map/ppermute | solution.py:871
  157.2 17.1 %collective-permute-start.29 = (bf16[1,192,1536]{2,1,0:T(8,128)(2,1)}, bf16[1,192,1536]{2,1,0:T(8,128)(2,1)S(1)}, u32[]{:S(2)}, u32[]{:S(2)}) collective-permute-start(bf16[1,192,1536]{2,1,0:T(8,128)(2,1)} %get-tuple-element.241), channel_id=1, source_target_pairs={{0,2},{1,3},{2,0},{3,1},{4,6},{5,7},{6,4},{7,5},{8,10},{9,11},{10,... | collective-permute-start | bytes 1769480 | tf_op jit(solution)/shard_map/ppermute | solution.py:871
  157.6 16.7 %collective-permute-start.30 = (bf16[2,96,1536]{2,1,0:T(8,128)(2,1)}, bf16[2,96,1536]{2,1,0:T(8,128)(2,1)S(1)}, u32[]{:S(2)}, u32[]{:S(2)}) collective-permute-start(bf16[2,96,1536]{2,1,0:T(8,128)(2,1)} %get-tuple-element.242), channel_id=1, source_target_pairs={{0,4},{4,0},{8,12},{12,8},{16,20},{20,16},{24,28},{28,24},{1,5},{5... | collective-permute-start | bytes 1769480 | tf_op jit(solution)/shard_map/ppermute | solution.py:871
  159.2 15.0 %collective-permute-start.31 = (bf16[1,192,768]{2,1,0:T(8,128)(2,1)}, bf16[1,192,768]{2,1,0:T(8,128)(2,1)S(1)}, u32[]{:S(2)}, u32[]{:S(2)}) collective-permute-start(bf16[1,192,768]{2,1,0:T(8,128)(2,1)} %get-tuple-element.243.refs_8_), channel_id=1, source_target_pairs={{0,16},{4,20},{8,24},{12,28},{16,0},{20,4},{24,8},{28,12},{1,17},{... | collective-permute-start | bytes 884744 | tf_op jit(solution)/shard_map/ppermute | solution.py:871
  190.1 13.3 %collective-permute-start.36 = (bf16[2,192,1792]{2,1,0:T(8,128)(2,1)}, bf16[2,192,1792]{2,1,0:T(8,128)(2,1)S(1)}, u32[]{:S(2)}, u32[]{:S(2)}) collective-permute-start(bf16[2,192,1792]{2,1,0:T(8,128)(2,1)} %get-tuple-element.267), channel_id=1, source_target_pairs={{0,1},{1,0},{2,3},{3,2},{4,5},{5,4},{6,7},{7,6},{8,9},{9,8},{10,11... | collective-permute-start | bytes 4128776 | tf_op jit(solution)/shard_map/ppermute | solution.py:871
  211.1 17.5 %collective-permute-start.39 = (bf16[2,96,1792]{2,1,0:T(8,128)(2,1)}, bf16[2,96,1792]{2,1,0:T(8,128)(2,1)S(1)}, u32[]{:S(2)}, u32[]{:S(2)}) collective-permute-start(bf16[2,96,1792]{2,1,0:T(8,128)(2,1)} %get-tuple-element.290), channel_id=1, source_target_pairs={{0,4},{4,0},{8,12},{12,8},{16,20},{20,16},{24,28},{28,24},{1,5},{5... | collective-permute-start | bytes 2064392 | tf_op jit(solution)/shard_map/ppermute | solution.py:871
  212.7 15.9 %collective-permute-start.38 = (bf16[1,192,1536]{2,1,0:T(8,128)(2,1)}, bf16[1,192,1536]{2,1,0:T(8,128)(2,1)S(1)}, u32[]{:S(2)}, u32[]{:S(2)}) collective-permute-start(bf16[1,192,1536]{2,1,0:T(8,128)(2,1)} %get-tuple-element.289), channel_id=1, source_target_pairs={{0,2},{1,3},{2,0},{3,1},{4,6},{5,7},{6,4},{7,5},{8,10},{9,11},{10,... | collective-permute-start | bytes 1769480 | tf_op jit(solution)/shard_map/ppermute | solution.py:871
  213.2 15.4 %collective-permute-start.40 = (bf16[1,48,3072]{2,1,0:T(8,128)(2,1)}, bf16[1,48,3072]{2,1,0:T(8,128)(2,1)S(1)}, u32[]{:S(2)}, u32[]{:S(2)}) collective-permute-start(bf16[1,48,3072]{2,1,0:T(8,128)(2,1)} %get-tuple-element.291.refs_8_), channel_id=1, source_target_pairs={{0,16},{4,20},{8,24},{12,28},{16,0},{20,4},{24,8},{28,12},{1,17},{... | collective-permute-start | bytes 884744 | tf_op jit(solution)/shard_map/ppermute | solution.py:871
  253.6 30.8 %collective-permute-start.60 = (bf16[1,384,768]{2,1,0:T(8,128)(2,1)S(1)}, bf16[1,384,768]{2,1,0:T(8,128)(2,1)}, u32[]{:S(2)}, u32[]{:S(2)}) collective-permute-start(bf16[1,384,768]{2,1,0:T(8,128)(2,1)S(1)} %copy-done.25), channel_id=1, source_target_pairs={{0,4},{4,0},{8,12},{12,8},{16,20},{20,16},{24,28},{28,24},{1,5},{5... | collective-permute-start | bytes 1769480 | tf_op jit(solution)/shard_map/ppermute | solution.py:871
  255.2 34.2 %collective-permute-start.59 = (bf16[1,96,3072]{2,1,0:T(8,128)(2,1)S(1)}, bf16[1,96,3072]{2,1,0:T(8,128)(2,1)}, u32[]{:S(2)}, u32[]{:S(2)}) collective-permute-start(bf16[1,96,3072]{2,1,0:T(8,128)(2,1)S(1)} %copy-done.26), channel_id=1, source_target_pairs={{0,4},{4,0},{8,12},{12,8},{16,20},{20,16},{24,28},{28,24},{1,5},{5... | collective-permute-start | bytes 1769480 | tf_op jit(solution)/shard_map/ppermute | solution.py:871
  258.4 18.8 %collective-permute-start.52 = (bf16[16,5376]{1,0:T(8,128)(2,1)S(1)}, bf16[16,5376]{1,0:T(8,128)(2,1)S(1)}, u32[]{:S(2)}, u32[]{:S(2)}) collective-permute-start(bf16[16,5376]{1,0:T(8,128)(2,1)S(1)} %pad_maximum_fusion), channel_id=1, source_target_pairs={{0,8},{4,12},{8,0},{12,4},{16,24},{20,28},{24,16},{28,20},{1,9},{5... | collective-permute-start | bytes 516104 | tf_op jit(solution)/shard_map/ppermute | solution.py:871
  262.4 15.3 %collective-permute-start.51 = (bf16[1,48,1792]{2,1,0:T(8,128)(2,1)}, bf16[1,48,1792]{2,1,0:T(8,128)(2,1)S(1)}, u32[]{:S(2)}, u32[]{:S(2)}) collective-permute-start(bf16[1,48,1792]{2,1,0:T(8,128)(2,1)} %get-tuple-element.315.refs_2_), channel_id=1, source_target_pairs={{0,16},{4,20},{8,24},{12,28},{16,0},{20,4},{24,8},{28,12},{1,17},{... | collective-permute-start | bytes 516104 | tf_op jit(solution)/shard_map/ppermute | solution.py:871
  (78 other events, 401.0 us)
